TPU v7x, 32 devices: a whole 2x2x4 slice. The times are simulated.
32 devices in a mesh: fsdp: 2 (over core), ctx: 4 (over y, x), tp: 4 (over z).
Axes of the slice: x: 2, y: 2, z: 4, core: 2. Of those that a mesh axis runs over, the one named last changes fastest.
Arguments:
- tokens: bfloat16 [4096, 1024], P(('fsdp', 'ctx')), may hold values from -6 to 6
- out_grad: bfloat16 [4096, 1024], P(('fsdp', 'ctx')), may hold values from -6 to 6
- segment_ids: int32 [2, 2048], P('fsdp'), may hold values from 0 to 3, never falling along the last dimension, each value on 1 to 1024 neighbouring positions
- owner_order: int32 [2, 2048], P('fsdp'), may hold values from 0 to 2047, as said below
- attn_gain: bfloat16 [2, 1024], P(None, ('fsdp', 'ctx')), may hold values from 0.5 to 1.5
- w_query: bfloat16 [2, 1024, 1024], P(None, ('fsdp', 'ctx'), 'tp'), may hold values from -0.1875 to 0.1875
- w_key: bfloat16 [2, 1024, 1024], P(None, ('fsdp', 'ctx'), 'tp'), may hold values from -0.1875 to 0.1875
- w_value: bfloat16 [2, 1024, 1024], P(None, ('fsdp', 'ctx'), 'tp'), may hold values from -0.1875 to 0.1875
- w_out: bfloat16 [2, 1024, 1024], P(None, 'tp', ('fsdp', 'ctx')), may hold values from -0.75 to 0.75
- mlp_gain: bfloat16 [2, 1024], P(None, ('fsdp', 'ctx')), may hold values from 0.5 to 1.5
- w_gate: bfloat16 [2, 1024, 2816], P(None, ('fsdp', 'ctx'), 'tp'), may hold values from -0.1875 to 0.1875
- w_up: bfloat16 [2, 1024, 2816], P(None, ('fsdp', 'ctx'), 'tp'), may hold values from -0.1875 to 0.1875
- w_down: bfloat16 [2, 2816, 1024], P(None, 'tp', ('fsdp', 'ctx')), may hold values from -0.109375 to 0.109375
Outputs:
- outputs: bfloat16 [4096, 1024], P(('fsdp', 'ctx'))
- grad_tokens: float32 [4096, 1024], P(('fsdp', 'ctx'))
- grad_attn_gain: float32 [2, 1024], P(None, ('fsdp', 'ctx'))
- grad_w_query: float32 [2, 1024, 1024], P(None, ('fsdp', 'ctx'), 'tp')
- grad_w_key: float32 [2, 1024, 1024], P(None, ('fsdp', 'ctx'), 'tp')
- grad_w_value: float32 [2, 1024, 1024], P(None, ('fsdp', 'ctx'), 'tp')
- grad_w_out: float32 [2, 1024, 1024], P(None, 'tp', ('fsdp', 'ctx'))
- grad_mlp_gain: float32 [2, 1024], P(None, ('fsdp', 'ctx'))
- grad_w_gate: float32 [2, 1024, 2816], P(None, ('fsdp', 'ctx'), 'tp')
- grad_w_up: float32 [2, 1024, 2816], P(None, ('fsdp', 'ctx'), 'tp')
- grad_w_down: float32 [2, 2816, 1024], P(None, 'tp', ('fsdp', 'ctx'))
Inputs may be any that keep to these rules, and one draw needn't show every extreme that they name: `segment_ids`: along a row the numbers never fall; each sequence holds 1 to 1024 positions and some sequence holds exactly 1024. `owner_order`: each row is a permutation of the positions of its pack. With n = 4, owner slots c * 512 + s * 512 / n + g (g below 512 / n) hold positions from s * 512 to (s + 1) * 512 - 1.
All inputs are finite; a program needn't handle non-finite values.
Results may differ from a plain program's by a relative error of at most 0.02.
Values may be sent and summed in bfloat16 or wider, within the bound.
No kernel may reach another device: no remote copies, remote signals or barrier semaphores. Data moves between devices by JAX's collectives and lax.ppermute only.
A program may use at most 320 MiB of HBM per device.

v0:
```python
import functools

import jax
import jax.numpy as jnp
from jax import lax
from jax.experimental import pallas as pl
from jax.experimental.pallas import tpu as pltpu
from jax.sharding import PartitionSpec as P

HEAD = 64
HALF = HEAD // 2
LAYERS = 2
EPS = 1e-05
THETA = 10000.0
NEG = -1e30
BF = jnp.bfloat16
F32 = jnp.float32
IN_VMEM = pl.BlockSpec(memory_space=pltpu.VMEM)
IN_SMEM = pl.BlockSpec(memory_space=pltpu.SMEM)


def dot(left, right, left_dim, right_dim):
    return lax.dot_general(
        left, right, (((left_dim,), (right_dim,)), ((), ())), preferred_element_type=F32
    )


def mm(left, right):
    return jnp.dot(left, right, preferred_element_type=F32)


class Plan:
    def __init__(self):
        self.fsdp = lax.axis_size("fsdp")
        self.ctx = lax.axis_size("ctx")
        self.tp = lax.axis_size("tp")
        self.high = self.fsdp // 2
        f = lax.axis_index("fsdp")
        z = lax.axis_index("tp")
        self.c = f % 2
        self.fh = f // 2
        self.x = lax.axis_index("ctx")
        self.zl = z % 2
        self.zp = z // 2
        self.ci = self.x % 4
        self.part = self.c * 2 + self.zl
        self.peers = self.high * self.ctx

    def core(self, value):
        return lax.ppermute(value, "fsdp", [(i, i ^ 1) for i in range(self.fsdp)])

    def near(self, value):
        return lax.ppermute(value, "tp", [(i, i ^ 1) for i in range(self.tp)])

    def far(self, value):
        return lax.ppermute(value, "tp", [(i, i ^ 2) for i in range(self.tp)])

    def side(self, value, k):
        return lax.ppermute(value, "ctx", [(i, i ^ k) for i in range(self.ctx)])

    def high_fsdp(self, value, k):
        return lax.ppermute(value, "fsdp", [(i, i ^ (2 * k)) for i in range(self.fsdp)])


def flip_list(blocks, index):
    bit = 1
    while bit < len(blocks):
        on = (index & bit) != 0
        blocks = [jnp.where(on, blocks[i ^ bit], blocks[i]) for i in range(len(blocks))]
        bit *= 2
    return blocks


def place(blocks, index, axis):
    width = blocks[0].shape[axis]
    shape = list(blocks[0].shape)
    shape[axis] = width * len(blocks)
    full = jnp.zeros(shape, blocks[0].dtype)
    for i, block in enumerate(blocks):
        full = lax.dynamic_update_slice_in_dim(full, block, (index ^ i) * width, axis)
    return full


def to_block_order(plan, rows):
    width = rows.shape[1] // (2 * plan.peers)
    parts = []
    for h in range(plan.high):
        for x in range(plan.ctx):
            for c in range(2):
                start = ((h * 2 + c) * plan.ctx + x) * width
                parts.append(rows[:, start : start + width])
    return jnp.concatenate(parts, axis=1)


def from_block_order(plan, rows):
    width = rows.shape[1] // (2 * plan.peers)
    parts = []
    for h in range(plan.high):
        for c in range(2):
            for x in range(plan.ctx):
                start = ((h * plan.ctx + x) * 2 + c) * width
                parts.append(rows[:, start : start + width])
    return jnp.concatenate(parts, axis=1)


def gather_rows(plan, rows):
    pair = jnp.concatenate([rows, plan.near(rows)], axis=0)
    return jnp.concatenate([pair, plan.core(pair)], axis=0)


def sum_rows(plan, partial):
    half = partial.shape[0] // 2
    pair = partial[:half] + plan.core(partial[half:].astype(BF)).astype(F32)
    half = half // 2
    return pair[:half] + plan.near(pair[half:].astype(BF)).astype(F32)


def natural_rows(plan, rows):
    count = rows.shape[0] // 4
    parts = [
        lax.dynamic_slice_in_dim(rows, (plan.part ^ i) * count, count, 0) for i in range(4)
    ]
    return jnp.concatenate(parts, axis=0)


def own_columns(plan, halves):
    keep = lax.dynamic_index_in_dim(halves, plan.c, 0, False)
    got = plan.core(lax.dynamic_index_in_dim(halves, 1 - plan.c, 0, False))
    return jnp.where(
        plan.c == 0,
        jnp.concatenate([keep, got], axis=1),
        jnp.concatenate([got, keep], axis=1),
    )


def all_columns(plan, rows, direct):
    if direct and plan.peers == 4:
        return place([rows] + [plan.side(rows, k) for k in range(1, 4)], plan.x, 1)
    full = lax.all_gather(rows, "ctx", axis=1, tiled=True)
    if plan.high > 1:
        parts = [full] + [plan.high_fsdp(full, k) for k in range(1, plan.high)]
        full = place(parts, plan.fh, 1)
    return full


def columns_sum(plan, grad, direct):
    if plan.high > 1:
        width = grad.shape[1] // plan.high
        parts = [
            lax.dynamic_slice_in_dim(grad, (plan.fh ^ k) * width, width, 1)
            for k in range(plan.high)
        ]
        grad = parts[0]
        for k in range(1, plan.high):
            grad = grad + plan.high_fsdp(parts[k], k)
    if direct and plan.ctx == 4:
        width = grad.shape[1] // 4
        parts = [
            lax.dynamic_slice_in_dim(grad, (plan.x ^ k) * width, width, 1) for k in range(4)
        ]
        total = parts[0].astype(F32)
        for k in range(1, 4):
            total = total + plan.side(parts[k], k).astype(F32)
        return total
    return lax.psum_scatter(grad, "ctx", scatter_dimension=1, tiled=True)


def together(value, *others):
    many = isinstance(value, list)
    got = lax.optimization_barrier((*value, *others) if many else (value, *others))
    count = len(value) if many else 1
    first = list(got[:count]) if many else got[0]
    return (first, *got[count:])


def with_far(own, far, counts):
    parts = []
    start = 0
    for rows in counts:
        parts += [own[start : start + rows], far[start : start + rows]]
        start += rows
    return jnp.concatenate(parts, axis=0)


def far_halves(total, counts):
    mine, far = [], []
    start = 0
    for rows in counts:
        mine.append(total[start : start + rows])
        far.append(total[start + rows : start + 2 * rows])
        start += 2 * rows
    return jnp.concatenate(mine, axis=0).astype(F32), jnp.concatenate(far, axis=0).astype(BF)


def core_halves(plan, own, counts):
    width = own.shape[1]
    left, right = own[:, : width // 2], own[:, width // 2 :]
    kept = jnp.where(plan.c == 0, left, right)
    got = plan.core(jnp.where(plan.c == 0, right, left).astype(BF)).astype(F32)
    low = jnp.where(plan.c == 0, kept, got)
    high = jnp.where(plan.c == 0, got, kept)
    out = []
    start = 0
    for rows in counts:
        out.append((low[start : start + rows], high[start : start + rows]))
        start += rows
    return out


def split_hidden(weight):
    return weight.reshape(2, weight.shape[0] // 2, weight.shape[1])


def turn(values, cos_tab, sine_tab):
    first, second = values[..., :HALF, :], values[..., HALF:, :]
    return jnp.concatenate(
        [first * cos_tab - second * sine_tab, second * cos_tab + first * sine_tab], axis=-2
    )


def to_heads(plan, values):
    got = [lax.dynamic_index_in_dim(values, plan.ci, 0, False)]
    for k in range(1, 4):
        got.append(plan.side(lax.dynamic_index_in_dim(values, plan.ci ^ k, 0, False), k))
    return got


def from_heads(plan, blocks):
    got = [blocks[0]] + [plan.side(blocks[k], k) for k in range(1, 4)]
    return place([block[None] for block in got], plan.ci, 0)


def more_keys(plan, blocks):
    full = list(blocks)
    for m in range(1, plan.ctx // 4):
        full += [plan.side(block, 4 * m) for block in blocks]
    return full


def more_keys_sum(plan, blocks):
    total = list(blocks[:4])
    for m in range(1, plan.ctx // 4):
        total = [total[k] + plan.side(blocks[4 * m + k], 4 * m) for k in range(4)]
    return total


def seen(first_row, part, key_block, query_block, size):
    turned = part * (size // 4)
    key = key_block * size + (lax.broadcasted_iota(jnp.int32, (size, 1), 0) ^ turned)
    query = query_block * size + (lax.broadcasted_iota(jnp.int32, (1, size), 1) ^ turned)
    return (key <= query) & (key >= first_row)


def attend_kernel(count, place_ref, first_ref, *refs):
    blocks, (out_ref, low_ref, lse_ref, kt_ref, v_ref) = refs[:count], refs[count:]
    size = blocks[0].shape[2]
    x, part = place_ref[0], place_ref[1]
    for k in range(count):
        kt_ref[x ^ k] = blocks[k][1].T
        v_ref[x ^ k] = blocks[k][2]
    for k in range(4):
        block = x ^ k
        query = blocks[k][0] * BF(HEAD ** (-0.5))
        first_row = first_ref[k]

        def step(kb, carry):
            peak, total, acc = carry
            s = mm(kt_ref[kb], query)
            s = jnp.where(seen(first_row, part, kb, block, size), s, NEG)
            top = jnp.maximum(peak, jnp.max(s, axis=0, keepdims=True))
            p = jnp.exp(s - top)
            fade = jnp.exp(peak - top)
            total = fade * total + jnp.sum(p, axis=0, keepdims=True)
            return top, total, fade * acc + mm(v_ref[kb], p.astype(BF))

        start = (
            jnp.full((1, size), NEG, F32),
            jnp.zeros((1, size), F32),
            jnp.zeros((HEAD, size), F32),
        )
        peak, total, acc = lax.fori_loop(place_ref[2 + block], block + 1, step, start)
        acc = acc / total
        out_ref[k] = acc
        low_ref[k] = acc.astype(BF)
        lse_ref[k] = peak + jnp.log(total)


def attend(where_all, first_query, blocks):
    count = len(blocks)
    size = blocks[0].shape[2]
    return pl.pallas_call(
        functools.partial(attend_kernel, count),
        out_shape=(
            jax.ShapeDtypeStruct((4, HEAD, size), F32),
            jax.ShapeDtypeStruct((4, HEAD, size), BF),
            jax.ShapeDtypeStruct((4, 1, size), F32),
        ),
        in_specs=[IN_SMEM] + [IN_VMEM] * (1 + count),
        out_specs=(IN_VMEM,) * 3,
        scratch_shapes=[
            pltpu.VMEM((count, size, HEAD), BF),
            pltpu.VMEM((count, HEAD, size), BF),
        ],
        name="attend",
    )(where_all, first_query, *blocks)


def back_kernel(count, place_ref, first_ref, out_ref, lse_ref, *refs):
    blocks, grads = refs[:count], refs[count : count + 4]
    dq_ref, dk_ref, dv_ref, kt_ref, vt_ref, k_ref, dks_ref, dvs_ref = refs[count + 4 :]
    size = blocks[0].shape[2]
    x, part = place_ref[0], place_ref[1]
    for k in range(count):
        kt_ref[x ^ k] = blocks[k][1].T
        vt_ref[x ^ k] = blocks[k][2].T
        k_ref[x ^ k] = blocks[k][1]
    dks_ref[...] = jnp.zeros_like(dks_ref)
    dvs_ref[...] = jnp.zeros_like(dvs_ref)
    for k in range(4):
        block = x ^ k
        query = blocks[k][0] * BF(HEAD ** (-0.5))
        query_t = query.T
        grad = grads[k][...]
        grad_t = grad.T
        delta = jnp.sum(grad.astype(F32) * out_ref[k], axis=0, keepdims=True)
        lse = lse_ref[k]
        first_row = first_ref[k]

        def step(kb, dq):
            s = mm(kt_ref[kb], query)
            p = jnp.where(seen(first_row, part, kb, block, size), jnp.exp(s - lse), 0.0)
            dp = mm(vt_ref[kb], grad)
            ds = (p * (dp - delta)).astype(BF)
            dvs_ref[kb] += mm(p.astype(BF), grad_t)
            dks_ref[kb] += mm(ds, query_t)
            return dq + mm(k_ref[kb], ds)

        dq = lax.fori_loop(
            place_ref[2 + block], block + 1, step, jnp.zeros((HEAD, size), F32)
        )
        dq_ref[k] = dq * HEAD ** (-0.5)
    for k in range(count):
        dk_ref[k] = dks_ref[x ^ k].T
        dv_ref[k] = dvs_ref[x ^ k].T


def attend_back(where_all, first_query, blocks, grads, out, log_total):
    count = len(blocks)
    size = blocks[0].shape[2]
    return pl.pallas_call(
        functools.partial(back_kernel, count),
        out_shape=(
            jax.ShapeDtypeStruct((4, HEAD, size), F32),
            jax.ShapeDtypeStruct((count, HEAD, size), F32),
            jax.ShapeDtypeStruct((count, HEAD, size), F32),
        ),
        in_specs=[IN_SMEM] + [IN_VMEM] * (3 + count + 4),
        out_specs=(IN_VMEM,) * 3,
        scratch_shapes=[
            pltpu.VMEM((count, size, HEAD), BF),
            pltpu.VMEM((count, size, HEAD), BF),
            pltpu.VMEM((count, HEAD, size), BF),
            pltpu.VMEM((count, size, HEAD), F32),
            pltpu.VMEM((count, size, HEAD), F32),
        ],
        name="attend_back",
    )(where_all, first_query, out, log_total, *blocks, *grads)


def norm_scale(stream):
    return lax.rsqrt(jnp.mean(stream * stream, axis=-1, keepdims=True) + EPS)


def norm_back(stream, scale, gain, grad_normed):
    weighted = grad_normed * gain
    grad_gain = jnp.sum(grad_normed * stream * scale, axis=0, keepdims=True)
    grad_stream = scale * weighted - stream * scale**3 * jnp.mean(
        weighted * stream, axis=1, keepdims=True
    )
    return (grad_gain, grad_stream)


def local(
    tokens,
    out_grad,
    segment_ids,
    owner_order,
    attn_gain,
    w_query,
    w_key,
    w_value,
    w_out,
    mlp_gain,
    w_gate,
    w_up,
    w_down,
):
    plan = Plan()
    tok_rows = tokens.shape[0]
    part_rows = tok_rows // 4
    model = tokens.shape[1]

    gains = jnp.concatenate([attn_gain, mlp_gain], axis=0)
    gains = jnp.concatenate([gains, jnp.zeros((12, gains.shape[1]), BF)], axis=0)
    qkv_rows = 3 * w_query.shape[2] // 2
    out_rows = w_out.shape[1] // 2
    mlp_rows = w_down.shape[1] // 2
    counts = [qkv_rows, out_rows] + [mlp_rows] * 3

    def own_weights(level):
        qkv = [split_hidden(w[level].T) for w in (w_query, w_key, w_value)]
        return [
            jnp.concatenate(qkv, axis=1),
            split_hidden(w_out[level]),
            split_hidden(w_gate[level].T),
            split_hidden(w_up[level].T),
            split_hidden(w_down[level]),
        ]

    groups = own_weights(0)
    own = own_columns(plan, groups[0])
    far_first = plan.far(own)
    own_rest = own_columns(plan, jnp.concatenate(groups[1:], axis=1))
    got = plan.core(gains)
    gain_pair = jnp.where(
        plan.c == 0,
        jnp.concatenate([gains, got], axis=1),
        jnp.concatenate([got, gains], axis=1),
    )
    own_rest, far_first = together(own_rest, far_first)
    first = jnp.concatenate([own, far_first, gain_pair], axis=0)
    first = all_columns(plan, first, True)
    w_qkv, gain_full = first[: 2 * qkv_rows], first[2 * qkv_rows :].astype(F32)
    last_far = plan.far(own_rest)
    own_later = []
    for level in range(1, LAYERS):
        own = own_columns(plan, jnp.concatenate(own_weights(level), axis=1))
        own_later.append(own)
    cuts = [0, qkv_rows + out_rows]
    for _ in range(3):
        cuts.append(cuts[-1] + mlp_rows)
    full = [(w_qkv, None, None)]
    def own_rows(array):
        mine = lax.dynamic_slice_in_dim(array, plan.part * part_rows, part_rows, 0)
        got = plan.core(
            lax.dynamic_slice_in_dim(array, (plan.part ^ 2) * part_rows, part_rows, 0)
        )
        return to_block_order(plan, jnp.where(plan.c == plan.zp, mine, got))

    token_rows = own_rows(tokens)
    tokens_all = gather_rows(plan, token_rows).astype(F32)
    stream = token_rows.astype(F32)
    grad_stream = own_rows(out_grad).astype(F32)

    segment = jnp.where(plan.c == plan.zp, segment_ids, plan.core(segment_ids))[0]
    pack = segment.shape[0]
    index_all = jnp.arange(pack, dtype=jnp.int32)
    run_start = jnp.concatenate([jnp.ones((1,), dtype=bool), segment[1:] != segment[:-1]])
    run_first = lax.cummax(jnp.where(run_start, index_all, jnp.zeros_like(index_all)), axis=0)
    where_all = jnp.concatenate(
        [jnp.stack([plan.x, plan.part]).astype(jnp.int32), run_first[::tok_rows] // tok_rows]
    )

    def by_peer(row):
        grid = row.reshape(plan.ctx, 4, part_rows)
        blocks = [lax.dynamic_index_in_dim(grid, plan.x ^ k, 0, False) for k in range(4)]
        grid = jnp.stack(blocks)
        return jnp.concatenate(flip_list([grid[:, i] for i in range(4)], plan.part), axis=1)

    positions = by_peer((index_all - run_first).astype(F32))
    first_query = by_peer(run_first)[:, None, :]
    frequency = THETA ** (-(jnp.arange(HALF, dtype=F32) * 2.0 / HEAD))
    angles = frequency[None, :, None] * positions[:, None, :]
    cos_all, sine_all = jnp.cos(angles), jnp.sin(angles)
    cos_own, sine_own = cos_all[0], sine_all[0]

    kept = []
    first_values = None
    out_branch = None
    for level in range(LAYERS):
        w_qkv, w_o, w_mlp = full[level]
        width = 2 * mlp_rows
        if level == 0:
            scale_all = norm_scale(tokens_all)
            scale_attn = scale_all[:part_rows]
            normed_all = (tokens_all * scale_all * gain_full[:1]).astype(BF)
        else:
            scale_attn = norm_scale(stream)
            normed = (stream * scale_attn * gain_full[level : level + 1]).astype(BF)
            normed_all = gather_rows(plan, normed)
        qkv = dot(w_qkv, normed_all, 1, 1)
        if level == 0:
            rest = with_far(own_rest, last_far, counts[1:])
            rest, w_o = rest[2 * out_rows :], rest[: 2 * out_rows]
            rest, qkv = together(rest, qkv)
            rest = all_columns(plan, rest, False)
            w_mlp = (rest[: 2 * width], rest[2 * width :])
        qkv = qkv.reshape(2, 3, 2, HEAD, tok_rows)
        query = turn(qkv[:, 0], cos_own, sine_own).astype(BF)
        key = turn(qkv[:, 1], cos_own, sine_own).astype(BF)
        if level == 0:
            first_values = qkv[:, 2]
            mixed = first_values
        else:
            mixed = 0.5 * qkv[:, 2] + 0.5 * first_values
        heads = jnp.stack([query, key, mixed.astype(BF)], axis=2)
        heads = more_keys(plan, to_heads(plan, heads.reshape(4, 3, HEAD, tok_rows)))
        ahead = level + 1 < LAYERS
        far_next = []

        def next_far():
            i = len(far_next)
            piece = own_later[level][cuts[i] : cuts[i + 1]]
            if far_next:
                piece, far_next[-1] = together(piece, far_next[-1])
            return plan.far(piece)

        if ahead:
            heads, got = together(heads, next_far())
            far_next.append(got)
        if level == 0:
            heads, w_o = together(heads, w_o)
            w_o = all_columns(plan, w_o, True)
        out, out_low, log_total = attend(where_all, first_query, heads)
        if ahead:
            out_low, got = together(out_low, next_far())
            far_next.append(got)
        if level == LAYERS - 1:
            out_low, out_branch = together(out_low, gather_rows(plan, grad_stream.astype(BF)))
        attended = from_heads(plan, [out_low[k] for k in range(4)])
        attended = attended.reshape(4 * HEAD, tok_rows)
        if ahead:
            attended, got = together(attended, next_far())
            far_next.append(got)
        branch = sum_rows(plan, dot(attended, w_o, 0, 0))
        if ahead:
            branch, got = together(branch, next_far())
            far_next.append(got)
            own = own_later[level]
            w_attn = with_far(own[: cuts[1]], far_next[0], counts[:2])
            w_attn = all_columns(plan, w_attn, False)
            rest = with_far(own[cuts[1] :], jnp.concatenate(far_next[1:], axis=0), counts[2:])
            rest = all_columns(plan, rest, False)
            later = (rest[: 2 * width], rest[2 * width :])
            full.append((w_attn[: 2 * qkv_rows], w_attn[2 * qkv_rows :], later))
        middle = stream + branch
        scale_mlp = norm_scale(middle)
        normed_mlp = (middle * scale_mlp * gain_full[2 + level : 3 + level]).astype(BF)
        normed_mlp_all = gather_rows(plan, normed_mlp)
        w_gu, w_d = w_mlp
        full[level] = (w_qkv, w_o, w_gu, w_d)
        gate_up = dot(normed_mlp_all, w_gu, 1, 1)
        gate, upward = gate_up[:, :width], gate_up[:, width:]
        hidden = (gate * jax.nn.sigmoid(gate) * upward).astype(BF)
        if level < LAYERS - 1:
            result = middle + sum_rows(plan, dot(hidden, w_d, 1, 0))
        kept.append(
            (
                stream,
                scale_attn,
                normed_all,
                heads,
                out,
                log_total,
                attended,
                middle,
                scale_mlp,
                normed_mlp_all,
                gate_up,
                hidden,
            )
        )
        if level < LAYERS - 1:
            stream = result

    def to_pack(rows, other):
        mine = jnp.where(plan.c == plan.zp, rows, other)
        got = plan.core(jnp.where(plan.c == plan.zp, other, rows))
        count = rows.shape[0]
        near = plan.near(jnp.concatenate([mine, got], axis=0))
        return jnp.concatenate([mine, near[:count], got, near[count:]], axis=0)


    def weight_grads(grad_qkv, grad_wo, grad_wg, grad_wu, grad_wd):
        third = qkv_rows // 3

        def member(i):
            rows = [half[i * third : (i + 1) * third] for half in grad_qkv]
            return jnp.concatenate(rows, axis=0).T

        return (
            member(0),
            member(1),
            member(2),
            jnp.concatenate(grad_wo, axis=0),
            jnp.concatenate(grad_wg, axis=0).T,
            jnp.concatenate(grad_wu, axis=0).T,
            jnp.concatenate(grad_wd, axis=0),
        )

    grads = [None] * LAYERS
    gain_rows = [None] * (2 * LAYERS)
    carried = None
    for level in reversed(range(LAYERS)):
        (
            stream,
            scale_attn,
            normed_all,
            heads,
            out,
            log_total,
            attended,
            middle,
            scale_mlp,
            normed_mlp_all,
            gate_up,
            hidden,
        ) = kept[level]
        w_qkv, w_o, w_gu, w_d = full[level]
        width = 2 * mlp_rows
        if level == LAYERS - 1:
            branch = out_branch
        else:
            branch = gather_rows(plan, grad_stream.astype(BF))
        grad_hidden = dot(branch, w_d, 1, 1)
        gate, upward = gate_up[:, :width], gate_up[:, width:]
        sigma = jax.nn.sigmoid(gate)
        grad_gate = (grad_hidden * upward * sigma * (1.0 + gate * (1.0 - sigma))).astype(BF)
        grad_up = (grad_hidden * gate * sigma).astype(BF)
        grad_gu = jnp.concatenate([grad_gate, grad_up], axis=1)
        partial, grad_gu = together(dot(grad_gu, w_gu, 1, 0), grad_gu)
        grad_normed = sum_rows(plan, partial)
        grad_wd = dot(hidden, branch, 0, 0).astype(BF)
        grad_wgu = dot(grad_gu, normed_mlp_all, 0, 0).astype(BF)
        grad_mlp = jnp.concatenate([grad_wgu, grad_wd], axis=0)
        if level == 0:
            grad_normed, grad_mlp, sum_attn = together(grad_normed, grad_mlp, sum_attn)
        else:
            grad_normed, grad_mlp = together(grad_normed, grad_mlp)
        sum_mlp = columns_sum(plan, grad_mlp, False)
        gain_rows[2 + level], through = norm_back(
            middle, scale_mlp, gain_full[2 + level : 3 + level], grad_normed
        )
        grad_middle = grad_stream + through
        branch = gather_rows(plan, grad_middle.astype(BF))
        if level == 0:
            later_mlp, branch = together(later_mlp, branch)
            mine_mlp, far = far_halves(later_mlp, counts[2:])
            mine_attn, far_attn = far_halves(sum_attn, counts[:2])
            far_a = plan.far(far[: 2 * mlp_rows])
        if level == LAYERS - 1:
            partial, branch = together(dot(hidden, w_d, 1, 0), branch)
            last = sum_rows(plan, partial)
        grad_wo = dot(attended, branch, 1, 0).astype(BF)
        grad_attended = dot(w_o, branch, 1, 1).astype(BF)
        grad_attended = to_heads(plan, grad_attended.reshape(4, HEAD, tok_rows))
        if level == 0:
            far_b, far_a = together(far[2 * mlp_rows :], far_a)
            far_b = plan.far(far_b)
            grad_attended, far_a, grad_wo = together(grad_attended, far_a, grad_wo)
            sum_wo = columns_sum(plan, grad_wo, True)
        elif level == LAYERS - 1:
            grad_attended, last = together(grad_attended, last)
            last = from_block_order(plan, (middle + last).astype(BF))
            other = plan.far(last)
        grad_q, grad_k, grad_v = attend_back(
            where_all, first_query, heads, grad_attended, out, log_total
        )
        if level == 0:
            far_attn, far_b = together(far_attn, far_b)
            far_c = plan.far(far_attn)
            grad_q, far_b, sum_wo = together(grad_q, far_b, sum_wo)
        elif level == LAYERS - 1:
            grad_q, other = together(grad_q, other)
            last = to_pack(last, other)
        grad_k = more_keys_sum(plan, grad_k)
        grad_v = more_keys_sum(plan, grad_v)
        if level > 0:
            grad_v = [0.5 * block for block in grad_v]
            if carried is None:
                carried = grad_v
            else:
                carried = [left + right for left, right in zip(carried, grad_v)]
        else:
            grad_v = [left + right for left, right in zip(grad_v, carried)]
        grad_heads = [
            jnp.stack(
                [
                    turn(grad_q[k], cos_all[k], -sine_all[k]).astype(BF),
                    turn(grad_k[k], cos_all[k], -sine_all[k]).astype(BF),
                    grad_v[k].astype(BF),
                ]
            )
            for k in range(4)
        ]
        grad_qkv = from_heads(plan, grad_heads).reshape(2, 2, 3, HEAD, tok_rows)
        grad_qkv = jnp.swapaxes(grad_qkv, 1, 2).reshape(-1, tok_rows)
        if level == 0:
            mine_first, far = far_halves(sum_mlp, counts[2:])
            far_d, far_c = together(far[: 2 * mlp_rows], far_c)
            far_d = plan.far(far_d)
            grad_qkv, far_c = together(grad_qkv, far_c)
        elif level == LAYERS - 1:
            grad_qkv, last = together(grad_qkv, last)
            outputs = natural_rows(plan, last)
        grad_wqkv = dot(grad_qkv, normed_all, 1, 0).astype(BF)
        grad_normed = sum_rows(plan, dot(grad_qkv, w_qkv, 0, 0))
        if level == 0:
            far_e = far[2 * mlp_rows :]
            grad_normed, far_d, far_e, grad_wqkv = together(
                grad_normed, far_d, far_e, grad_wqkv
            )
            far_e = plan.far(far_e)
            sum_qkv = columns_sum(plan, grad_wqkv, True)
            got = jnp.concatenate([far_c, far_a, far_b], axis=0).astype(F32)
            mine = jnp.concatenate([mine_attn, mine_mlp], axis=0)
            grads[1] = weight_grads(*core_halves(plan, mine + got, counts))
        else:
            grad_normed, later_mlp = together(grad_normed, sum_mlp)
            grad_attn = jnp.concatenate([grad_wqkv, grad_wo], axis=0)
            sum_attn = columns_sum(plan, grad_attn, False)
        gain_rows[level], through = norm_back(
            stream, scale_attn, gain_full[level : level + 1], grad_normed
        )
        grad_stream = grad_middle + through

    rows = from_block_order(plan, grad_stream.astype(BF))
    other, sum_qkv = together(plan.far(rows), sum_qkv)
    group_rows = tok_rows // plan.ctx
    owner_grid = owner_order[0].reshape(plan.ctx, plan.ctx, group_rows)
    local_rows = (
        lax.dynamic_index_in_dim(owner_grid, plan.x, 1, False) - plan.x * tok_rows
    ).reshape(tok_rows)
    local_rows = local_rows ^ (plan.part * part_rows)
    slots, far_e = together(to_pack(rows, other)[local_rows], far_e)
    grad_tokens = lax.all_to_all(slots, "ctx", split_axis=0, concat_axis=0, tiled=True)

    got = jnp.concatenate([far_d, far_e], axis=0).astype(F32)
    rest = core_halves(plan, mine_first + got, counts[2:])
    gain_sum = jnp.concatenate(gain_rows + [jnp.zeros((12, model), F32)], axis=0)
    gain_sum = gain_sum + plan.near(gain_sum)
    gain_sum = columns_sum(plan, gain_sum, True)
    mine, far = far_halves(jnp.concatenate([sum_qkv, sum_wo], axis=0), counts[:2])
    far = jnp.concatenate([far, gain_sum.astype(BF)], axis=0)
    far = plan.far(far)
    grad_tokens, far = together(grad_tokens, far)
    grad_tokens = grad_tokens.astype(F32)
    total = jnp.concatenate([mine, gain_sum], axis=0) + far.astype(F32)
    first = core_halves(plan, total, [qkv_rows, out_rows, gain_sum.shape[0]])
    total = first[2][0] + first[2][1]
    grads[0] = weight_grads(first[0], first[1], *rest)

    stacked = [jnp.stack([grads[level][i] for level in range(LAYERS)]) for i in range(7)]
    return (
        outputs,
        grad_tokens,
        total[:2],
        stacked[0],
        stacked[1],
        stacked[2],
        stacked[3],
        total[2:4],
        stacked[4],
        stacked[5],
        stacked[6],
    )


def solution(mesh):
    columns = P(None, ("fsdp", "ctx"), "tp")
    rows = P(None, "tp", ("fsdp", "ctx"))
    gain = P(None, ("fsdp", "ctx"))
    tokens = P(("fsdp", "ctx"), None)
    return jax.shard_map(
        local,
        mesh=mesh,
        in_specs=(
            tokens,
            tokens,
            P("fsdp", None),
            P("fsdp", None),
            gain,
            columns,
            columns,
            columns,
            rows,
            gain,
            columns,
            columns,
            rows,
        ),
        out_specs=(
            tokens,
            tokens,
            gain,
            columns,
            columns,
            columns,
            rows,
            gain,
            columns,
            columns,
            rows,
        ),
        check_vma=False,
    )
```

profile of v0, /device:TPU:0, one launch (start us, length us, event | category | flops | bytes accessed | tf_op | source)
XLA Modules:
  0.0 577.1 jit_solution(483526873392371706)
XLA Ops:
  17.8 3.8 collective-permute-start.4
  23.8 7.6 %collective-permute-done.4 = bf16[384,256]{1,0:T(8,128)(2,1)S(1)} collective-permute-done((bf16[384,256]{1,0:T(8,128)(2,1)S(1)}, bf16[384,256]{1,0:T(8,128)(2,1)S(1)}, u32[]{:S(2)}, u32[]{:S(2)}) %collective-permute-start.4) | collective-permute-done | bytes 196640 | tf_op jit(solution)/shard_map/ppermute | solution.py:56
  36.8 7.1 %collective-permute-done.7 = bf16[784,256]{1,0:T(8,128)(2,1)S(1)} collective-permute-done((bf16[784,256]{1,0:T(8,128)(2,1)S(1)}, bf16[784,256]{1,0:T(8,128)(2,1)S(1)}, u32[]{:S(2)}, u32[]{:S(2)}) %collective-permute-start.7) | collective-permute-done | bytes 401440 | tf_op jit(solution)/shard_map/ppermute | solution.py:59
  43.9 8.3 %collective-permute-done.8 = bf16[784,256]{1,0:T(8,128)(2,1)S(1)} collective-permute-done((bf16[784,256]{1,0:T(8,128)(2,1)S(1)}, bf16[784,256]{1,0:T(8,128)(2,1)S(1)}, u32[]{:S(2)}, u32[]{:S(2)}) %collective-permute-start.8) | collective-permute-done | bytes 401440 | tf_op jit(solution)/shard_map/ppermute | solution.py:59
  52.3 11.9 %collective-permute-done.5 = bf16[1184,256]{1,0:T(8,128)(2,1)S(1)} collective-permute-done((bf16[1184,256]{1,0:T(8,128)(2,1)S(1)}, bf16[1184,256]{1,0:T(8,128)(2,1)S(1)}, u32[]{:S(2)}, u32[]{:S(2)}) %collective-permute-start.5) | collective-permute-done | bytes 606240 | tf_op jit(solution)/shard_map/ppermute | solution.py:56
  69.1 3.3 fusion.17
  82.9 6.1 %collective-permute-done.16 = bf16[512,256]{1,0:T(8,128)(2,1)S(1)} collective-permute-done((bf16[512,256]{1,0:T(8,128)(2,1)S(1)}, bf16[512,256]{1,0:T(8,128)(2,1)S(1)}, u32[]{:S(2)}, u32[]{:S(2)}) %collective-permute-start.16) | collective-permute-done | bytes 262176 | tf_op jit(solution)/shard_map/ppermute | solution.py:56
  91.3 6.3 %collective-permute-done.15.refs_3_ = bf16[3,64,512]{2,1,0:T(8,128)(2,1)S(1)} collective-permute-done((bf16[3,64,512]{2,1,0:T(8,128)(2,1)S(1)}, bf16[3,64,512]{2,1,0:T(8,128)(2,1)S(1)}, u32[]{:S(2)}, u32[]{:S(2)}) %collective-permute-start.15) | collective-permute-done | bytes 196640 | tf_op jit(solution)/shard_map/ppermute | solution.py:59
  101.9 2.9 collective-permute-start.17
  105.8 6.4 %attend.2 = (f32[4,64,512]{2,1,0:T(8,128)}, bf16[4,64,512]{2,1,0:T(8,128)(2,1)}, f32[4,1,512]{2,1,0:T(1,128)}) custom-call(s32[6]{0:T(128)} %pad_add_fusion.2.place_ref, s32[4,1,512]{2,1,0:T(1,128)} %broadcast_in_dim.84.first_ref, bf16[3,64,512]{2,1,0:T(8,128)(2,1)} %get-tuple-element.111.refs_0_, bf16[3,64,512]{2,1,0:T(8,128)(2,1)} %copy-done.42, ...), custom_call_target="tpu_custom_call" | custom-call | tf_op jit(solution)/shard_map/attend/pallas_call | solution.py:291
  121.0 3.4 collective-permute-done.19
  124.8 3.1 collective-permute-done.21
  133.4 3.1 collective-permute-start.27
  136.6 5.7 collective-permute-done.26
  148.4 4.2 collective-permute-done.28
  155.3 4.0 fusion.6
  169.0 6.3 %collective-permute-done.31 = bf16[128,1024]{1,0:T(8,128)(2,1)} collective-permute-done((bf16[128,1024]{1,0:T(8,128)(2,1)}, bf16[128,1024]{1,0:T(8,128)(2,1)}, u32[]{:S(2)}, u32[]{:S(2)}) %collective-permute-start.31) | collective-permute-done | bytes 262176 | tf_op jit(solution)/shard_map/ppermute | solution.py:53
  180.3 5.0 collective-permute-done.32
  188.0 7.8 %collective-permute-done.38 = bf16[128,1024]{1,0:T(8,128)(2,1)S(1)} collective-permute-done((bf16[128,1024]{1,0:T(8,128)(2,1)S(1)}, bf16[128,1024]{1,0:T(8,128)(2,1)S(1)}, u32[]{:S(2)}, u32[]{:S(2)}) %collective-permute-start.38) | collective-permute-done | bytes 262176 | tf_op jit(solution)/shard_map/ppermute | solution.py:53
  207.1 3.3 collective-permute-done.34.refs_1_
  211.0 4.6 collective-permute-done.36.refs_3_
  215.6 6.9 %attend.3 = (f32[4,64,512]{2,1,0:T(8,128)}, bf16[4,64,512]{2,1,0:T(8,128)(2,1)}, f32[4,1,512]{2,1,0:T(1,128)}) custom-call(s32[6]{0:T(128)} %pad_add_fusion.2.place_ref, s32[4,1,512]{2,1,0:T(1,128)} %broadcast_in_dim.84.first_ref, bf16[3,64,512]{2,1,0:T(8,128)(2,1)} %get-tuple-element.341.refs_0_, bf16[3,64,512]{2,1,0:T(8,128)(2,1)} %copy-done.45, ...), custom_call_target="tpu_custom_call" | custom-call | tf_op jit(solution)/shard_map/attend/pallas_call | solution.py:291
  237.9 6.9 %collective-permute-done.44 = bf16[128,1024]{1,0:T(8,128)(2,1)S(1)} collective-permute-done((bf16[128,1024]{1,0:T(8,128)(2,1)S(1)}, bf16[128,1024]{1,0:T(8,128)(2,1)S(1)}, u32[]{:S(2)}, u32[]{:S(2)}) %collective-permute-start.44) | collective-permute-done | bytes 262176 | tf_op jit(solution)/shard_map/ppermute | solution.py:53
  246.6 6.0 %collective-permute-done.45 = bf16[128,1024]{1,0:T(8,128)(2,1)S(1)} collective-permute-done((bf16[128,1024]{1,0:T(8,128)(2,1)S(1)}, bf16[128,1024]{1,0:T(8,128)(2,1)S(1)}, u32[]{:S(2)}, u32[]{:S(2)}) %collective-permute-start.45) | collective-permute-done | bytes 262176 | tf_op jit(solution)/shard_map/ppermute | solution.py:53
  255.8 4.0 fusion.2
  273.4 4.9 collective-permute-done.48
  282.7 6.2 %collective-permute-done.49 = bf16[128,1024]{1,0:T(8,128)(2,1)S(1)} collective-permute-done((bf16[128,1024]{1,0:T(8,128)(2,1)S(1)}, bf16[128,1024]{1,0:T(8,128)(2,1)S(1)}, u32[]{:S(2)}, u32[]{:S(2)}) %collective-permute-start.49) | collective-permute-done | bytes 262176 | tf_op jit(solution)/shard_map/ppermute | solution.py:53
  315.0 3.7 collective-permute-start.56
  318.7 8.7 %attend_back.2 = (f32[4,64,512]{2,1,0:T(8,128)}, f32[4,64,512]{2,1,0:T(8,128)}, f32[4,64,512]{2,1,0:T(8,128)}) custom-call(s32[6]{0:T(128)} %pad_add_fusion.2.place_ref, s32[4,1,512]{2,1,0:T(1,128)} %broadcast_in_dim.84.first_ref, f32[4,64,512]{2,1,0:T(8,128)} %get-tuple-element.126.out_ref, f32[4,1,512]{2,1,0:T(1,128)} %get-tuple-element.127.lse_ref, ...), custom_call_target="tpu_custom_call" | custom-call | tf_op jit(solution)/shard_map/attend_back/pallas_call | solution.py:350
  335.7 5.6 collective-permute-done.57
  341.4 7.5 %collective-permute-done.58 = bf16[3,64,512]{2,1,0:T(8,128)(2,1)S(1)} collective-permute-done((bf16[3,64,512]{2,1,0:T(8,128)(2,1)S(1)}, bf16[3,64,512]{2,1,0:T(8,128)(2,1)S(1)}, u32[]{:S(2)}, u32[]{:S(2)}) %collective-permute-start.58) | collective-permute-done | bytes 196640 | tf_op jit(solution)/shard_map/ppermute | solution.py:59
  359.6 4.6 collective-permute-done.63
  368.1 7.2 %collective-permute-done.64 = bf16[128,1024]{1,0:T(8,128)(2,1)S(1)} collective-permute-done((bf16[128,1024]{1,0:T(8,128)(2,1)S(1)}, bf16[128,1024]{1,0:T(8,128)(2,1)S(1)}, u32[]{:S(2)}, u32[]{:S(2)}) %collective-permute-start.64) | collective-permute-done | bytes 262176 | tf_op jit(solution)/shard_map/ppermute | solution.py:53
  390.4 5.9 %collective-permute-done.67 = bf16[128,1024]{1,0:T(8,128)(2,1)S(1)} collective-permute-done((bf16[128,1024]{1,0:T(8,128)(2,1)}, bf16[128,1024]{1,0:T(8,128)(2,1)S(1)}, u32[]{:S(2)}, u32[]{:S(2)}) %collective-permute-start.67) | collective-permute-done | bytes 262176 | tf_op jit(solution)/shard_map/ppermute | solution.py:53
  402.9 6.2 %collective-permute-done.68 = bf16[128,1024]{1,0:T(8,128)(2,1)S(1)} collective-permute-done((bf16[128,1024]{1,0:T(8,128)(2,1)S(1)}, bf16[128,1024]{1,0:T(8,128)(2,1)S(1)}, u32[]{:S(2)}, u32[]{:S(2)}) %collective-permute-start.68) | collective-permute-done | bytes 262176 | tf_op jit(solution)/shard_map/ppermute | solution.py:53
  418.8 12.4 %collective-permute-done.73 = bf16[704,256]{1,0:T(8,128)(2,1)S(1)} collective-permute-done((bf16[704,256]{1,0:T(8,128)(2,1)S(1)}, bf16[704,256]{1,0:T(8,128)(2,1)S(1)}, u32[]{:S(2)}, u32[]{:S(2)}) %collective-permute-start.73) | collective-permute-done | bytes 360480 | tf_op jit(solution)/shard_map/ppermute | solution.py:56
  432.1 3.1 collective-permute-start.77
  435.8 8.8 %attend_back.3 = (f32[4,64,512]{2,1,0:T(8,128)}, f32[4,64,512]{2,1,0:T(8,128)}, f32[4,64,512]{2,1,0:T(8,128)}) custom-call(s32[6]{0:T(128)} %pad_add_fusion.2.place_ref, s32[4,1,512]{2,1,0:T(1,128)} %broadcast_in_dim.84.first_ref, f32[4,64,512]{2,1,0:T(8,128)} %get-tuple-element.156.out_ref, f32[4,1,512]{2,1,0:T(1,128)} %get-tuple-element.157.lse_ref, ...), custom_call_target="tpu_custom_call" | custom-call | tf_op jit(solution)/shard_map/attend_back/pallas_call | solution.py:350
  453.4 4.6 collective-permute-start.81
  458.1 4.3 collective-permute-done.80
  464.7 3.8 collective-permute-done.81
  477.6 13.3 %collective-permute-done.83 = bf16[128,1024]{1,0:T(8,128)(2,1)S(1)} collective-permute-done((bf16[128,1024]{1,0:T(8,128)(2,1)S(1)}, bf16[128,1024]{1,0:T(8,128)(2,1)S(1)}, u32[]{:S(2)}, u32[]{:S(2)}) %collective-permute-start.83) | collective-permute-done | bytes 262176 | tf_op jit(solution)/shard_map/ppermute | solution.py:53
  495.4 9.3 %collective-permute-done.88 = bf16[768,256]{1,0:T(8,128)(2,1)S(1)} collective-permute-done((bf16[768,256]{1,0:T(8,128)(2,1)S(1)}, bf16[768,256]{1,0:T(8,128)(2,1)S(1)}, u32[]{:S(2)}, u32[]{:S(2)}) %collective-permute-start.88) | collective-permute-done | bytes 393248 | tf_op jit(solution)/shard_map/ppermute | solution.py:59
  504.6 6.5 %collective-permute-done.87 = bf16[768,256]{1,0:T(8,128)(2,1)S(1)} collective-permute-done((bf16[768,256]{1,0:T(8,128)(2,1)S(1)}, bf16[768,256]{1,0:T(8,128)(2,1)S(1)}, u32[]{:S(2)}, u32[]{:S(2)}) %collective-permute-start.87) | collective-permute-done | bytes 393248 | tf_op jit(solution)/shard_map/ppermute | solution.py:59
  518.3 15.0 %collective-permute-done.92 = f32[16,1024]{1,0:T(8,128)S(1)} collective-permute-done((f32[16,1024]{1,0:T(8,128)S(1)}, f32[16,1024]{1,0:T(8,128)S(1)}, u32[]{:S(2)}, u32[]{:S(2)}) %collective-permute-start.92) | collective-permute-done | bytes 65568 | tf_op jit(solution)/shard_map/ppermute | solution.py:53
  543.8 3.5 all-to-all-start
  551.2 7.5 %collective-permute-done.96 = bf16[528,256]{1,0:T(8,128)(2,1)} collective-permute-done((bf16[528,256]{1,0:T(8,128)(2,1)}, bf16[528,256]{1,0:T(8,128)(2,1)}, u32[]{:S(2)}, u32[]{:S(2)}) %collective-permute-start.96) | collective-permute-done | bytes 270368 | tf_op jit(solution)/shard_map/ppermute | solution.py:56
  558.6 3.2 all-to-all-done
  (756 shorter events, 266.0 us)
Async XLA Ops:
  7.2 148.1 %all-gather.6.cloned.1.call-start = ((), (), s32[]{:S(2)}) async-start(), calls=%async_computation.5 | async-start | bytes 5406720 | tf_op jit(solution)/shard_map/all_gather | solution.py:139
  13.5 60.7 %collective-permute-start.1 = (bf16[1568,128]{1,0:T(8,128)(2,1)}, bf16[1568,128]{1,0:T(8,128)(2,1)}, u32[]{:S(2)}, u32[]{:S(2)}) collective-permute-start(bf16[1568,128]{1,0:T(8,128)(2,1)} %get-tuple-element.337), channel_id=1, source_target_pairs={{0,16},{16,0},{1,17},{17,1},{2,18},{18,2},{3,19},{19,3},{4,20},{20... | collective-permute-start | bytes 1204232 | tf_op jit(solution)/shard_map/ppermute | solution.py:50
  17.8 13.5 %collective-permute-start.4 = (bf16[384,256]{1,0:T(8,128)(2,1)S(1)}, bf16[384,256]{1,0:T(8,128)(2,1)S(1)}, u32[]{:S(2)}, u32[]{:S(2)}) collective-permute-start(bf16[384,256]{1,0:T(8,128)(2,1)S(1)} %maximum_select_fusion.2), channel_id=1, source_target_pairs={{0,2},{1,3},{2,0},{3,1},{4,6},{5,7},{6,4},{7,5},{8,10},{9,11},{10,... | collective-permute-start | bytes 589832 | tf_op jit(solution)/shard_map/ppermute | solution.py:56
  21.9 14.0 %collective-permute-start.11 = (bf16[128,1024]{1,0:T(8,128)(2,1)S(1)}, bf16[128,1024]{1,0:T(8,128)(2,1)S(1)}, u32[]{:S(2)}, u32[]{:S(2)}) collective-permute-start(bf16[128,1024]{1,0:T(8,128)(2,1)S(1)} %constant_dynamic-update-slice_fusion.7), channel_id=1, source_target_pairs={{0,1},{1,0},{2,3},{3,2},{4,5},{5,4},{6,7},{7,6},{8,9},{9,8},{10,11... | collective-permute-start | bytes 786440 | tf_op jit(solution)/shard_map/ppermute | solution.py:53
  31.6 12.2 %collective-permute-start.7 = (bf16[784,256]{1,0:T(8,128)(2,1)S(1)}, bf16[784,256]{1,0:T(8,128)(2,1)S(1)}, u32[]{:S(2)}, u32[]{:S(2)}) collective-permute-start(bf16[784,256]{1,0:T(8,128)(2,1)S(1)} %get-tuple-element.383), channel_id=1, source_target_pairs={{0,4},{4,0},{8,12},{12,8},{1,5},{5,1},{9,13},{13,9},{2,6},{6,2},{1... | collective-permute-start | bytes 1204232 | tf_op jit(solution)/shard_map/ppermute | solution.py:59
  33.2 18.9 %collective-permute-start.8 = (bf16[784,256]{1,0:T(8,128)(2,1)S(1)}, bf16[784,256]{1,0:T(8,128)(2,1)S(1)}, u32[]{:S(2)}, u32[]{:S(2)}) collective-permute-start(bf16[784,256]{1,0:T(8,128)(2,1)S(1)} %get-tuple-element.383), channel_id=1, source_target_pairs={{0,8},{4,12},{8,0},{12,4},{1,9},{5,13},{9,1},{13,5},{2,10},{6,14},... | collective-permute-start | bytes 1204232 | tf_op jit(solution)/shard_map/ppermute | solution.py:59
  34.8 17.5 %collective-permute-start.9 = (bf16[784,256]{1,0:T(8,128)(2,1)S(1)}, bf16[784,256]{1,0:T(8,128)(2,1)S(1)}, u32[]{:S(2)}, u32[]{:S(2)}) collective-permute-start(bf16[784,256]{1,0:T(8,128)(2,1)S(1)} %get-tuple-element.383), channel_id=1, source_target_pairs={{0,12},{4,8},{8,4},{12,0},{1,13},{5,9},{9,5},{13,1},{2,14},{6,10},... | collective-permute-start | bytes 1204232 | tf_op jit(solution)/shard_map/ppermute | solution.py:59
  35.9 28.3 %collective-permute-start.5 = (bf16[1184,256]{1,0:T(8,128)(2,1)S(1)}, bf16[1184,256]{1,0:T(8,128)(2,1)S(1)}, u32[]{:S(2)}, u32[]{:S(2)}) collective-permute-start(bf16[1184,256]{1,0:T(8,128)(2,1)S(1)} %maximum_select_fusion.1), channel_id=1, source_target_pairs={{0,2},{1,3},{2,0},{3,1},{4,6},{5,7},{6,4},{7,5},{8,10},{9,11},{10,... | collective-permute-start | bytes 1818632 | tf_op jit(solution)/shard_map/ppermute | solution.py:56
  43.9 23.9 %collective-permute-start.12 = (bf16[256,1024]{1,0:T(8,128)(2,1)}, bf16[256,1024]{1,0:T(8,128)(2,1)}, u32[]{:S(2)}, u32[]{:S(2)}) collective-permute-start(bf16[256,1024]{1,0:T(8,128)(2,1)} %pad_maximum_fusion.22), channel_id=1, source_target_pairs={{0,16},{16,0},{1,17},{17,1},{2,18},{18,2},{3,19},{19,3},{4,20},{20... | collective-permute-start | bytes 1572872 | tf_op jit(solution)/shard_map/ppermute | solution.py:50
  72.4 124.3 %all-gather.4.cloned.1.call-start = ((), (), s32[]{:S(2)}) async-start(), calls=%async_computation.4 | async-start | bytes 2621440 | tf_op jit(solution)/shard_map/all_gather | solution.py:139
  75.6 13.3 %collective-permute-start.16 = (bf16[512,256]{1,0:T(8,128)(2,1)S(1)}, bf16[512,256]{1,0:T(8,128)(2,1)S(1)}, u32[]{:S(2)}, u32[]{:S(2)}) collective-permute-start(bf16[512,256]{1,0:T(8,128)(2,1)S(1)} %slice.1192), channel_id=1, source_target_pairs={{0,2},{1,3},{2,0},{3,1},{4,6},{5,7},{6,4},{7,5},{8,10},{9,11},{10,... | collective-permute-start | bytes 786440 | tf_op jit(solution)/shard_map/ppermute | solution.py:56
  78.1 11.9 %collective-permute-start.13 = (bf16[3,64,512]{2,1,0:T(8,128)(2,1)S(1)}, bf16[3,64,512]{2,1,0:T(8,128)(2,1)S(1)}, u32[]{:S(2)}, u32[]{:S(2)}) collective-permute-start(bf16[3,64,512]{2,1,0:T(8,128)(2,1)S(1)} %get-tuple-element.344), channel_id=1, source_target_pairs={{0,4},{4,0},{8,12},{12,8},{1,5},{5,1},{9,13},{13,9},{2,6},{6,2},{1... | collective-permute-start | bytes 589832 | tf_op jit(solution)/shard_map/ppermute | solution.py:59
  79.4 11.9 %collective-permute-start.14 = (bf16[3,64,512]{2,1,0:T(8,128)(2,1)S(1)}, bf16[3,64,512]{2,1,0:T(8,128)(2,1)S(1)}, u32[]{:S(2)}, u32[]{:S(2)}) collective-permute-start(bf16[3,64,512]{2,1,0:T(8,128)(2,1)S(1)} %get-tuple-element.343), channel_id=1, source_target_pairs={{0,8},{4,12},{8,0},{12,4},{1,9},{5,13},{9,1},{13,5},{2,10},{6,14},... | collective-permute-start | bytes 589832 | tf_op jit(solution)/shard_map/ppermute | solution.py:59
  80.9 16.7 %collective-permute-start.15 = (bf16[3,64,512]{2,1,0:T(8,128)(2,1)S(1)}, bf16[3,64,512]{2,1,0:T(8,128)(2,1)S(1)}, u32[]{:S(2)}, u32[]{:S(2)}) collective-permute-start(bf16[3,64,512]{2,1,0:T(8,128)(2,1)S(1)} %get-tuple-element.342), channel_id=1, source_target_pairs={{0,12},{4,8},{8,4},{12,0},{1,13},{5,9},{9,5},{13,1},{2,14},{6,10},... | collective-permute-start | bytes 589832 | tf_op jit(solution)/shard_map/ppermute | solution.py:59
  97.6 14.6 %collective-permute-start.22 = (bf16[256,256]{1,0:T(8,128)(2,1)}, bf16[256,256]{1,0:T(8,128)(2,1)}, u32[]{:S(2)}, u32[]{:S(2)}) collective-permute-start(bf16[256,256]{1,0:T(8,128)(2,1)} %pad_maximum_fusion.57), channel_id=1, source_target_pairs={{0,4},{4,0},{8,12},{12,8},{1,5},{5,1},{9,13},{13,9},{2,6},{6,2},{1... | collective-permute-start | bytes 393224 | tf_op jit(solution)/shard_map/ppermute | solution.py:59
  100.1 13.1 %collective-permute-start.23 = (bf16[256,256]{1,0:T(8,128)(2,1)}, bf16[256,256]{1,0:T(8,128)(2,1)}, u32[]{:S(2)}, u32[]{:S(2)}) collective-permute-start(bf16[256,256]{1,0:T(8,128)(2,1)} %pad_maximum_fusion.57), channel_id=1, source_target_pairs={{0,8},{4,12},{8,0},{12,4},{1,9},{5,13},{9,1},{13,5},{2,10},{6,14},... | collective-permute-start | bytes 393224 | tf_op jit(solution)/shard_map/ppermute | solution.py:59
  100.8 16.3 %collective-permute-start.24 = (bf16[256,256]{1,0:T(8,128)(2,1)}, bf16[256,256]{1,0:T(8,128)(2,1)}, u32[]{:S(2)}, u32[]{:S(2)}) collective-permute-start(bf16[256,256]{1,0:T(8,128)(2,1)} %pad_maximum_fusion.57), channel_id=1, source_target_pairs={{0,12},{4,8},{8,4},{12,0},{1,13},{5,9},{9,5},{13,1},{2,14},{6,10},... | collective-permute-start | bytes 393224 | tf_op jit(solution)/shard_map/ppermute | solution.py:59
  101.9 12.2 %collective-permute-start.17 = (bf16[352,256]{1,0:T(8,128)(2,1)S(1)}, bf16[352,256]{1,0:T(8,128)(2,1)}, u32[]{:S(2)}, u32[]{:S(2)}) collective-permute-start(bf16[352,256]{1,0:T(8,128)(2,1)S(1)} %get-tuple-element.116), channel_id=1, source_target_pairs={{0,2},{1,3},{2,0},{3,1},{4,6},{5,7},{6,4},{7,5},{8,10},{9,11},{10,... | collective-permute-start | bytes 540680 | tf_op jit(solution)/shard_map/ppermute | solution.py:56
  130.3 17.1 %collective-permute-start.37 = (bf16[128,1024]{1,0:T(8,128)(2,1)}, bf16[128,1024]{1,0:T(8,128)(2,1)}, u32[]{:S(2)}, u32[]{:S(2)}) collective-permute-start(bf16[128,1024]{1,0:T(8,128)(2,1)} %constant_dynamic-slice_fusion.15), channel_id=1, source_target_pairs={{0,16},{16,0},{1,17},{17,1},{2,18},{18,2},{3,19},{19,3},{4,20},{20... | collective-permute-start | bytes 786440 | tf_op jit(solution)/shard_map/ppermute | solution.py:50
  147.1 106.4 %all-gather.8.cloned.1.call-start = ((), (), s32[]{:S(2)}) async-start(), calls=%async_computation.6 | async-start | bytes 5406720 | tf_op jit(solution)/shard_map/all_gather | solution.py:139
  168.9 196.5 %reduce-scatter.4.cloned.1.call-start = ((), (), s32[]{:S(2)}) async-start(), calls=%async_computation.7 | async-start | bytes 5406720 | tf_op jit(solution)/shard_map/reduce_scatter | solution.py:165
  203.9 11.7 %collective-permute-start.36 = (bf16[3,64,512]{2,1,0:T(8,128)(2,1)S(1)}, bf16[3,64,512]{2,1,0:T(8,128)(2,1)}, u32[]{:S(2)}, u32[]{:S(2)}) collective-permute-start(bf16[3,64,512]{2,1,0:T(8,128)(2,1)S(1)} %get-tuple-element.338), channel_id=1, source_target_pairs={{0,12},{4,8},{8,4},{12,0},{1,13},{5,9},{9,5},{13,1},{2,14},{6,10},... | collective-permute-start | bytes 589832 | tf_op jit(solution)/shard_map/ppermute | solution.py:59
  289.9 107.6 %reduce-scatter.6.cloned.1.call-start = ((), (), s32[]{:S(2)}) async-start(), calls=%async_computation.8 | async-start | bytes 2621440 | tf_op jit(solution)/shard_map/reduce_scatter | solution.py:165
  315.0 15.5 %collective-permute-start.56 = (bf16[128,1024]{1,0:T(8,128)(2,1)}, bf16[128,1024]{1,0:T(8,128)(2,1)}, u32[]{:S(2)}, u32[]{:S(2)}) collective-permute-start(bf16[128,1024]{1,0:T(8,128)(2,1)} %constant_dynamic-update-slice_fusion.29), channel_id=1, source_target_pairs={{0,2},{1,3},{2,0},{3,1},{4,6},{5,7},{6,4},{7,5},{8,10},{9,11},{10,... | collective-permute-start | bytes 786440 | tf_op jit(solution)/shard_map/ppermute | solution.py:56
  332.9 16.0 %collective-permute-start.58 = (bf16[3,64,512]{2,1,0:T(8,128)(2,1)S(1)}, bf16[3,64,512]{2,1,0:T(8,128)(2,1)S(1)}, u32[]{:S(2)}, u32[]{:S(2)}) collective-permute-start(bf16[3,64,512]{2,1,0:T(8,128)(2,1)S(1)} %pad_maximum_fusion.52), channel_id=1, source_target_pairs={{0,8},{4,12},{8,0},{12,4},{1,9},{5,13},{9,1},{13,5},{2,10},{6,14},... | collective-permute-start | bytes 589832 | tf_op jit(solution)/shard_map/ppermute | solution.py:59
  333.5 15.4 %collective-permute-start.59 = (bf16[3,64,512]{2,1,0:T(8,128)(2,1)S(1)}, bf16[3,64,512]{2,1,0:T(8,128)(2,1)S(1)}, u32[]{:S(2)}, u32[]{:S(2)}) collective-permute-start(bf16[3,64,512]{2,1,0:T(8,128)(2,1)S(1)} %pad_maximum_fusion.53), channel_id=1, source_target_pairs={{0,12},{4,8},{8,4},{12,0},{1,13},{5,9},{9,5},{13,1},{2,14},{6,10},... | collective-permute-start | bytes 589832 | tf_op jit(solution)/shard_map/ppermute | solution.py:59
  335.7 13.8 %collective-permute-start.61 = (bf16[256,1024]{1,0:T(8,128)(2,1)S(1)}, bf16[256,1024]{1,0:T(8,128)(2,1)S(1)}, u32[]{:S(2)}, u32[]{:S(2)}) collective-permute-start(bf16[256,1024]{1,0:T(8,128)(2,1)S(1)} %pad_maximum_fusion.29), channel_id=1, source_target_pairs={{0,1},{1,0},{2,3},{3,2},{4,5},{5,4},{6,7},{7,6},{8,9},{9,8},{10,11... | collective-permute-start | bytes 1572872 | tf_op jit(solution)/shard_map/ppermute | solution.py:53
  359.4 103.1 %reduce-scatter.8.cloned.1.call-start = ((), (), s32[]{:S(2)}) async-start(), calls=%async_computation.9 | async-start | bytes 5406720 | tf_op jit(solution)/shard_map/reduce_scatter | solution.py:165
  412.0 19.1 %collective-permute-start.73 = (bf16[704,256]{1,0:T(8,128)(2,1)S(1)}, bf16[704,256]{1,0:T(8,128)(2,1)S(1)}, u32[]{:S(2)}, u32[]{:S(2)}) collective-permute-start(bf16[704,256]{1,0:T(8,128)(2,1)S(1)} %pad_maximum_fusion.42), channel_id=1, source_target_pairs={{0,2},{1,3},{2,0},{3,1},{4,6},{5,7},{6,4},{7,5},{8,10},{9,11},{10,... | collective-permute-start | bytes 1081352 | tf_op jit(solution)/shard_map/ppermute | solution.py:56
  414.9 16.3 %collective-permute-start.70 = (bf16[64,512]{1,0:T(8,128)(2,1)S(1)}, bf16[64,512]{1,0:T(8,128)(2,1)S(1)}, u32[]{:S(2)}, u32[]{:S(2)}) collective-permute-start(bf16[64,512]{1,0:T(8,128)(2,1)S(1)} %get-tuple-element.401), channel_id=1, source_target_pairs={{0,4},{4,0},{8,12},{12,8},{1,5},{5,1},{9,13},{13,9},{2,6},{6,2},{1... | collective-permute-start | bytes 196616 | tf_op jit(solution)/shard_map/ppermute | solution.py:59
  415.8 15.4 %collective-permute-start.71 = (bf16[64,512]{1,0:T(8,128)(2,1)S(1)}, bf16[64,512]{1,0:T(8,128)(2,1)S(1)}, u32[]{:S(2)}, u32[]{:S(2)}) collective-permute-start(bf16[64,512]{1,0:T(8,128)(2,1)S(1)} %get-tuple-element.400), channel_id=1, source_target_pairs={{0,8},{4,12},{8,0},{12,4},{1,9},{5,13},{9,1},{13,5},{2,10},{6,14},... | collective-permute-start | bytes 196616 | tf_op jit(solution)/shard_map/ppermute | solution.py:59
  417.0 14.3 %collective-permute-start.72 = (bf16[64,512]{1,0:T(8,128)(2,1)S(1)}, bf16[64,512]{1,0:T(8,128)(2,1)S(1)}, u32[]{:S(2)}, u32[]{:S(2)}) collective-permute-start(bf16[64,512]{1,0:T(8,128)(2,1)S(1)} %get-tuple-element.399), channel_id=1, source_target_pairs={{0,12},{4,8},{8,4},{12,0},{1,13},{5,9},{9,5},{13,1},{2,14},{6,10},... | collective-permute-start | bytes 196616 | tf_op jit(solution)/shard_map/ppermute | solution.py:59
  431.2 17.6 %collective-permute-start.74 = (bf16[352,256]{1,0:T(8,128)(2,1)}, bf16[352,256]{1,0:T(8,128)(2,1)}, u32[]{:S(2)}, u32[]{:S(2)}) collective-permute-start(bf16[352,256]{1,0:T(8,128)(2,1)} %get-tuple-element.168), channel_id=1, source_target_pairs={{0,2},{1,3},{2,0},{3,1},{4,6},{5,7},{6,4},{7,5},{8,10},{9,11},{10,... | collective-permute-start | bytes 540680 | tf_op jit(solution)/shard_map/ppermute | solution.py:56
  432.1 14.9 %collective-permute-start.77 = (bf16[256,256]{1,0:T(8,128)(2,1)}, bf16[256,256]{1,0:T(8,128)(2,1)S(1)}, u32[]{:S(2)}, u32[]{:S(2)}) collective-permute-start(bf16[256,256]{1,0:T(8,128)(2,1)} %get-tuple-element.373), channel_id=1, source_target_pairs={{0,12},{4,8},{8,4},{12,0},{1,13},{5,9},{9,5},{13,1},{2,14},{6,10},... | collective-permute-start | bytes 393224 | tf_op jit(solution)/shard_map/ppermute | solution.py:59
  435.2 11.9 %collective-permute-start.76 = (bf16[256,256]{1,0:T(8,128)(2,1)}, bf16[256,256]{1,0:T(8,128)(2,1)}, u32[]{:S(2)}, u32[]{:S(2)}) collective-permute-start(bf16[256,256]{1,0:T(8,128)(2,1)} %get-tuple-element.374), channel_id=1, source_target_pairs={{0,8},{4,12},{8,0},{12,4},{1,9},{5,13},{9,1},{13,5},{2,10},{6,14},... | collective-permute-start | bytes 393224 | tf_op jit(solution)/shard_map/ppermute | solution.py:59
  435.2 12.5 %collective-permute-start.75 = (bf16[256,256]{1,0:T(8,128)(2,1)S(1)}, bf16[256,256]{1,0:T(8,128)(2,1)}, u32[]{:S(2)}, u32[]{:S(2)}) collective-permute-start(bf16[256,256]{1,0:T(8,128)(2,1)S(1)} %get-tuple-element.372), channel_id=1, source_target_pairs={{0,4},{4,0},{8,12},{12,8},{1,5},{5,1},{9,13},{13,9},{2,6},{6,2},{1... | collective-permute-start | bytes 393224 | tf_op jit(solution)/shard_map/ppermute | solution.py:59
  453.4 15.2 %collective-permute-start.81 = (bf16[512,256]{1,0:T(8,128)(2,1)}, bf16[512,256]{1,0:T(8,128)(2,1)S(1)}, u32[]{:S(2)}, u32[]{:S(2)}) collective-permute-start(bf16[512,256]{1,0:T(8,128)(2,1)} %pad_maximum_fusion.45), channel_id=1, source_target_pairs={{0,2},{1,3},{2,0},{3,1},{4,6},{5,7},{6,4},{7,5},{8,10},{9,11},{10,... | collective-permute-start | bytes 786440 | tf_op jit(solution)/shard_map/ppermute | solution.py:56
  471.6 19.3 %collective-permute-start.84 = (bf16[704,256]{1,0:T(8,128)(2,1)S(1)}, bf16[704,256]{1,0:T(8,128)(2,1)S(1)}, u32[]{:S(2)}, u32[]{:S(2)}) collective-permute-start(bf16[704,256]{1,0:T(8,128)(2,1)S(1)} %pad_maximum_fusion.43), channel_id=1, source_target_pairs={{0,2},{1,3},{2,0},{3,1},{4,6},{5,7},{6,4},{7,5},{8,10},{9,11},{10,... | collective-permute-start | bytes 1081352 | tf_op jit(solution)/shard_map/ppermute | solution.py:56
  474.3 16.6 %collective-permute-start.83 = (bf16[128,1024]{1,0:T(8,128)(2,1)S(1)}, bf16[128,1024]{1,0:T(8,128)(2,1)S(1)}, u32[]{:S(2)}, u32[]{:S(2)}) collective-permute-start(bf16[128,1024]{1,0:T(8,128)(2,1)S(1)} %slice.1786), channel_id=1, source_target_pairs={{0,1},{1,0},{2,3},{3,2},{4,5},{5,4},{6,7},{7,6},{8,9},{9,8},{10,11... | collective-permute-start | bytes 786440 | tf_op jit(solution)/shard_map/ppermute | solution.py:53
  491.7 12.9 %collective-permute-start.88 = (bf16[768,256]{1,0:T(8,128)(2,1)S(1)}, bf16[768,256]{1,0:T(8,128)(2,1)S(1)}, u32[]{:S(2)}, u32[]{:S(2)}) collective-permute-start(bf16[768,256]{1,0:T(8,128)(2,1)S(1)} %get-tuple-element.258), channel_id=1, source_target_pairs={{0,12},{4,8},{8,4},{12,0},{1,13},{5,9},{9,5},{13,1},{2,14},{6,10},... | collective-permute-start | bytes 1179656 | tf_op jit(solution)/shard_map/ppermute | solution.py:59
  492.7 18.4 %collective-permute-start.87 = (bf16[768,256]{1,0:T(8,128)(2,1)S(1)}, bf16[768,256]{1,0:T(8,128)(2,1)S(1)}, u32[]{:S(2)}, u32[]{:S(2)}) collective-permute-start(bf16[768,256]{1,0:T(8,128)(2,1)S(1)} %get-tuple-element.259), channel_id=1, source_target_pairs={{0,8},{4,12},{8,0},{12,4},{1,9},{5,13},{9,1},{13,5},{2,10},{6,14},... | collective-permute-start | bytes 1179656 | tf_op jit(solution)/shard_map/ppermute | solution.py:59
  494.2 16.9 %collective-permute-start.86 = (bf16[768,256]{1,0:T(8,128)(2,1)S(1)}, bf16[768,256]{1,0:T(8,128)(2,1)S(1)}, u32[]{:S(2)}, u32[]{:S(2)}) collective-permute-start(bf16[768,256]{1,0:T(8,128)(2,1)S(1)} %get-tuple-element.257), channel_id=1, source_target_pairs={{0,4},{4,0},{8,12},{12,8},{1,5},{5,1},{9,13},{13,9},{2,6},{6,2},{1... | collective-permute-start | bytes 1179656 | tf_op jit(solution)/shard_map/ppermute | solution.py:59
  495.3 16.1 %collective-permute-start.85 = (bf16[128,1024]{1,0:T(8,128)(2,1)S(1)}, bf16[128,1024]{1,0:T(8,128)(2,1)S(1)}, u32[]{:S(2)}, u32[]{:S(2)}) collective-permute-start(bf16[128,1024]{1,0:T(8,128)(2,1)S(1)} %constant_dynamic-update-slice_fusion.37), channel_id=1, source_target_pairs={{0,2},{1,3},{2,0},{3,1},{4,6},{5,7},{6,4},{7,5},{8,10},{9,11},{10,... | collective-permute-start | bytes 786440 | tf_op jit(solution)/shard_map/ppermute | solution.py:56
  513.7 23.7 %collective-permute-start.90 = (bf16[256,1024]{1,0:T(8,128)(2,1)S(1)}, bf16[256,1024]{1,0:T(8,128)(2,1)S(1)}, u32[]{:S(2)}, u32[]{:S(2)}) collective-permute-start(bf16[256,1024]{1,0:T(8,128)(2,1)S(1)} %pad_maximum_fusion.32), channel_id=1, source_target_pairs={{0,1},{1,0},{2,3},{3,2},{4,5},{5,4},{6,7},{7,6},{8,9},{9,8},{10,11... | collective-permute-start | bytes 1572872 | tf_op jit(solution)/shard_map/ppermute | solution.py:53
  515.5 17.8 %collective-permute-start.92 = (f32[16,1024]{1,0:T(8,128)S(1)}, f32[16,1024]{1,0:T(8,128)S(1)}, u32[]{:S(2)}, u32[]{:S(2)}) collective-permute-start(f32[16,1024]{1,0:T(8,128)S(1)} %concatenate.570), channel_id=1, source_target_pairs={{0,1},{1,0},{2,3},{3,2},{4,5},{5,4},{6,7},{7,6},{8,9},{9,8},{10,11... | collective-permute-start | bytes 196616 | tf_op jit(solution)/shard_map/ppermute | solution.py:53
  518.2 22.1 %collective-permute-start.91 = (bf16[352,256]{1,0:T(8,128)(2,1)}, bf16[352,256]{1,0:T(8,128)(2,1)}, u32[]{:S(2)}, u32[]{:S(2)}) collective-permute-start(bf16[352,256]{1,0:T(8,128)(2,1)} %get-tuple-element.182), channel_id=1, source_target_pairs={{0,2},{1,3},{2,0},{3,1},{4,6},{5,7},{6,4},{7,5},{8,10},{9,11},{10,... | collective-permute-start | bytes 540680 | tf_op jit(solution)/shard_map/ppermute | solution.py:56
  543.8 14.9 %collective-permute-start.96 = (bf16[528,256]{1,0:T(8,128)(2,1)}, bf16[528,256]{1,0:T(8,128)(2,1)}, u32[]{:S(2)}, u32[]{:S(2)}) collective-permute-start(bf16[528,256]{1,0:T(8,128)(2,1)} %pad_maximum_fusion.44), channel_id=1, source_target_pairs={{0,2},{1,3},{2,0},{3,1},{4,6},{5,7},{6,4},{7,5},{8,10},{9,11},{10,... | collective-permute-start | bytes 811016 | tf_op jit(solution)/shard_map/ppermute | solution.py:56
  543.8 18.0 %all-to-all-start = ((bf16[4,128,1024]{2,1,0:T(8,128)(2,1)}), bf16[4,128,1024]{2,1,0:T(8,128)(2,1)S(1)}, u32[]{:S(2)}, u32[]{:S(2)}) async-start(bf16[4,128,1024]{2,1,0:T(8,128)(2,1)} %bitcast.126), calls=%async_computation.3 | async-start | bytes 2097152 | tf_op jit(solution)/shard_map/all_to_all | solution.py:736
  (176 other events, 1120.4 us)
Sparse Core Ops, SparseCore 0:
  72.5 65.6 all-gather.5
  147.2 34.9 all-gather.3
  184.1 58.0 all-gather.7
  290.0 66.9 reduce-scatter.3
  360.3 34.8 reduce-scatter.5
  398.1 57.8 reduce-scatter.7
where the time goes:
time: 586 us; the launch traced here: 577 us
  waiting for transfers between devices  259 us (44%)
  starting transfers between devices  95.3 us (16%)
  other arithmetic  67.9 us (12%)
  local copies, waits for them, and re-layouts  60.5 us (10%)
  matrix products  45.7 us (8%)
  Pallas kernels  30.8 us (5%)
  between operations  17.5 us (3%)
    ppermute x19, waiting for transfers between devices, near(): return lax.ppermute(value, 'tp', [(i, i ^ 1) for i in range(self.tp)])  107 us
    ppermute x39, waiting for transfers between devices, side(): return lax.ppermute(value, 'ctx', [(i, i ^ k) for i in range(self.ctx)])  79.7 us
    ppermute x14, waiting for transfers between devices, far(): return lax.ppermute(value, 'tp', [(i, i ^ 2) for i in range(self.tp)])  55.8 us
    ppermute x39, starting transfers between devices, side(): return lax.ppermute(value, 'ctx', [(i, i ^ k) for i in range(self.ctx)])  46.3 us
    dot_general x24, matrix products, dot(): lax.dot_general(left, right, (((left_dim,), (right_dim,)), ((), ())), pre...  45.7 us
    unnamed x271, local copies, waits for them, and re-layouts  24.3 us
    ppermute x14, starting transfers between devices, far(): return lax.ppermute(value, 'tp', [(i, i ^ 2) for i in range(self.tp)])  21.4 us
    ppermute x19, starting transfers between devices, near(): return lax.ppermute(value, 'tp', [(i, i ^ 1) for i in range(self.tp)])  18.2 us
  transfers between devices with their start and end apart: 107, of which 57 were waited for; matrix products, arithmetic and copies ran while one was open for 26% of the time, Pallas kernels for 5%

commit v1 on v0

--- a/solution.py
+++ b/solution.py
@@ -418,6 +418,26 @@
         ]
 
     groups = own_weights(0)
+    own_later = []
+    for level in range(1, LAYERS):
+        own = own_columns(plan, jnp.concatenate(own_weights(level), axis=1))
+        own_later.append(own)
+    cuts = [0, qkv_rows + out_rows]
+    for _ in range(3):
+        cuts.append(cuts[-1] + mlp_rows)
+    def own_rows(array):
+        mine = lax.dynamic_slice_in_dim(array, plan.part * part_rows, part_rows, 0)
+        got = plan.core(
+            lax.dynamic_slice_in_dim(array, (plan.part ^ 2) * part_rows, part_rows, 0)
+        )
+        return to_block_order(plan, jnp.where(plan.c == plan.zp, mine, got))
+
+    token_rows = own_rows(tokens)
+    tokens_all = gather_rows(plan, token_rows).astype(F32)
+    stream = token_rows.astype(F32)
+    grad_rows = own_rows(out_grad)
+    grad_stream = grad_rows.astype(F32)
+
     own = own_columns(plan, groups[0])
     far_first = plan.far(own)
     own_rest = own_columns(plan, jnp.concatenate(groups[1:], axis=1))
@@ -427,30 +447,12 @@
         jnp.concatenate([gains, got], axis=1),
         jnp.concatenate([got, gains], axis=1),
     )
-    own_rest, far_first = together(own_rest, far_first)
+    own_rest, far_first, grad_rows = together(own_rest, far_first, grad_rows)
+    out_branch = gather_rows(plan, grad_rows)
     first = jnp.concatenate([own, far_first, gain_pair], axis=0)
-    first = all_columns(plan, first, True)
+    first, out_branch = together(all_columns(plan, first, True), out_branch)
     w_qkv, gain_full = first[: 2 * qkv_rows], first[2 * qkv_rows :].astype(F32)
     last_far = plan.far(own_rest)
-    own_later = []
-    for level in range(1, LAYERS):
-        own = own_columns(plan, jnp.concatenate(own_weights(level), axis=1))
-        own_later.append(own)
-    cuts = [0, qkv_rows + out_rows]
-    for _ in range(3):
-        cuts.append(cuts[-1] + mlp_rows)
-    full = [(w_qkv, None, None)]
-    def own_rows(array):
-        mine = lax.dynamic_slice_in_dim(array, plan.part * part_rows, part_rows, 0)
-        got = plan.core(
-            lax.dynamic_slice_in_dim(array, (plan.part ^ 2) * part_rows, part_rows, 0)
-        )
-        return to_block_order(plan, jnp.where(plan.c == plan.zp, mine, got))
-
-    token_rows = own_rows(tokens)
-    tokens_all = gather_rows(plan, token_rows).astype(F32)
-    stream = token_rows.astype(F32)
-    grad_stream = own_rows(out_grad).astype(F32)
 
     segment = jnp.where(plan.c == plan.zp, segment_ids, plan.core(segment_ids))[0]
     pack = segment.shape[0]
@@ -474,9 +476,9 @@
     cos_all, sine_all = jnp.cos(angles), jnp.sin(angles)
     cos_own, sine_own = cos_all[0], sine_all[0]
 
+    full = [(w_qkv, None, None)]
     kept = []
     first_values = None
-    out_branch = None
     for level in range(LAYERS):
         w_qkv, w_o, w_mlp = full[level]
         width = 2 * mlp_rows
@@ -489,12 +491,6 @@
             normed = (stream * scale_attn * gain_full[level : level + 1]).astype(BF)
             normed_all = gather_rows(plan, normed)
         qkv = dot(w_qkv, normed_all, 1, 1)
-        if level == 0:
-            rest = with_far(own_rest, last_far, counts[1:])
-            rest, w_o = rest[2 * out_rows :], rest[: 2 * out_rows]
-            rest, qkv = together(rest, qkv)
-            rest = all_columns(plan, rest, False)
-            w_mlp = (rest[: 2 * width], rest[2 * width :])
         qkv = qkv.reshape(2, 3, 2, HEAD, tok_rows)
         query = turn(qkv[:, 0], cos_own, sine_own).astype(BF)
         key = turn(qkv[:, 1], cos_own, sine_own).astype(BF)
@@ -515,18 +511,16 @@
                 piece, far_next[-1] = together(piece, far_next[-1])
             return plan.far(piece)
 
-        if ahead:
-            heads, got = together(heads, next_far())
-            far_next.append(got)
         if level == 0:
-            heads, w_o = together(heads, w_o)
-            w_o = all_columns(plan, w_o, True)
+            heads, last_far = together(heads, last_far)
+            rest = with_far(own_rest, last_far, counts[1:])
+            w_o = all_columns(plan, rest[: 2 * out_rows], True)
+            rest = all_columns(plan, rest[2 * out_rows :], False)
+            w_mlp = (rest[: 2 * width], rest[2 * width :])
         out, out_low, log_total = attend(where_all, first_query, heads)
         if ahead:
             out_low, got = together(out_low, next_far())
             far_next.append(got)
-        if level == LAYERS - 1:
-            out_low, out_branch = together(out_low, gather_rows(plan, grad_stream.astype(BF)))
         attended = from_heads(plan, [out_low[k] for k in range(4)])
         attended = attended.reshape(4 * HEAD, tok_rows)
         if ahead:
@@ -536,13 +530,6 @@
         if ahead:
             branch, got = together(branch, next_far())
             far_next.append(got)
-            own = own_later[level]
-            w_attn = with_far(own[: cuts[1]], far_next[0], counts[:2])
-            w_attn = all_columns(plan, w_attn, False)
-            rest = with_far(own[cuts[1] :], jnp.concatenate(far_next[1:], axis=0), counts[2:])
-            rest = all_columns(plan, rest, False)
-            later = (rest[: 2 * width], rest[2 * width :])
-            full.append((w_attn[: 2 * qkv_rows], w_attn[2 * qkv_rows :], later))
         middle = stream + branch
         scale_mlp = norm_scale(middle)
         normed_mlp = (middle * scale_mlp * gain_full[2 + level : 3 + level]).astype(BF)
@@ -552,6 +539,16 @@
         gate_up = dot(normed_mlp_all, w_gu, 1, 1)
         gate, upward = gate_up[:, :width], gate_up[:, width:]
         hidden = (gate * jax.nn.sigmoid(gate) * upward).astype(BF)
+        if ahead:
+            hidden, got = together(hidden, next_far())
+            far_next.append(got)
+            own = own_later[level]
+            w_attn = with_far(own[: cuts[1]], far_next[0], counts[:2])
+            w_attn = all_columns(plan, w_attn, False)
+            rest = with_far(own[cuts[1] :], jnp.concatenate(far_next[1:], axis=0), counts[2:])
+            rest = all_columns(plan, rest, False)
+            later = (rest[: 2 * width], rest[2 * width :])
+            full.append((w_attn[: 2 * qkv_rows], w_attn[2 * qkv_rows :], later))
         if level < LAYERS - 1:
             result = middle + sum_rows(plan, dot(hidden, w_d, 1, 0))
         kept.append(
@@ -647,7 +644,7 @@
             later_mlp, branch = together(later_mlp, branch)
             mine_mlp, far = far_halves(later_mlp, counts[2:])
             mine_attn, far_attn = far_halves(sum_attn, counts[:2])
-            far_a = plan.far(far[: 2 * mlp_rows])
+            far_a = plan.far(far[:mlp_rows])
         if level == LAYERS - 1:
             partial, branch = together(dot(hidden, w_d, 1, 0), branch)
             last = sum_rows(plan, partial)
@@ -655,10 +652,9 @@
         grad_attended = dot(w_o, branch, 1, 1).astype(BF)
         grad_attended = to_heads(plan, grad_attended.reshape(4, HEAD, tok_rows))
         if level == 0:
-            far_b, far_a = together(far[2 * mlp_rows :], far_a)
+            far_b, far_a = together(far[mlp_rows : 2 * mlp_rows], far_a)
             far_b = plan.far(far_b)
-            grad_attended, far_a, grad_wo = together(grad_attended, far_a, grad_wo)
-            sum_wo = columns_sum(plan, grad_wo, True)
+            grad_attended, far_a = together(grad_attended, far_a)
         elif level == LAYERS - 1:
             grad_attended, last = together(grad_attended, last)
             last = from_block_order(plan, (middle + last).astype(BF))
@@ -667,9 +663,10 @@
             where_all, first_query, heads, grad_attended, out, log_total
         )
         if level == 0:
-            far_attn, far_b = together(far_attn, far_b)
-            far_c = plan.far(far_attn)
-            grad_q, far_b, sum_wo = together(grad_q, far_b, sum_wo)
+            far_c = jnp.concatenate([far_attn, far[2 * mlp_rows :]], axis=0)
+            far_c, far_b = together(far_c, far_b)
+            far_c = plan.far(far_c)
+            grad_q, far_b = together(grad_q, far_b)
         elif level == LAYERS - 1:
             grad_q, other = together(grad_q, other)
             last = to_pack(last, other)
@@ -697,7 +694,7 @@
         grad_qkv = jnp.swapaxes(grad_qkv, 1, 2).reshape(-1, tok_rows)
         if level == 0:
             mine_first, far = far_halves(sum_mlp, counts[2:])
-            far_d, far_c = together(far[: 2 * mlp_rows], far_c)
+            far_d, far_c = together(far[:mlp_rows], far_c)
             far_d = plan.far(far_d)
             grad_qkv, far_c = together(grad_qkv, far_c)
         elif level == LAYERS - 1:
@@ -706,26 +703,26 @@
         grad_wqkv = dot(grad_qkv, normed_all, 1, 0).astype(BF)
         grad_normed = sum_rows(plan, dot(grad_qkv, w_qkv, 0, 0))
         if level == 0:
-            far_e = far[2 * mlp_rows :]
-            grad_normed, far_d, far_e, grad_wqkv = together(
-                grad_normed, far_d, far_e, grad_wqkv
-            )
-            far_e = plan.far(far_e)
-            sum_qkv = columns_sum(plan, grad_wqkv, True)
-            got = jnp.concatenate([far_c, far_a, far_b], axis=0).astype(F32)
+            far_e = far[mlp_rows:]
+            grad_normed, far_d, far_e = together(grad_normed, far_d, far_e)
+            cut = qkv_rows + out_rows
+            got = jnp.concatenate([far_c[:cut], far_a, far_b, far_c[cut:]], axis=0).astype(F32)
             mine = jnp.concatenate([mine_attn, mine_mlp], axis=0)
             grads[1] = weight_grads(*core_halves(plan, mine + got, counts))
         else:
             grad_normed, later_mlp = together(grad_normed, sum_mlp)
-            grad_attn = jnp.concatenate([grad_wqkv, grad_wo], axis=0)
-            sum_attn = columns_sum(plan, grad_attn, False)
+        grad_attn = jnp.concatenate([grad_wqkv, grad_wo], axis=0)
+        sum_attn = columns_sum(plan, grad_attn, False)
         gain_rows[level], through = norm_back(
             stream, scale_attn, gain_full[level : level + 1], grad_normed
         )
         grad_stream = grad_middle + through
 
     rows = from_block_order(plan, grad_stream.astype(BF))
-    other, sum_qkv = together(plan.far(rows), sum_qkv)
+    gain_sum = jnp.concatenate(gain_rows + [jnp.zeros((12, model), F32)], axis=0)
+    gain_near = plan.near(gain_sum)
+    other, gain_near, far_e = together(plan.far(rows), gain_near, far_e)
+    far_e = plan.far(far_e)
     group_rows = tok_rows // plan.ctx
     owner_grid = owner_order[0].reshape(plan.ctx, plan.ctx, group_rows)
     local_rows = (
@@ -737,10 +734,8 @@
 
     got = jnp.concatenate([far_d, far_e], axis=0).astype(F32)
     rest = core_halves(plan, mine_first + got, counts[2:])
-    gain_sum = jnp.concatenate(gain_rows + [jnp.zeros((12, model), F32)], axis=0)
-    gain_sum = gain_sum + plan.near(gain_sum)
-    gain_sum = columns_sum(plan, gain_sum, True)
-    mine, far = far_halves(jnp.concatenate([sum_qkv, sum_wo], axis=0), counts[:2])
+    gain_sum = columns_sum(plan, gain_sum + gain_near, True)
+    mine, far = far_halves(sum_attn, counts[:2])
     far = jnp.concatenate([far, gain_sum.astype(BF)], axis=0)
     far = plan.far(far)
     grad_tokens, far = together(grad_tokens, far)

time: 586 us -> 570 us (0.973)
  other arithmetic: 67.9 us -> 59.5 us
    ppermute x39 -> x33, waiting for transfers between devices: 79.7 us -> 65 us  [side(): return lax.ppermute(value, 'ctx', [(i, i ^ k) for i in range(self.ctx)])]
    ppermute x14, waiting for transfers between devices: 55.8 us -> 44.5 us  [far(): return lax.ppermute(value, 'tp', [(i, i ^ 2) for i in range(self.tp)])]
    reduce_scatter x3 -> x4, waiting for transfers between devices: 0.06 us -> 9.78 us  [columns_sum(): return lax.psum_scatter(grad, 'ctx', scatter_dimension=1, tiled=True)]
    ppermute x39 -> x33, starting transfers between devices: 46.3 us -> 39.7 us  [side(): return lax.ppermute(value, 'ctx', [(i, i ^ k) for i in range(self.ctx)])]
    all_to_all x1, waiting for transfers between devices: 3.2 us -> 9.44 us  [local(): lax.all_to_all(slots, 'ctx', split_axis=0, concat_axis=0, tiled=True)]
    ppermute x19, waiting for transfers between devices: 107 us -> 113 us  [near(): return lax.ppermute(value, 'tp', [(i, i ^ 1) for i in range(self.tp)])]
    unnamed x271 -> x261, local copies, waits for them, and re-layouts: 24.3 us -> 28 us
  transfers between devices with their start and end apart: 107 -> 102, of which waited for: 57 -> 60; matrix products, arithmetic and copies ran while one was open for 26% -> 23% of each run, Pallas kernels for 5% -> 6%
where the time goes in v1:
time: 570 us; the launch traced here: 560 us
  waiting for transfers between devices  258 us (45%)
  starting transfers between devices  91.9 us (16%)
  local copies, waits for them, and re-layouts  61.2 us (11%)
  other arithmetic  59.5 us (10%)
  matrix products  41.4 us (7%)
  Pallas kernels  31 us (5%)
  between operations  17.5 us (3%)
    ppermute x19, waiting for transfers between devices, near(): return lax.ppermute(value, 'tp', [(i, i ^ 1) for i in range(self.tp)])  113 us
    ppermute x33, waiting for transfers between devices, side(): return lax.ppermute(value, 'ctx', [(i, i ^ k) for i in range(self.ctx)])  65 us
    ppermute x14, waiting for transfers between devices, far(): return lax.ppermute(value, 'tp', [(i, i ^ 2) for i in range(self.tp)])  44.5 us
    dot_general x24, matrix products, dot(): lax.dot_general(left, right, (((left_dim,), (right_dim,)), ((), ())), pre...  41.4 us
    ppermute x33, starting transfers between devices, side(): return lax.ppermute(value, 'ctx', [(i, i ^ k) for i in range(self.ctx)])  39.7 us
    unnamed x261, local copies, waits for them, and re-layouts  28 us
    ppermute x14, starting transfers between devices, far(): return lax.ppermute(value, 'tp', [(i, i ^ 2) for i in range(self.tp)])  26.9 us
    pallas_call x2, Pallas kernels, attend_back(): pl.pallas_call(functools.partial(back_kernel, count), out_shape=(jax.Shap...  17.5 us
  transfers between devices with their start and end apart: 102, of which 60 were waited for; matrix products, arithmetic and copies ran while one was open for 23% of the time, Pallas kernels for 6%

profile of v1, /device:TPU:0, one launch (start us, length us, event | category | flops | bytes accessed | tf_op | source)
XLA Modules:
  0.0 560.4 jit_solution(13372940089174591535)
XLA Ops:
  21.8 3.7 collective-permute-start.4
  31.6 3.8 collective-permute-done.4
  40.0 6.4 %collective-permute-done.10 = bf16[128,1024]{1,0:T(8,128)(2,1)S(1)} collective-permute-done((bf16[128,1024]{1,0:T(8,128)(2,1)S(1)}, bf16[128,1024]{1,0:T(8,128)(2,1)S(1)}, u32[]{:S(2)}, u32[]{:S(2)}) %collective-permute-start.10) | collective-permute-done | bytes 262176 | tf_op jit(solution)/shard_map/ppermute | solution.py:53
  49.1 7.2 %collective-permute-done.8 = bf16[784,256]{1,0:T(8,128)(2,1)S(1)} collective-permute-done((bf16[784,256]{1,0:T(8,128)(2,1)S(1)}, bf16[784,256]{1,0:T(8,128)(2,1)S(1)}, u32[]{:S(2)}, u32[]{:S(2)}) %collective-permute-start.8) | collective-permute-done | bytes 401440 | tf_op jit(solution)/shard_map/ppermute | solution.py:59
  64.9 9.5 %collective-permute-done.18 = bf16[1184,256]{1,0:T(8,128)(2,1)S(1)} collective-permute-done((bf16[1184,256]{1,0:T(8,128)(2,1)S(1)}, bf16[1184,256]{1,0:T(8,128)(2,1)S(1)}, u32[]{:S(2)}, u32[]{:S(2)}) %collective-permute-start.18) | collective-permute-done | bytes 606240 | tf_op jit(solution)/shard_map/ppermute | solution.py:56
  87.1 6.7 %attend.2 = (f32[4,64,512]{2,1,0:T(8,128)}, bf16[4,64,512]{2,1,0:T(8,128)(2,1)}, f32[4,1,512]{2,1,0:T(1,128)}) custom-call(s32[6]{0:T(128)} %pad_add_fusion.2.place_ref, s32[4,1,512]{2,1,0:T(1,128)} %broadcast_in_dim.84.first_ref, bf16[3,64,512]{2,1,0:T(8,128)(2,1)} %get-tuple-element.100.refs_0_, bf16[3,64,512]{2,1,0:T(8,128)(2,1)} %copy-done.42, ...), custom_call_target="tpu_custom_call" | custom-call | tf_op jit(solution)/shard_map/attend/pallas_call | solution.py:291
  93.8 6.1 %collective-permute-done.19 = bf16[512,256]{1,0:T(8,128)(2,1)S(1)} collective-permute-done((bf16[512,256]{1,0:T(8,128)(2,1)S(1)}, bf16[512,256]{1,0:T(8,128)(2,1)S(1)}, u32[]{:S(2)}, u32[]{:S(2)}) %collective-permute-start.19) | collective-permute-done | bytes 262176 | tf_op jit(solution)/shard_map/ppermute | solution.py:56
  108.2 8.3 %collective-permute-done.21 = bf16[64,512]{1,0:T(8,128)(2,1)S(1)} collective-permute-done((bf16[64,512]{1,0:T(8,128)(2,1)S(1)}, bf16[64,512]{1,0:T(8,128)(2,1)S(1)}, u32[]{:S(2)}, u32[]{:S(2)}) %collective-permute-start.21) | collective-permute-done | bytes 65568 | tf_op jit(solution)/shard_map/ppermute | solution.py:59
  118.6 4.3 collective-permute-done.23
  128.1 10.0 %collective-permute-done.28 = bf16[128,1024]{1,0:T(8,128)(2,1)S(1)} collective-permute-done((bf16[128,1024]{1,0:T(8,128)(2,1)S(1)}, bf16[128,1024]{1,0:T(8,128)(2,1)S(1)}, u32[]{:S(2)}, u32[]{:S(2)}) %collective-permute-start.28) | collective-permute-done | bytes 262176 | tf_op jit(solution)/shard_map/ppermute | solution.py:53
  140.2 6.3 %collective-permute-done.30 = bf16[128,1024]{1,0:T(8,128)(2,1)S(1)} collective-permute-done((bf16[128,1024]{1,0:T(8,128)(2,1)S(1)}, bf16[128,1024]{1,0:T(8,128)(2,1)S(1)}, u32[]{:S(2)}, u32[]{:S(2)}) %collective-permute-start.30) | collective-permute-done | bytes 262176 | tf_op jit(solution)/shard_map/ppermute | solution.py:53
  150.4 3.8 fusion.6
  155.8 5.2 collective-permute-done.32
  168.3 5.9 %collective-permute-done.34 = bf16[128,1024]{1,0:T(8,128)(2,1)} collective-permute-done((bf16[128,1024]{1,0:T(8,128)(2,1)S(1)}, bf16[128,1024]{1,0:T(8,128)(2,1)}, u32[]{:S(2)}, u32[]{:S(2)}) %collective-permute-start.34) | collective-permute-done | bytes 262176 | tf_op jit(solution)/shard_map/ppermute | solution.py:53
  176.0 7.2 %collective-permute-done.35 = bf16[128,1024]{1,0:T(8,128)(2,1)S(1)} collective-permute-done((bf16[128,1024]{1,0:T(8,128)(2,1)S(1)}, bf16[128,1024]{1,0:T(8,128)(2,1)S(1)}, u32[]{:S(2)}, u32[]{:S(2)}) %collective-permute-start.35) | collective-permute-done | bytes 262176 | tf_op jit(solution)/shard_map/ppermute | solution.py:53
  191.2 2.9 collective-permute-start.38
  194.5 7.9 %collective-permute-done.37.refs_1_ = bf16[3,64,512]{2,1,0:T(8,128)(2,1)S(1)} collective-permute-done((bf16[3,64,512]{2,1,0:T(8,128)(2,1)S(1)}, bf16[3,64,512]{2,1,0:T(8,128)(2,1)S(1)}, u32[]{:S(2)}, u32[]{:S(2)}) %collective-permute-start.37) | collective-permute-done | bytes 196640 | tf_op jit(solution)/shard_map/ppermute | solution.py:59
  205.1 4.9 collective-permute-done.39.refs_3_
  210.7 6.8 %attend.3 = (f32[4,64,512]{2,1,0:T(8,128)}, bf16[4,64,512]{2,1,0:T(8,128)(2,1)}, f32[4,1,512]{2,1,0:T(1,128)}) custom-call(s32[6]{0:T(128)} %pad_add_fusion.2.place_ref, s32[4,1,512]{2,1,0:T(1,128)} %broadcast_in_dim.84.first_ref, bf16[3,64,512]{2,1,0:T(8,128)(2,1)} %get-tuple-element.326.refs_0_, bf16[3,64,512]{2,1,0:T(8,128)(2,1)} %copy-done.45, ...), custom_call_target="tpu_custom_call" | custom-call | tf_op jit(solution)/shard_map/attend/pallas_call | solution.py:291
  232.8 6.9 %collective-permute-done.44 = bf16[128,1024]{1,0:T(8,128)(2,1)S(1)} collective-permute-done((bf16[128,1024]{1,0:T(8,128)(2,1)S(1)}, bf16[128,1024]{1,0:T(8,128)(2,1)S(1)}, u32[]{:S(2)}, u32[]{:S(2)}) %collective-permute-start.44) | collective-permute-done | bytes 262176 | tf_op jit(solution)/shard_map/ppermute | solution.py:53
  241.6 6.2 %collective-permute-done.45 = bf16[128,1024]{1,0:T(8,128)(2,1)S(1)} collective-permute-done((bf16[128,1024]{1,0:T(8,128)(2,1)S(1)}, bf16[128,1024]{1,0:T(8,128)(2,1)S(1)}, u32[]{:S(2)}, u32[]{:S(2)}) %collective-permute-start.45) | collective-permute-done | bytes 262176 | tf_op jit(solution)/shard_map/ppermute | solution.py:53
  249.9 4.1 fusion.2
  266.6 5.0 collective-permute-done.48
  275.3 6.3 %collective-permute-done.49 = bf16[128,1024]{1,0:T(8,128)(2,1)S(1)} collective-permute-done((bf16[128,1024]{1,0:T(8,128)(2,1)S(1)}, bf16[128,1024]{1,0:T(8,128)(2,1)S(1)}, u32[]{:S(2)}, u32[]{:S(2)}) %collective-permute-start.49) | collective-permute-done | bytes 262176 | tf_op jit(solution)/shard_map/ppermute | solution.py:53
  299.1 3.3 collective-permute-done.53.refs_7_
  308.1 3.6 collective-permute-start.56
  311.7 8.6 %attend_back.2 = (f32[4,64,512]{2,1,0:T(8,128)}, f32[4,64,512]{2,1,0:T(8,128)}, f32[4,64,512]{2,1,0:T(8,128)}) custom-call(s32[6]{0:T(128)} %pad_add_fusion.2.place_ref, s32[4,1,512]{2,1,0:T(1,128)} %broadcast_in_dim.84.first_ref, f32[4,64,512]{2,1,0:T(8,128)} %get-tuple-element.117.out_ref, f32[4,1,512]{2,1,0:T(1,128)} %get-tuple-element.118.lse_ref, ...), custom_call_target="tpu_custom_call" | custom-call | tf_op jit(solution)/shard_map/attend_back/pallas_call | solution.py:350
  328.7 6.6 %collective-permute-done.57 = bf16[3,64,512]{2,1,0:T(8,128)(2,1)S(1)} collective-permute-done((bf16[3,64,512]{2,1,0:T(8,128)(2,1)S(1)}, bf16[3,64,512]{2,1,0:T(8,128)(2,1)S(1)}, u32[]{:S(2)}, u32[]{:S(2)}) %collective-permute-start.57) | collective-permute-done | bytes 196640 | tf_op jit(solution)/shard_map/ppermute | solution.py:59
  335.4 6.1 %collective-permute-done.58 = bf16[3,64,512]{2,1,0:T(8,128)(2,1)S(1)} collective-permute-done((bf16[3,64,512]{2,1,0:T(8,128)(2,1)S(1)}, bf16[3,64,512]{2,1,0:T(8,128)(2,1)S(1)}, u32[]{:S(2)}, u32[]{:S(2)}) %collective-permute-start.58) | collective-permute-done | bytes 196640 | tf_op jit(solution)/shard_map/ppermute | solution.py:59
  350.0 5.4 collective-permute-done.63
  359.1 7.2 %collective-permute-done.64 = bf16[128,1024]{1,0:T(8,128)(2,1)S(1)} collective-permute-done((bf16[128,1024]{1,0:T(8,128)(2,1)S(1)}, bf16[128,1024]{1,0:T(8,128)(2,1)S(1)}, u32[]{:S(2)}, u32[]{:S(2)}) %collective-permute-start.64) | collective-permute-done | bytes 262176 | tf_op jit(solution)/shard_map/ppermute | solution.py:53
  380.5 5.8 %collective-permute-done.67 = bf16[128,1024]{1,0:T(8,128)(2,1)S(1)} collective-permute-done((bf16[128,1024]{1,0:T(8,128)(2,1)S(1)}, bf16[128,1024]{1,0:T(8,128)(2,1)S(1)}, u32[]{:S(2)}, u32[]{:S(2)}) %collective-permute-start.67) | collective-permute-done | bytes 262176 | tf_op jit(solution)/shard_map/ppermute | solution.py:53
  391.7 6.3 %collective-permute-done.68 = bf16[128,1024]{1,0:T(8,128)(2,1)S(1)} collective-permute-done((bf16[128,1024]{1,0:T(8,128)(2,1)S(1)}, bf16[128,1024]{1,0:T(8,128)(2,1)S(1)}, u32[]{:S(2)}, u32[]{:S(2)}) %collective-permute-start.68) | collective-permute-done | bytes 262176 | tf_op jit(solution)/shard_map/ppermute | solution.py:53
  408.9 3.3 collective-permute-done.73
  415.2 8.8 %attend_back.3 = (f32[4,64,512]{2,1,0:T(8,128)}, f32[4,64,512]{2,1,0:T(8,128)}, f32[4,64,512]{2,1,0:T(8,128)}) custom-call(s32[6]{0:T(128)} %pad_add_fusion.2.place_ref, s32[4,1,512]{2,1,0:T(1,128)} %broadcast_in_dim.84.first_ref, f32[4,64,512]{2,1,0:T(8,128)} %get-tuple-element.146.out_ref, f32[4,1,512]{2,1,0:T(1,128)} %get-tuple-element.147.lse_ref, ...), custom_call_target="tpu_custom_call" | custom-call | tf_op jit(solution)/shard_map/attend_back/pallas_call | solution.py:350
  430.2 4.0 collective-permute-start.78
  434.8 3.4 collective-permute-done.76
  438.3 2.9 collective-permute-done.77
  442.1 8.6 %reduce-scatter.9.cloned.1.call-done = bf16[2112,256]{1,0:T(8,128)(2,1)} async-done(((bf16[2112,1024]{1,0:T(8,128)(2,1)}), bf16[2112,256]{1,0:T(8,128)(2,1)}) %reduce-scatter.9.cloned.1.call-update) | async-done | bytes 1081360 | tf_op jit(solution)/shard_map/reduce_scatter | solution.py:165
  457.7 3.7 collective-permute-start.81
  472.2 6.3 %collective-permute-done.80 = bf16[128,1024]{1,0:T(8,128)(2,1)S(1)} collective-permute-done((bf16[128,1024]{1,0:T(8,128)(2,1)S(1)}, bf16[128,1024]{1,0:T(8,128)(2,1)S(1)}, u32[]{:S(2)}, u32[]{:S(2)}) %collective-permute-start.80) | collective-permute-done | bytes 262176 | tf_op jit(solution)/shard_map/ppermute | solution.py:53
  482.2 4.4 collective-permute-done.83
  486.6 7.0 %collective-permute-done.82 = bf16[128,1024]{1,0:T(8,128)(2,1)S(1)} collective-permute-done((bf16[128,1024]{1,0:T(8,128)(2,1)S(1)}, bf16[128,1024]{1,0:T(8,128)(2,1)S(1)}, u32[]{:S(2)}, u32[]{:S(2)}) %collective-permute-start.82) | collective-permute-done | bytes 262176 | tf_op jit(solution)/shard_map/ppermute | solution.py:56
  501.8 15.2 %collective-permute-done.85 = bf16[256,1024]{1,0:T(8,128)(2,1)S(1)} collective-permute-done((bf16[256,1024]{1,0:T(8,128)(2,1)S(1)}, bf16[256,1024]{1,0:T(8,128)(2,1)S(1)}, u32[]{:S(2)}, u32[]{:S(2)}) %collective-permute-start.85) | collective-permute-done | bytes 524320 | tf_op jit(solution)/shard_map/ppermute | solution.py:53
  517.2 3.0 gather_fusion
  523.0 3.5 all-to-all-start
  531.6 9.4 %all-to-all-done = bf16[4,128,1024]{2,1,0:T(8,128)(2,1)S(1)} async-done(((bf16[4,128,1024]{2,1,0:T(8,128)(2,1)}), bf16[4,128,1024]{2,1,0:T(8,128)(2,1)S(1)}, u32[]{:S(2)}, u32[]{:S(2)}) %all-to-all-start) | async-done | bytes 1048608 | tf_op jit(solution)/shard_map/all_to_all | solution.py:733
  541.1 4.2 collective-permute-done.90
  (731 shorter events, 256.5 us)
Async XLA Ops:
  7.2 143.2 %all-gather.6.cloned.1.call-start = ((), (), s32[]{:S(2)}) async-start(), calls=%async_computation.6 | async-start | bytes 5406720 | tf_op jit(solution)/shard_map/all_gather | solution.py:139
  7.2 12.5 %collective-permute-start = (s32[1,2048]{1,0:T(1,128)}, s32[1,2048]{1,0:T(1,128)S(1)}, u32[]{:S(2)}, u32[]{:S(2)}) collective-permute-start(s32[1,2048]{1,0:T(1,128)} %param.15), channel_id=1, source_target_pairs={{0,16},{16,0},{1,17},{17,1},{2,18},{18,2},{3,19},{19,3},{4,20},{20... | collective-permute-start | bytes 24584 | tf_op jit(solution)/shard_map/ppermute | solution.py:50
  8.5 10.7 %collective-permute-start.6 = (bf16[16,128]{1,0:T(8,128)(2,1)S(1)}, bf16[16,128]{1,0:T(8,128)(2,1)S(1)}, u32[]{:S(2)}, u32[]{:S(2)}) collective-permute-start(bf16[16,128]{1,0:T(8,128)(2,1)S(1)} %pad_maximum_fusion.60), channel_id=1, source_target_pairs={{0,16},{16,0},{1,17},{17,1},{2,18},{18,2},{3,19},{19,3},{4,20},{20... | collective-permute-start | bytes 12296 | tf_op jit(solution)/shard_map/ppermute | solution.py:50
  13.0 16.6 %collective-permute-start.3 = (bf16[1184,128]{1,0:T(8,128)(2,1)S(1)}, bf16[1184,128]{1,0:T(8,128)(2,1)S(1)}, u32[]{:S(2)}, u32[]{:S(2)}) collective-permute-start(bf16[1184,128]{1,0:T(8,128)(2,1)S(1)} %get-tuple-element.342), channel_id=1, source_target_pairs={{0,16},{16,0},{1,17},{17,1},{2,18},{18,2},{3,19},{19,3},{4,20},{20... | collective-permute-start | bytes 909320 | tf_op jit(solution)/shard_map/ppermute | solution.py:50
  21.8 13.5 %collective-permute-start.4 = (bf16[384,256]{1,0:T(8,128)(2,1)S(1)}, bf16[384,256]{1,0:T(8,128)(2,1)S(1)}, u32[]{:S(2)}, u32[]{:S(2)}) collective-permute-start(bf16[384,256]{1,0:T(8,128)(2,1)S(1)} %maximum_select_fusion.2), channel_id=1, source_target_pairs={{0,2},{1,3},{2,0},{3,1},{4,6},{5,7},{6,4},{7,5},{8,10},{9,11},{10,... | collective-permute-start | bytes 589832 | tf_op jit(solution)/shard_map/ppermute | solution.py:56
  27.9 11.9 %collective-permute-start.13 = (bf16[128,1024]{1,0:T(8,128)(2,1)S(1)}, bf16[128,1024]{1,0:T(8,128)(2,1)S(1)}, u32[]{:S(2)}, u32[]{:S(2)}) collective-permute-start(bf16[128,1024]{1,0:T(8,128)(2,1)S(1)} %constant_dynamic-update-slice_fusion.15), channel_id=1, source_target_pairs={{0,1},{1,0},{2,3},{3,2},{4,5},{5,4},{6,7},{7,6},{8,9},{9,8},{10,11... | collective-permute-start | bytes 786440 | tf_op jit(solution)/shard_map/ppermute | solution.py:53
  35.7 13.3 %collective-permute-start.7 = (bf16[784,256]{1,0:T(8,128)(2,1)S(1)}, bf16[784,256]{1,0:T(8,128)(2,1)S(1)}, u32[]{:S(2)}, u32[]{:S(2)}) collective-permute-start(bf16[784,256]{1,0:T(8,128)(2,1)S(1)} %get-tuple-element.369), channel_id=1, source_target_pairs={{0,4},{4,0},{8,12},{12,8},{1,5},{5,1},{9,13},{13,9},{2,6},{6,2},{1... | collective-permute-start | bytes 1204232 | tf_op jit(solution)/shard_map/ppermute | solution.py:59
  37.3 19.1 %collective-permute-start.8 = (bf16[784,256]{1,0:T(8,128)(2,1)S(1)}, bf16[784,256]{1,0:T(8,128)(2,1)S(1)}, u32[]{:S(2)}, u32[]{:S(2)}) collective-permute-start(bf16[784,256]{1,0:T(8,128)(2,1)S(1)} %get-tuple-element.369), channel_id=1, source_target_pairs={{0,8},{4,12},{8,0},{12,4},{1,9},{5,13},{9,1},{13,5},{2,10},{6,14},... | collective-permute-start | bytes 1204232 | tf_op jit(solution)/shard_map/ppermute | solution.py:59
  38.8 17.6 %collective-permute-start.9 = (bf16[784,256]{1,0:T(8,128)(2,1)S(1)}, bf16[784,256]{1,0:T(8,128)(2,1)S(1)}, u32[]{:S(2)}, u32[]{:S(2)}) collective-permute-start(bf16[784,256]{1,0:T(8,128)(2,1)S(1)} %get-tuple-element.369), channel_id=1, source_target_pairs={{0,12},{4,8},{8,4},{12,0},{1,13},{5,9},{9,5},{13,1},{2,14},{6,10},... | collective-permute-start | bytes 1204232 | tf_op jit(solution)/shard_map/ppermute | solution.py:59
  39.9 16.5 %collective-permute-start.14 = (bf16[256,1024]{1,0:T(8,128)(2,1)S(1)}, bf16[256,1024]{1,0:T(8,128)(2,1)S(1)}, u32[]{:S(2)}, u32[]{:S(2)}) collective-permute-start(bf16[256,1024]{1,0:T(8,128)(2,1)S(1)} %pad_maximum_fusion.24), channel_id=1, source_target_pairs={{0,16},{16,0},{1,17},{17,1},{2,18},{18,2},{3,19},{19,3},{4,20},{20... | collective-permute-start | bytes 1572872 | tf_op jit(solution)/shard_map/ppermute | solution.py:50
  46.4 28.0 %collective-permute-start.18 = (bf16[1184,256]{1,0:T(8,128)(2,1)S(1)}, bf16[1184,256]{1,0:T(8,128)(2,1)S(1)}, u32[]{:S(2)}, u32[]{:S(2)}) collective-permute-start(bf16[1184,256]{1,0:T(8,128)(2,1)S(1)} %maximum_select_fusion.1), channel_id=1, source_target_pairs={{0,2},{1,3},{2,0},{3,1},{4,6},{5,7},{6,4},{7,5},{8,10},{9,11},{10,... | collective-permute-start | bytes 1818632 | tf_op jit(solution)/shard_map/ppermute | solution.py:56
  61.4 13.0 %collective-permute-start.15 = (bf16[3,64,512]{2,1,0:T(8,128)(2,1)S(1)}, bf16[3,64,512]{2,1,0:T(8,128)(2,1)S(1)}, u32[]{:S(2)}, u32[]{:S(2)}) collective-permute-start(bf16[3,64,512]{2,1,0:T(8,128)(2,1)S(1)} %get-tuple-element.329), channel_id=1, source_target_pairs={{0,4},{4,0},{8,12},{12,8},{1,5},{5,1},{9,13},{13,9},{2,6},{6,2},{1... | collective-permute-start | bytes 589832 | tf_op jit(solution)/shard_map/ppermute | solution.py:59
  62.5 11.9 %collective-permute-start.16 = (bf16[3,64,512]{2,1,0:T(8,128)(2,1)S(1)}, bf16[3,64,512]{2,1,0:T(8,128)(2,1)S(1)}, u32[]{:S(2)}, u32[]{:S(2)}) collective-permute-start(bf16[3,64,512]{2,1,0:T(8,128)(2,1)S(1)} %get-tuple-element.328), channel_id=1, source_target_pairs={{0,8},{4,12},{8,0},{12,4},{1,9},{5,13},{9,1},{13,5},{2,10},{6,14},... | collective-permute-start | bytes 589832 | tf_op jit(solution)/shard_map/ppermute | solution.py:59
  63.4 11.0 %collective-permute-start.17 = (bf16[3,64,512]{2,1,0:T(8,128)(2,1)S(1)}, bf16[3,64,512]{2,1,0:T(8,128)(2,1)S(1)}, u32[]{:S(2)}, u32[]{:S(2)}) collective-permute-start(bf16[3,64,512]{2,1,0:T(8,128)(2,1)S(1)} %get-tuple-element.327), channel_id=1, source_target_pairs={{0,12},{4,8},{8,4},{12,0},{1,13},{5,9},{9,5},{13,1},{2,14},{6,10},... | collective-permute-start | bytes 589832 | tf_op jit(solution)/shard_map/ppermute | solution.py:59
  76.4 106.9 %all-gather.4.cloned.1.call-start = ((), (), s32[]{:S(2)}) async-start(), calls=%async_computation.5 | async-start | bytes 2621440 | tf_op jit(solution)/shard_map/all_gather | solution.py:139
  85.0 14.9 %collective-permute-start.19 = (bf16[512,256]{1,0:T(8,128)(2,1)S(1)}, bf16[512,256]{1,0:T(8,128)(2,1)S(1)}, u32[]{:S(2)}, u32[]{:S(2)}) collective-permute-start(bf16[512,256]{1,0:T(8,128)(2,1)S(1)} %slice.1201), channel_id=1, source_target_pairs={{0,2},{1,3},{2,0},{3,1},{4,6},{5,7},{6,4},{7,5},{8,10},{9,11},{10,... | collective-permute-start | bytes 786440 | tf_op jit(solution)/shard_map/ppermute | solution.py:56
  102.6 15.8 %collective-permute-start.24 = (bf16[256,256]{1,0:T(8,128)(2,1)S(1)}, bf16[256,256]{1,0:T(8,128)(2,1)S(1)}, u32[]{:S(2)}, u32[]{:S(2)}) collective-permute-start(bf16[256,256]{1,0:T(8,128)(2,1)S(1)} %get-tuple-element.405), channel_id=1, source_target_pairs={{0,4},{4,0},{8,12},{12,8},{1,5},{5,1},{9,13},{13,9},{2,6},{6,2},{1... | collective-permute-start | bytes 393224 | tf_op jit(solution)/shard_map/ppermute | solution.py:59
  103.2 15.2 %collective-permute-start.25 = (bf16[256,256]{1,0:T(8,128)(2,1)S(1)}, bf16[256,256]{1,0:T(8,128)(2,1)S(1)}, u32[]{:S(2)}, u32[]{:S(2)}) collective-permute-start(bf16[256,256]{1,0:T(8,128)(2,1)S(1)} %get-tuple-element.405), channel_id=1, source_target_pairs={{0,8},{4,12},{8,0},{12,4},{1,9},{5,13},{9,1},{13,5},{2,10},{6,14},... | collective-permute-start | bytes 393224 | tf_op jit(solution)/shard_map/ppermute | solution.py:59
  104.8 13.8 %collective-permute-start.26 = (bf16[256,256]{1,0:T(8,128)(2,1)S(1)}, bf16[256,256]{1,0:T(8,128)(2,1)S(1)}, u32[]{:S(2)}, u32[]{:S(2)}) collective-permute-start(bf16[256,256]{1,0:T(8,128)(2,1)S(1)} %get-tuple-element.405), channel_id=1, source_target_pairs={{0,12},{4,8},{8,4},{12,0},{1,13},{5,9},{9,5},{13,1},{2,14},{6,10},... | collective-permute-start | bytes 393224 | tf_op jit(solution)/shard_map/ppermute | solution.py:59
  125.8 12.3 %collective-permute-start.28 = (bf16[128,1024]{1,0:T(8,128)(2,1)S(1)}, bf16[128,1024]{1,0:T(8,128)(2,1)S(1)}, u32[]{:S(2)}, u32[]{:S(2)}) collective-permute-start(bf16[128,1024]{1,0:T(8,128)(2,1)S(1)} %slice.1793), channel_id=1, source_target_pairs={{0,1},{1,0},{2,3},{3,2},{4,5},{5,4},{6,7},{7,6},{8,9},{9,8},{10,11... | collective-permute-start | bytes 786440 | tf_op jit(solution)/shard_map/ppermute | solution.py:53
  126.0 12.2 %collective-permute-start.29 = (bf16[352,256]{1,0:T(8,128)(2,1)S(1)}, bf16[352,256]{1,0:T(8,128)(2,1)S(1)}, u32[]{:S(2)}, u32[]{:S(2)}) collective-permute-start(bf16[352,256]{1,0:T(8,128)(2,1)S(1)} %get-tuple-element.112), channel_id=1, source_target_pairs={{0,2},{1,3},{2,0},{3,1},{4,6},{5,7},{6,4},{7,5},{8,10},{9,11},{10,... | collective-permute-start | bytes 540680 | tf_op jit(solution)/shard_map/ppermute | solution.py:56
  140.2 109.7 %all-gather.8.cloned.1.call-start = ((), (), s32[]{:S(2)}) async-start(), calls=%async_computation.7 | async-start | bytes 5406720 | tf_op jit(solution)/shard_map/all_gather | solution.py:139
  149.0 12.0 %collective-permute-start.32 = (bf16[352,256]{1,0:T(8,128)(2,1)}, bf16[352,256]{1,0:T(8,128)(2,1)}, u32[]{:S(2)}, u32[]{:S(2)}) collective-permute-start(bf16[352,256]{1,0:T(8,128)(2,1)} %get-tuple-element.115), channel_id=1, source_target_pairs={{0,2},{1,3},{2,0},{3,1},{4,6},{5,7},{6,4},{7,5},{8,10},{9,11},{10,... | collective-permute-start | bytes 540680 | tf_op jit(solution)/shard_map/ppermute | solution.py:56
  168.2 188.2 %reduce-scatter.5.cloned.1.call-start = ((), (), s32[]{:S(2)}) async-start(), calls=%async_computation.8 | async-start | bytes 5406720 | tf_op jit(solution)/shard_map/reduce_scatter | solution.py:165
  190.4 12.0 %collective-permute-start.37 = (bf16[3,64,512]{2,1,0:T(8,128)(2,1)S(1)}, bf16[3,64,512]{2,1,0:T(8,128)(2,1)S(1)}, u32[]{:S(2)}, u32[]{:S(2)}) collective-permute-start(bf16[3,64,512]{2,1,0:T(8,128)(2,1)S(1)} %get-tuple-element.325), channel_id=1, source_target_pairs={{0,4},{4,0},{8,12},{12,8},{1,5},{5,1},{9,13},{13,9},{2,6},{6,2},{1... | collective-permute-start | bytes 589832 | tf_op jit(solution)/shard_map/ppermute | solution.py:59
  191.2 13.9 %collective-permute-start.38 = (bf16[3,64,512]{2,1,0:T(8,128)(2,1)S(1)}, bf16[3,64,512]{2,1,0:T(8,128)(2,1)S(1)}, u32[]{:S(2)}, u32[]{:S(2)}) collective-permute-start(bf16[3,64,512]{2,1,0:T(8,128)(2,1)S(1)} %get-tuple-element.324), channel_id=1, source_target_pairs={{0,8},{4,12},{8,0},{12,4},{1,9},{5,13},{9,1},{13,5},{2,10},{6,14},... | collective-permute-start | bytes 589832 | tf_op jit(solution)/shard_map/ppermute | solution.py:59
  194.1 15.9 %collective-permute-start.39 = (bf16[3,64,512]{2,1,0:T(8,128)(2,1)S(1)}, bf16[3,64,512]{2,1,0:T(8,128)(2,1)S(1)}, u32[]{:S(2)}, u32[]{:S(2)}) collective-permute-start(bf16[3,64,512]{2,1,0:T(8,128)(2,1)S(1)} %get-tuple-element.323), channel_id=1, source_target_pairs={{0,12},{4,8},{8,4},{12,0},{1,13},{5,9},{9,5},{13,1},{2,14},{6,10},... | collective-permute-start | bytes 589832 | tf_op jit(solution)/shard_map/ppermute | solution.py:59
  282.3 105.3 %reduce-scatter.7.cloned.1.call-start = ((), (), s32[]{:S(2)}) async-start(), calls=%async_computation.9 | async-start | bytes 2621440 | tf_op jit(solution)/shard_map/reduce_scatter | solution.py:165
  308.1 15.4 %collective-permute-start.56 = (bf16[128,1024]{1,0:T(8,128)(2,1)}, bf16[128,1024]{1,0:T(8,128)(2,1)}, u32[]{:S(2)}, u32[]{:S(2)}) collective-permute-start(bf16[128,1024]{1,0:T(8,128)(2,1)} %constant_dynamic-update-slice_fusion.29), channel_id=1, source_target_pairs={{0,2},{1,3},{2,0},{3,1},{4,6},{5,7},{6,4},{7,5},{8,10},{9,11},{10,... | collective-permute-start | bytes 786440 | tf_op jit(solution)/shard_map/ppermute | solution.py:56
  323.6 11.8 %collective-permute-start.57 = (bf16[3,64,512]{2,1,0:T(8,128)(2,1)S(1)}, bf16[3,64,512]{2,1,0:T(8,128)(2,1)S(1)}, u32[]{:S(2)}, u32[]{:S(2)}) collective-permute-start(bf16[3,64,512]{2,1,0:T(8,128)(2,1)S(1)} %pad_maximum_fusion.51), channel_id=1, source_target_pairs={{0,4},{4,0},{8,12},{12,8},{1,5},{5,1},{9,13},{13,9},{2,6},{6,2},{1... | collective-permute-start | bytes 589832 | tf_op jit(solution)/shard_map/ppermute | solution.py:59
  325.4 16.1 %collective-permute-start.58 = (bf16[3,64,512]{2,1,0:T(8,128)(2,1)S(1)}, bf16[3,64,512]{2,1,0:T(8,128)(2,1)S(1)}, u32[]{:S(2)}, u32[]{:S(2)}) collective-permute-start(bf16[3,64,512]{2,1,0:T(8,128)(2,1)S(1)} %pad_maximum_fusion.52), channel_id=1, source_target_pairs={{0,8},{4,12},{8,0},{12,4},{1,9},{5,13},{9,1},{13,5},{2,10},{6,14},... | collective-permute-start | bytes 589832 | tf_op jit(solution)/shard_map/ppermute | solution.py:59
  326.0 15.5 %collective-permute-start.59 = (bf16[3,64,512]{2,1,0:T(8,128)(2,1)S(1)}, bf16[3,64,512]{2,1,0:T(8,128)(2,1)S(1)}, u32[]{:S(2)}, u32[]{:S(2)}) collective-permute-start(bf16[3,64,512]{2,1,0:T(8,128)(2,1)S(1)} %pad_maximum_fusion.53), channel_id=1, source_target_pairs={{0,12},{4,8},{8,4},{12,0},{1,13},{5,9},{9,5},{13,1},{2,14},{6,10},... | collective-permute-start | bytes 589832 | tf_op jit(solution)/shard_map/ppermute | solution.py:59
  328.6 13.8 %collective-permute-start.61 = (bf16[256,1024]{1,0:T(8,128)(2,1)S(1)}, bf16[256,1024]{1,0:T(8,128)(2,1)S(1)}, u32[]{:S(2)}, u32[]{:S(2)}) collective-permute-start(bf16[256,1024]{1,0:T(8,128)(2,1)S(1)} %pad_maximum_fusion.30), channel_id=1, source_target_pairs={{0,1},{1,0},{2,3},{3,2},{4,5},{5,4},{6,7},{7,6},{8,9},{9,8},{10,11... | collective-permute-start | bytes 1572872 | tf_op jit(solution)/shard_map/ppermute | solution.py:53
  349.7 101.0 %reduce-scatter.9.cloned.1.call-start = ((), (), s32[]{:S(2)}) async-start(), calls=%async_computation.10 | async-start | bytes 5406720 | tf_op jit(solution)/shard_map/reduce_scatter | solution.py:165
  387.6 141.0 %reduce-scatter.11.cloned.1.call-start = ((), (), s32[]{:S(2)}) async-start(), calls=%async_computation.11 | async-start | bytes 2621440 | tf_op jit(solution)/shard_map/reduce_scatter | solution.py:165
  400.5 11.8 %collective-permute-start.73 = (bf16[352,256]{1,0:T(8,128)(2,1)S(1)}, bf16[352,256]{1,0:T(8,128)(2,1)S(1)}, u32[]{:S(2)}, u32[]{:S(2)}) collective-permute-start(bf16[352,256]{1,0:T(8,128)(2,1)S(1)} %get-tuple-element.260), channel_id=1, source_target_pairs={{0,2},{1,3},{2,0},{3,1},{4,6},{5,7},{6,4},{7,5},{8,10},{9,11},{10,... | collective-permute-start | bytes 540680 | tf_op jit(solution)/shard_map/ppermute | solution.py:56
  414.5 11.8 %collective-permute-start.74 = (bf16[352,256]{1,0:T(8,128)(2,1)S(1)}, bf16[352,256]{1,0:T(8,128)(2,1)S(1)}, u32[]{:S(2)}, u32[]{:S(2)}) collective-permute-start(bf16[352,256]{1,0:T(8,128)(2,1)S(1)} %get-tuple-element.158), channel_id=1, source_target_pairs={{0,2},{1,3},{2,0},{3,1},{4,6},{5,7},{6,4},{7,5},{8,10},{9,11},{10,... | collective-permute-start | bytes 540680 | tf_op jit(solution)/shard_map/ppermute | solution.py:56
  428.7 12.5 %collective-permute-start.77 = (bf16[3,64,512]{2,1,0:T(8,128)(2,1)S(1)}, bf16[3,64,512]{2,1,0:T(8,128)(2,1)S(1)}, u32[]{:S(2)}, u32[]{:S(2)}) collective-permute-start(bf16[3,64,512]{2,1,0:T(8,128)(2,1)S(1)} %pad_maximum_fusion.56), channel_id=1, source_target_pairs={{0,12},{4,8},{8,4},{12,0},{1,13},{5,9},{9,5},{13,1},{2,14},{6,10},... | collective-permute-start | bytes 589832 | tf_op jit(solution)/shard_map/ppermute | solution.py:59
  430.2 22.7 %collective-permute-start.78 = (bf16[864,256]{1,0:T(8,128)(2,1)}, bf16[864,256]{1,0:T(8,128)(2,1)S(1)}, u32[]{:S(2)}, u32[]{:S(2)}) collective-permute-start(bf16[864,256]{1,0:T(8,128)(2,1)} %pad_maximum_fusion.34), channel_id=1, source_target_pairs={{0,2},{1,3},{2,0},{3,1},{4,6},{5,7},{6,4},{7,5},{8,10},{9,11},{10,... | collective-permute-start | bytes 1327112 | tf_op jit(solution)/shard_map/ppermute | solution.py:56
  457.7 20.9 %collective-permute-start.81 = (bf16[352,256]{1,0:T(8,128)(2,1)}, bf16[352,256]{1,0:T(8,128)(2,1)}, u32[]{:S(2)}, u32[]{:S(2)}) collective-permute-start(bf16[352,256]{1,0:T(8,128)(2,1)} %get-tuple-element.167), channel_id=1, source_target_pairs={{0,2},{1,3},{2,0},{3,1},{4,6},{5,7},{6,4},{7,5},{8,10},{9,11},{10,... | collective-permute-start | bytes 540680 | tf_op jit(solution)/shard_map/ppermute | solution.py:56
  479.2 14.3 %collective-permute-start.82 = (bf16[128,1024]{1,0:T(8,128)(2,1)S(1)}, bf16[128,1024]{1,0:T(8,128)(2,1)S(1)}, u32[]{:S(2)}, u32[]{:S(2)}) collective-permute-start(bf16[128,1024]{1,0:T(8,128)(2,1)S(1)} %constant_dynamic-update-slice_fusion.37), channel_id=1, source_target_pairs={{0,2},{1,3},{2,0},{3,1},{4,6},{5,7},{6,4},{7,5},{8,10},{9,11},{10,... | collective-permute-start | bytes 786440 | tf_op jit(solution)/shard_map/ppermute | solution.py:56
  495.3 21.8 %collective-permute-start.85 = (bf16[256,1024]{1,0:T(8,128)(2,1)S(1)}, bf16[256,1024]{1,0:T(8,128)(2,1)S(1)}, u32[]{:S(2)}, u32[]{:S(2)}) collective-permute-start(bf16[256,1024]{1,0:T(8,128)(2,1)S(1)} %pad_maximum_fusion.33), channel_id=1, source_target_pairs={{0,1},{1,0},{2,3},{3,2},{4,5},{5,4},{6,7},{7,6},{8,9},{9,8},{10,11... | collective-permute-start | bytes 1572872 | tf_op jit(solution)/shard_map/ppermute | solution.py:53
  496.1 24.1 %collective-permute-start.86 = (bf16[704,256]{1,0:T(8,128)(2,1)}, bf16[704,256]{1,0:T(8,128)(2,1)}, u32[]{:S(2)}, u32[]{:S(2)}) collective-permute-start(bf16[704,256]{1,0:T(8,128)(2,1)} %pad_maximum_fusion.44), channel_id=1, source_target_pairs={{0,2},{1,3},{2,0},{3,1},{4,6},{5,7},{6,4},{7,5},{8,10},{9,11},{10,... | collective-permute-start | bytes 1081352 | tf_op jit(solution)/shard_map/ppermute | solution.py:56
  498.2 24.0 %collective-permute-start.89 = (f32[16,256]{1,0:T(8,128)S(1)}, f32[16,256]{1,0:T(8,128)S(1)}, u32[]{:S(2)}, u32[]{:S(2)}) collective-permute-start(f32[16,256]{1,0:T(8,128)S(1)} %get-tuple-element.418), channel_id=1, source_target_pairs={{0,12},{4,8},{8,4},{12,0},{1,13},{5,9},{9,5},{13,1},{2,14},{6,10},... | collective-permute-start | bytes 49160 | tf_op jit(solution)/shard_map/ppermute | solution.py:59
  499.7 22.5 %collective-permute-start.88 = (f32[16,256]{1,0:T(8,128)S(1)}, f32[16,256]{1,0:T(8,128)}, u32[]{:S(2)}, u32[]{:S(2)}) collective-permute-start(f32[16,256]{1,0:T(8,128)S(1)} %get-tuple-element.419), channel_id=1, source_target_pairs={{0,8},{4,12},{8,0},{12,4},{1,9},{5,13},{9,1},{13,5},{2,10},{6,14},... | collective-permute-start | bytes 49160 | tf_op jit(solution)/shard_map/ppermute | solution.py:59
  501.1 21.1 %collective-permute-start.87 = (f32[16,256]{1,0:T(8,128)S(1)}, f32[16,256]{1,0:T(8,128)}, u32[]{:S(2)}, u32[]{:S(2)}) collective-permute-start(f32[16,256]{1,0:T(8,128)S(1)} %get-tuple-element.417), channel_id=1, source_target_pairs={{0,4},{4,0},{8,12},{12,8},{1,5},{5,1},{9,13},{13,9},{2,6},{6,2},{1... | collective-permute-start | bytes 49160 | tf_op jit(solution)/shard_map/ppermute | solution.py:59
  523.0 18.1 %all-to-all-start = ((bf16[4,128,1024]{2,1,0:T(8,128)(2,1)}), bf16[4,128,1024]{2,1,0:T(8,128)(2,1)S(1)}, u32[]{:S(2)}, u32[]{:S(2)}) async-start(bf16[4,128,1024]{2,1,0:T(8,128)(2,1)} %bitcast.130), calls=%async_computation.3 | async-start | bytes 2097152 | tf_op jit(solution)/shard_map/all_to_all | solution.py:733
  530.6 14.7 %collective-permute-start.90 = (bf16[528,256]{1,0:T(8,128)(2,1)S(1)}, bf16[528,256]{1,0:T(8,128)(2,1)}, u32[]{:S(2)}, u32[]{:S(2)}) collective-permute-start(bf16[528,256]{1,0:T(8,128)(2,1)S(1)} %pad_maximum_fusion.45), channel_id=1, source_target_pairs={{0,2},{1,3},{2,0},{3,1},{4,6},{5,7},{6,4},{7,5},{8,10},{9,11},{10,... | collective-permute-start | bytes 811016 | tf_op jit(solution)/shard_map/ppermute | solution.py:56
  (164 other events, 954.4 us)
Sparse Core Ops, SparseCore 0:
  76.5 60.6 all-gather.5
  140.3 36.3 all-gather.3
  178.5 64.8 all-gather.7
  282.4 66.5 reduce-scatter.4
  352.3 35.1 reduce-scatter.6
  390.4 60.2 reduce-scatter.8
  465.5 33.3 reduce-scatter.10

commit v2 on v1

--- a/solution.py
+++ b/solution.py
@@ -252,15 +252,19 @@
 
 
 def attend_kernel(count, place_ref, first_ref, *refs):
-    blocks, (out_ref, low_ref, lse_ref, kt_ref, v_ref) = refs[:count], refs[count:]
+    blocks, (out_ref, low_ref, lse_ref, kt_ref, v_ref, q_ref) = refs[:count], refs[count:]
     size = blocks[0].shape[2]
     x, part = place_ref[0], place_ref[1]
     for k in range(count):
         kt_ref[x ^ k] = blocks[k][1].T
         v_ref[x ^ k] = blocks[k][2]
     for k in range(4):
+        q_ref[k] = blocks[k][0] * BF(HEAD ** (-0.5))
+
+    @pl.loop(0, 4)
+    def _(k):
         block = x ^ k
-        query = blocks[k][0] * BF(HEAD ** (-0.5))
+        query = q_ref[k]
         first_row = first_ref[k]
 
         def step(kb, carry):
@@ -300,6 +304,7 @@
         scratch_shapes=[
             pltpu.VMEM((count, size, HEAD), BF),
             pltpu.VMEM((count, HEAD, size), BF),
+            pltpu.VMEM((4, HEAD, size), BF),
         ],
         name="attend",
     )(where_all, first_query, *blocks)
@@ -307,7 +312,8 @@
 
 def back_kernel(count, place_ref, first_ref, out_ref, lse_ref, *refs):
     blocks, grads = refs[:count], refs[count : count + 4]
-    dq_ref, dk_ref, dv_ref, kt_ref, vt_ref, k_ref, dks_ref, dvs_ref = refs[count + 4 :]
+    dq_ref, dk_ref, dv_ref, kt_ref, vt_ref, k_ref, dks_ref, dvs_ref = refs[count + 4 : -2]
+    q_ref, grad_ref = refs[-2:]
     size = blocks[0].shape[2]
     x, part = place_ref[0], place_ref[1]
     for k in range(count):
@@ -317,10 +323,15 @@
     dks_ref[...] = jnp.zeros_like(dks_ref)
     dvs_ref[...] = jnp.zeros_like(dvs_ref)
     for k in range(4):
+        q_ref[k] = blocks[k][0] * BF(HEAD ** (-0.5))
+        grad_ref[k] = grads[k][...]
+
+    @pl.loop(0, 4)
+    def _(k):
         block = x ^ k
-        query = blocks[k][0] * BF(HEAD ** (-0.5))
+        query = q_ref[k]
         query_t = query.T
-        grad = grads[k][...]
+        grad = grad_ref[k]
         grad_t = grad.T
         delta = jnp.sum(grad.astype(F32) * out_ref[k], axis=0, keepdims=True)
         lse = lse_ref[k]
@@ -339,6 +350,7 @@
             place_ref[2 + block], block + 1, step, jnp.zeros((HEAD, size), F32)
         )
         dq_ref[k] = dq * HEAD ** (-0.5)
+
     for k in range(count):
         dk_ref[k] = dks_ref[x ^ k].T
         dv_ref[k] = dvs_ref[x ^ k].T
@@ -362,6 +374,8 @@
             pltpu.VMEM((count, HEAD, size), BF),
             pltpu.VMEM((count, size, HEAD), F32),
             pltpu.VMEM((count, size, HEAD), F32),
+            pltpu.VMEM((4, HEAD, size), BF),
+            pltpu.VMEM((4, HEAD, size), BF),
         ],
         name="attend_back",
     )(where_all, first_query, out, log_total, *blocks, *grads)
@@ -422,9 +436,9 @@
     for level in range(1, LAYERS):
         own = own_columns(plan, jnp.concatenate(own_weights(level), axis=1))
         own_later.append(own)
-    cuts = [0, qkv_rows + out_rows]
-    for _ in range(3):
-        cuts.append(cuts[-1] + mlp_rows)
+    cut = qkv_rows + out_rows
+    pieces = [(cut, cut + mlp_rows), (0, cut)]
+    pieces += [(cut + i * mlp_rows, cut + (i + 1) * mlp_rows) for i in (1, 2)]
     def own_rows(array):
         mine = lax.dynamic_slice_in_dim(array, plan.part * part_rows, part_rows, 0)
         got = plan.core(
@@ -450,7 +464,7 @@
     own_rest, far_first, grad_rows = together(own_rest, far_first, grad_rows)
     out_branch = gather_rows(plan, grad_rows)
     first = jnp.concatenate([own, far_first, gain_pair], axis=0)
-    first, out_branch = together(all_columns(plan, first, True), out_branch)
+    first = all_columns(plan, first, True)
     w_qkv, gain_full = first[: 2 * qkv_rows], first[2 * qkv_rows :].astype(F32)
     last_far = plan.far(own_rest)
 
@@ -491,6 +505,8 @@
             normed = (stream * scale_attn * gain_full[level : level + 1]).astype(BF)
             normed_all = gather_rows(plan, normed)
         qkv = dot(w_qkv, normed_all, 1, 1)
+        if level + 1 < LAYERS:
+            qkv, own_later[level] = together(qkv, own_later[level])
         qkv = qkv.reshape(2, 3, 2, HEAD, tok_rows)
         query = turn(qkv[:, 0], cos_own, sine_own).astype(BF)
         key = turn(qkv[:, 1], cos_own, sine_own).astype(BF)
@@ -505,21 +521,26 @@
         far_next = []
 
         def next_far():
-            i = len(far_next)
-            piece = own_later[level][cuts[i] : cuts[i + 1]]
+            nonlocal last_far
+            start, end = pieces[len(far_next)]
+            piece = own_later[level][start:end]
             if far_next:
                 piece, far_next[-1] = together(piece, far_next[-1])
+            else:
+                piece, last_far = together(piece, last_far)
             return plan.far(piece)
 
         if level == 0:
-            heads, last_far = together(heads, last_far)
+            got = next_far()
+            heads, last_far, out_branch, got = together(heads, last_far, out_branch, got)
+            far_next.append(got)
             rest = with_far(own_rest, last_far, counts[1:])
             w_o = all_columns(plan, rest[: 2 * out_rows], True)
             rest = all_columns(plan, rest[2 * out_rows :], False)
             w_mlp = (rest[: 2 * width], rest[2 * width :])
         out, out_low, log_total = attend(where_all, first_query, heads)
         if ahead:
-            out_low, got = together(out_low, next_far())
+            out_low, got, w_o = together(out_low, next_far(), w_o)
             far_next.append(got)
         attended = from_heads(plan, [out_low[k] for k in range(4)])
         attended = attended.reshape(4 * HEAD, tok_rows)
@@ -540,12 +561,11 @@
         gate, upward = gate_up[:, :width], gate_up[:, width:]
         hidden = (gate * jax.nn.sigmoid(gate) * upward).astype(BF)
         if ahead:
-            hidden, got = together(hidden, next_far())
-            far_next.append(got)
             own = own_later[level]
-            w_attn = with_far(own[: cuts[1]], far_next[0], counts[:2])
+            w_attn = with_far(own[:cut], far_next[1], counts[:2])
             w_attn = all_columns(plan, w_attn, False)
-            rest = with_far(own[cuts[1] :], jnp.concatenate(far_next[1:], axis=0), counts[2:])
+            got = jnp.concatenate([far_next[0], far_next[2], far_next[3]], axis=0)
+            rest = with_far(own[cut:], got, counts[2:])
             rest = all_columns(plan, rest, False)
             later = (rest[: 2 * width], rest[2 * width :])
             full.append((w_attn[: 2 * qkv_rows], w_attn[2 * qkv_rows :], later))
@@ -693,15 +713,17 @@
         grad_qkv = from_heads(plan, grad_heads).reshape(2, 2, 3, HEAD, tok_rows)
         grad_qkv = jnp.swapaxes(grad_qkv, 1, 2).reshape(-1, tok_rows)
         if level == 0:
-            mine_first, far = far_halves(sum_mlp, counts[2:])
-            far_d, far_c = together(far[:mlp_rows], far_c)
-            far_d = plan.far(far_d)
             grad_qkv, far_c = together(grad_qkv, far_c)
         elif level == LAYERS - 1:
             grad_qkv, last = together(grad_qkv, last)
             outputs = natural_rows(plan, last)
         grad_wqkv = dot(grad_qkv, normed_all, 1, 0).astype(BF)
-        grad_normed = sum_rows(plan, dot(grad_qkv, w_qkv, 0, 0))
+        partial = dot(grad_qkv, w_qkv, 0, 0)
+        if level == 0:
+            mine_first, far = far_halves(sum_mlp, counts[2:])
+            far_d, partial = together(far[:mlp_rows], partial)
+            far_d = plan.far(far_d)
+        grad_normed = sum_rows(plan, partial)
         if level == 0:
             far_e = far[mlp_rows:]
             grad_normed, far_d, far_e = together(grad_normed, far_d, far_e)

time: 570 us -> 575 us (level)
  other arithmetic: 59.5 us -> 70.6 us
  waiting for transfers between devices: 258 us -> 247 us
    ppermute x14, starting transfers between devices: 26.9 us -> 16.8 us  [far(): return lax.ppermute(value, 'tp', [(i, i ^ 2) for i in range(self.tp)])]
    reduce_scatter x4, starting transfers between devices: 0.55 us -> 10.6 us  [columns_sum(): return lax.psum_scatter(grad, 'ctx', scatter_dimension=1, tiled=True)]
    reduce_scatter x4, waiting for transfers between devices: 9.78 us -> 0.06 us  [columns_sum(): return lax.psum_scatter(grad, 'ctx', scatter_dimension=1, tiled=True)]
    ppermute x14, waiting for transfers between devices: 44.5 us -> 51.6 us  [far(): return lax.ppermute(value, 'tp', [(i, i ^ 2) for i in range(self.tp)])]
    all_to_all x1, waiting for transfers between devices: 9.44 us -> 2.62 us  [local(): lax.all_to_all(slots, 'ctx', split_axis=0, concat_axis=0, tiled=True)]
    unnamed x261 -> x283, local copies, waits for them, and re-layouts: 28 us -> 22.2 us
  transfers between devices with their start and end apart: 102 -> 102, of which waited for: 60 -> 60; matrix products, arithmetic and copies ran while one was open for 23% -> 26% of each run, Pallas kernels for 6% -> 6%
where the time goes in v2:
time: 575 us; the launch traced here: 565 us
  waiting for transfers between devices  247 us (43%)
  starting transfers between devices  89.8 us (16%)
  other arithmetic  70.6 us (12%)
  local copies, waits for them, and re-layouts  57.7 us (10%)
  matrix products  46.5 us (8%)
  Pallas kernels  35.9 us (6%)
  between operations  17.4 us (3%)
    ppermute x19, waiting for transfers between devices, near(): return lax.ppermute(value, 'tp', [(i, i ^ 1) for i in range(self.tp)])  114 us
    ppermute x33, waiting for transfers between devices, side(): return lax.ppermute(value, 'ctx', [(i, i ^ k) for i in range(self.ctx)])  60.7 us
    ppermute x14, waiting for transfers between devices, far(): return lax.ppermute(value, 'tp', [(i, i ^ 2) for i in range(self.tp)])  51.6 us
    dot_general x24, matrix products, dot(): lax.dot_general(left, right, (((left_dim,), (right_dim,)), ((), ())), pre...  46.5 us
    ppermute x33, starting transfers between devices, side(): return lax.ppermute(value, 'ctx', [(i, i ^ k) for i in range(self.ctx)])  39.6 us
    unnamed x283, local copies, waits for them, and re-layouts  22.2 us
    pallas_call x2, Pallas kernels, attend_back(): pl.pallas_call(functools.partial(back_kernel, count), out_shape=(jax.Shap...  20.2 us
    ppermute x28, waiting for transfers between devices, core(): return lax.ppermute(value, 'fsdp', [(i, i ^ 1) for i in range(self.fsdp)])  17.9 us
  transfers between devices with their start and end apart: 102, of which 60 were waited for; matrix products, arithmetic and copies ran while one was open for 26% of the time, Pallas kernels for 6%

profile of v2, /device:TPU:0, one launch (start us, length us, event | category | flops | bytes accessed | tf_op | source)
XLA Modules:
  0.0 565.3 jit_solution(867599982755157376)
XLA Ops:
  20.9 3.7 collective-permute-start.3
  29.9 4.5 collective-permute-done.3
  40.4 3.4 collective-permute-start.16
  43.9 5.4 collective-permute-done.17
  50.0 5.3 collective-permute-done.7
  64.4 5.2 collective-permute-done.16
  71.4 7.8 %collective-permute-done.19 = bf16[352,256]{1,0:T(8,128)(2,1)S(1)} collective-permute-done((bf16[352,256]{1,0:T(8,128)(2,1)S(1)}, bf16[352,256]{1,0:T(8,128)(2,1)S(1)}, u32[]{:S(2)}, u32[]{:S(2)}) %collective-permute-start.19) | collective-permute-done | bytes 180256 | tf_op jit(solution)/shard_map/ppermute | solution.py:56
  89.6 7.9 %attend.2 = (f32[4,64,512]{2,1,0:T(8,128)}, bf16[4,64,512]{2,1,0:T(8,128)(2,1)}, f32[4,1,512]{2,1,0:T(1,128)}) custom-call(s32[6]{0:T(128)} %pad_add_fusion.2.place_ref, s32[4,1,512]{2,1,0:T(1,128)} %broadcast_in_dim.84.first_ref, bf16[3,64,512]{2,1,0:T(8,128)(2,1)} %get-tuple-element.106.refs_0_, bf16[3,64,512]{2,1,0:T(8,128)(2,1)} %copy-done.43, ...), custom_call_target="tpu_custom_call" | custom-call | tf_op jit(solution)/shard_map/attend/pallas_call | solution.py:295
  98.5 3.1 collective-permute-done.20
  111.7 4.4 collective-permute-done.27
  119.0 3.1 collective-permute-start.30
  122.1 9.0 %collective-permute-done.29 = bf16[128,1024]{1,0:T(8,128)(2,1)S(1)} collective-permute-done((bf16[128,1024]{1,0:T(8,128)(2,1)S(1)}, bf16[128,1024]{1,0:T(8,128)(2,1)S(1)}, u32[]{:S(2)}, u32[]{:S(2)}) %collective-permute-start.29) | collective-permute-done | bytes 262176 | tf_op jit(solution)/shard_map/ppermute | solution.py:53
  134.6 5.3 collective-permute-done.31
  143.0 3.9 fusion.6
  157.0 5.8 %collective-permute-done.34 = bf16[128,1024]{1,0:T(8,128)(2,1)} collective-permute-done((bf16[128,1024]{1,0:T(8,128)(2,1)}, bf16[128,1024]{1,0:T(8,128)(2,1)}, u32[]{:S(2)}, u32[]{:S(2)}) %collective-permute-start.34) | collective-permute-done | bytes 262176 | tf_op jit(solution)/shard_map/ppermute | solution.py:53
  166.9 6.1 %collective-permute-done.35 = bf16[128,1024]{1,0:T(8,128)(2,1)S(1)} collective-permute-done((bf16[128,1024]{1,0:T(8,128)(2,1)S(1)}, bf16[128,1024]{1,0:T(8,128)(2,1)S(1)}, u32[]{:S(2)}, u32[]{:S(2)}) %collective-permute-start.35) | collective-permute-done | bytes 262176 | tf_op jit(solution)/shard_map/ppermute | solution.py:53
  184.4 6.7 %collective-permute-done.37.refs_1_ = bf16[3,64,512]{2,1,0:T(8,128)(2,1)S(1)} collective-permute-done((bf16[3,64,512]{2,1,0:T(8,128)(2,1)S(1)}, bf16[3,64,512]{2,1,0:T(8,128)(2,1)S(1)}, u32[]{:S(2)}, u32[]{:S(2)}) %collective-permute-start.37) | collective-permute-done | bytes 196640 | tf_op jit(solution)/shard_map/ppermute | solution.py:59
  191.1 4.3 collective-permute-done.38.refs_2_
  195.4 4.2 collective-permute-done.39.refs_3_
  199.6 7.8 %attend.3 = (f32[4,64,512]{2,1,0:T(8,128)}, bf16[4,64,512]{2,1,0:T(8,128)(2,1)}, f32[4,1,512]{2,1,0:T(1,128)}) custom-call(s32[6]{0:T(128)} %pad_add_fusion.2.place_ref, s32[4,1,512]{2,1,0:T(1,128)} %broadcast_in_dim.84.first_ref, bf16[3,64,512]{2,1,0:T(8,128)(2,1)} %get-tuple-element.332.refs_0_, bf16[3,64,512]{2,1,0:T(8,128)(2,1)} %copy-done.46, ...), custom_call_target="tpu_custom_call" | custom-call | tf_op jit(solution)/shard_map/attend/pallas_call | solution.py:295
  223.3 7.3 %collective-permute-done.44 = bf16[128,1024]{1,0:T(8,128)(2,1)S(1)} collective-permute-done((bf16[128,1024]{1,0:T(8,128)(2,1)S(1)}, bf16[128,1024]{1,0:T(8,128)(2,1)S(1)}, u32[]{:S(2)}, u32[]{:S(2)}) %collective-permute-start.44) | collective-permute-done | bytes 262176 | tf_op jit(solution)/shard_map/ppermute | solution.py:53
  232.1 6.5 %collective-permute-done.45 = bf16[128,1024]{1,0:T(8,128)(2,1)S(1)} collective-permute-done((bf16[128,1024]{1,0:T(8,128)(2,1)S(1)}, bf16[128,1024]{1,0:T(8,128)(2,1)S(1)}, u32[]{:S(2)}, u32[]{:S(2)}) %collective-permute-start.45) | collective-permute-done | bytes 262176 | tf_op jit(solution)/shard_map/ppermute | solution.py:53
  241.7 4.0 fusion.2
  258.9 5.3 collective-permute-done.48
  268.2 6.7 %collective-permute-done.49 = bf16[128,1024]{1,0:T(8,128)(2,1)S(1)} collective-permute-done((bf16[128,1024]{1,0:T(8,128)(2,1)S(1)}, bf16[128,1024]{1,0:T(8,128)(2,1)S(1)}, u32[]{:S(2)}, u32[]{:S(2)}) %collective-permute-start.49) | collective-permute-done | bytes 262176 | tf_op jit(solution)/shard_map/ppermute | solution.py:53
  275.8 10.2 %reduce-scatter.7.cloned.1.call-start = ((), (), s32[]{:S(2)}) async-start(), calls=%async_computation.9 | async-start | bytes 2621440 | tf_op jit(solution)/shard_map/reduce_scatter | solution.py:165
  302.2 3.5 collective-permute-done.53.refs_7_
  310.8 10.1 %attend_back.2 = (f32[4,64,512]{2,1,0:T(8,128)}, f32[4,64,512]{2,1,0:T(8,128)}, f32[4,64,512]{2,1,0:T(8,128)}) custom-call(s32[6]{0:T(128)} %pad_add_fusion.2.place_ref, s32[4,1,512]{2,1,0:T(1,128)} %broadcast_in_dim.84.first_ref, f32[4,64,512]{2,1,0:T(8,128)} %get-tuple-element.123.out_ref, f32[4,1,512]{2,1,0:T(1,128)} %get-tuple-element.124.lse_ref, ...), custom_call_target="tpu_custom_call" | custom-call | tf_op jit(solution)/shard_map/attend_back/pallas_call | solution.py:362
  330.5 3.0 collective-permute-done.57
  333.5 5.2 collective-permute-done.58
  338.9 5.3 collective-permute-done.61
  354.2 4.8 collective-permute-done.63
  363.5 7.1 %collective-permute-done.64 = bf16[128,1024]{1,0:T(8,128)(2,1)S(1)} collective-permute-done((bf16[128,1024]{1,0:T(8,128)(2,1)S(1)}, bf16[128,1024]{1,0:T(8,128)(2,1)S(1)}, u32[]{:S(2)}, u32[]{:S(2)}) %collective-permute-start.64) | collective-permute-done | bytes 262176 | tf_op jit(solution)/shard_map/ppermute | solution.py:53
  385.8 5.8 %collective-permute-done.67 = bf16[128,1024]{1,0:T(8,128)(2,1)S(1)} collective-permute-done((bf16[128,1024]{1,0:T(8,128)(2,1)}, bf16[128,1024]{1,0:T(8,128)(2,1)S(1)}, u32[]{:S(2)}, u32[]{:S(2)}) %collective-permute-start.67) | collective-permute-done | bytes 262176 | tf_op jit(solution)/shard_map/ppermute | solution.py:53
  397.6 6.8 %collective-permute-done.68 = bf16[128,1024]{1,0:T(8,128)(2,1)S(1)} collective-permute-done((bf16[128,1024]{1,0:T(8,128)(2,1)S(1)}, bf16[128,1024]{1,0:T(8,128)(2,1)S(1)}, u32[]{:S(2)}, u32[]{:S(2)}) %collective-permute-start.68) | collective-permute-done | bytes 262176 | tf_op jit(solution)/shard_map/ppermute | solution.py:53
  412.9 6.2 %collective-permute-done.73 = bf16[352,256]{1,0:T(8,128)(2,1)S(1)} collective-permute-done((bf16[352,256]{1,0:T(8,128)(2,1)S(1)}, bf16[352,256]{1,0:T(8,128)(2,1)S(1)}, u32[]{:S(2)}, u32[]{:S(2)}) %collective-permute-start.73) | collective-permute-done | bytes 180256 | tf_op jit(solution)/shard_map/ppermute | solution.py:56
  421.0 10.1 %attend_back.3 = (f32[4,64,512]{2,1,0:T(8,128)}, f32[4,64,512]{2,1,0:T(8,128)}, f32[4,64,512]{2,1,0:T(8,128)}) custom-call(s32[6]{0:T(128)} %pad_add_fusion.2.place_ref, s32[4,1,512]{2,1,0:T(1,128)} %broadcast_in_dim.84.first_ref, f32[4,64,512]{2,1,0:T(8,128)} %get-tuple-element.153.out_ref, f32[4,1,512]{2,1,0:T(1,128)} %get-tuple-element.154.lse_ref, ...), custom_call_target="tpu_custom_call" | custom-call | tf_op jit(solution)/shard_map/attend_back/pallas_call | solution.py:362
  437.5 8.2 %collective-permute-done.75 = bf16[3,64,512]{2,1,0:T(8,128)(2,1)S(1)} collective-permute-done((bf16[3,64,512]{2,1,0:T(8,128)(2,1)S(1)}, bf16[3,64,512]{2,1,0:T(8,128)(2,1)S(1)}, u32[]{:S(2)}, u32[]{:S(2)}) %collective-permute-start.75) | collective-permute-done | bytes 196640 | tf_op jit(solution)/shard_map/ppermute | solution.py:59
  446.4 7.8 %collective-permute-done.77 = bf16[3,64,512]{2,1,0:T(8,128)(2,1)S(1)} collective-permute-done((bf16[3,64,512]{2,1,0:T(8,128)(2,1)S(1)}, bf16[3,64,512]{2,1,0:T(8,128)(2,1)S(1)}, u32[]{:S(2)}, u32[]{:S(2)}) %collective-permute-start.77) | collective-permute-done | bytes 196640 | tf_op jit(solution)/shard_map/ppermute | solution.py:59
  454.2 3.8 collective-permute-done.78
  463.7 3.7 fusion.15
  477.7 8.9 %collective-permute-done.80 = bf16[128,1024]{1,0:T(8,128)(2,1)S(1)} collective-permute-done((bf16[128,1024]{1,0:T(8,128)(2,1)S(1)}, bf16[128,1024]{1,0:T(8,128)(2,1)S(1)}, u32[]{:S(2)}, u32[]{:S(2)}) %collective-permute-start.80) | collective-permute-done | bytes 262176 | tf_op jit(solution)/shard_map/ppermute | solution.py:53
  492.5 5.0 collective-permute-done.83
  497.5 5.2 collective-permute-done.82
  514.0 11.3 %collective-permute-done.85 = bf16[256,1024]{1,0:T(8,128)(2,1)S(1)} collective-permute-done((bf16[256,1024]{1,0:T(8,128)(2,1)S(1)}, bf16[256,1024]{1,0:T(8,128)(2,1)S(1)}, u32[]{:S(2)}, u32[]{:S(2)}) %collective-permute-start.85) | collective-permute-done | bytes 524320 | tf_op jit(solution)/shard_map/ppermute | solution.py:53
  525.4 3.0 gather_fusion
  532.4 3.5 all-to-all-start
  538.9 8.6 %collective-permute-done.90 = bf16[528,256]{1,0:T(8,128)(2,1)} collective-permute-done((bf16[528,256]{1,0:T(8,128)(2,1)}, bf16[528,256]{1,0:T(8,128)(2,1)}, u32[]{:S(2)}, u32[]{:S(2)}) %collective-permute-start.90) | collective-permute-done | bytes 270368 | tf_op jit(solution)/shard_map/ppermute | solution.py:56
  (753 shorter events, 263.9 us)
Async XLA Ops:
  7.2 135.8 %all-gather.6.cloned.1.call-start = ((), (), s32[]{:S(2)}) async-start(), calls=%async_computation.6 | async-start | bytes 5406720 | tf_op jit(solution)/shard_map/all_gather | solution.py:139
  11.6 17.0 %collective-permute-start.2 = (bf16[1184,128]{1,0:T(8,128)(2,1)}, bf16[1184,128]{1,0:T(8,128)(2,1)}, u32[]{:S(2)}, u32[]{:S(2)}) collective-permute-start(bf16[1184,128]{1,0:T(8,128)(2,1)} %get-tuple-element.348), channel_id=1, source_target_pairs={{0,16},{16,0},{1,17},{17,1},{2,18},{18,2},{3,19},{19,3},{4,20},{20... | collective-permute-start | bytes 909320 | tf_op jit(solution)/shard_map/ppermute | solution.py:50
  17.2 21.0 %collective-permute-start.12 = (bf16[1568,128]{1,0:T(8,128)(2,1)}, bf16[1568,128]{1,0:T(8,128)(2,1)S(1)}, u32[]{:S(2)}, u32[]{:S(2)}) collective-permute-start(bf16[1568,128]{1,0:T(8,128)(2,1)} %get-tuple-element.328), channel_id=1, source_target_pairs={{0,16},{16,0},{1,17},{17,1},{2,18},{18,2},{3,19},{19,3},{4,20},{20... | collective-permute-start | bytes 1204232 | tf_op jit(solution)/shard_map/ppermute | solution.py:50
  20.9 13.5 %collective-permute-start.3 = (bf16[384,256]{1,0:T(8,128)(2,1)S(1)}, bf16[384,256]{1,0:T(8,128)(2,1)S(1)}, u32[]{:S(2)}, u32[]{:S(2)}) collective-permute-start(bf16[384,256]{1,0:T(8,128)(2,1)S(1)} %maximum_select_fusion.2), channel_id=1, source_target_pairs={{0,2},{1,3},{2,0},{3,1},{4,6},{5,7},{6,4},{7,5},{8,10},{9,11},{10,... | collective-permute-start | bytes 589832 | tf_op jit(solution)/shard_map/ppermute | solution.py:56
  27.0 13.4 %collective-permute-start.10 = (bf16[128,1024]{1,0:T(8,128)(2,1)S(1)}, bf16[128,1024]{1,0:T(8,128)(2,1)S(1)}, u32[]{:S(2)}, u32[]{:S(2)}) collective-permute-start(bf16[128,1024]{1,0:T(8,128)(2,1)S(1)} %constant_dynamic-update-slice_fusion.8), channel_id=1, source_target_pairs={{0,1},{1,0},{2,3},{3,2},{4,5},{5,4},{6,7},{7,6},{8,9},{9,8},{10,11... | collective-permute-start | bytes 786440 | tf_op jit(solution)/shard_map/ppermute | solution.py:53
  34.7 14.7 %collective-permute-start.6 = (bf16[784,256]{1,0:T(8,128)(2,1)S(1)}, bf16[784,256]{1,0:T(8,128)(2,1)S(1)}, u32[]{:S(2)}, u32[]{:S(2)}) collective-permute-start(bf16[784,256]{1,0:T(8,128)(2,1)S(1)} %get-tuple-element.375), channel_id=1, source_target_pairs={{0,4},{4,0},{8,12},{12,8},{1,5},{5,1},{9,13},{13,9},{2,6},{6,2},{1... | collective-permute-start | bytes 1204232 | tf_op jit(solution)/shard_map/ppermute | solution.py:59
  36.3 19.1 %collective-permute-start.7 = (bf16[784,256]{1,0:T(8,128)(2,1)S(1)}, bf16[784,256]{1,0:T(8,128)(2,1)S(1)}, u32[]{:S(2)}, u32[]{:S(2)}) collective-permute-start(bf16[784,256]{1,0:T(8,128)(2,1)S(1)} %get-tuple-element.375), channel_id=1, source_target_pairs={{0,8},{4,12},{8,0},{12,4},{1,9},{5,13},{9,1},{13,5},{2,10},{6,14},... | collective-permute-start | bytes 1204232 | tf_op jit(solution)/shard_map/ppermute | solution.py:59
  37.8 17.6 %collective-permute-start.8 = (bf16[784,256]{1,0:T(8,128)(2,1)S(1)}, bf16[784,256]{1,0:T(8,128)(2,1)S(1)}, u32[]{:S(2)}, u32[]{:S(2)}) collective-permute-start(bf16[784,256]{1,0:T(8,128)(2,1)S(1)} %get-tuple-element.375), channel_id=1, source_target_pairs={{0,12},{4,8},{8,4},{12,0},{1,13},{5,9},{9,5},{13,1},{2,14},{6,10},... | collective-permute-start | bytes 1204232 | tf_op jit(solution)/shard_map/ppermute | solution.py:59
  38.2 11.1 %collective-permute-start.17 = (bf16[128,1024]{1,0:T(8,128)(2,1)S(1)}, bf16[128,1024]{1,0:T(8,128)(2,1)S(1)}, u32[]{:S(2)}, u32[]{:S(2)}) collective-permute-start(bf16[128,1024]{1,0:T(8,128)(2,1)S(1)} %constant_dynamic-update-slice_fusion), channel_id=1, source_target_pairs={{0,1},{1,0},{2,3},{3,2},{4,5},{5,4},{6,7},{7,6},{8,9},{9,8},{10,11... | collective-permute-start | bytes 786440 | tf_op jit(solution)/shard_map/ppermute | solution.py:53
  40.4 29.2 %collective-permute-start.16 = (bf16[1184,256]{1,0:T(8,128)(2,1)S(1)}, bf16[1184,256]{1,0:T(8,128)(2,1)S(1)}, u32[]{:S(2)}, u32[]{:S(2)}) collective-permute-start(bf16[1184,256]{1,0:T(8,128)(2,1)S(1)} %maximum_select_fusion.1), channel_id=1, source_target_pairs={{0,2},{1,3},{2,0},{3,1},{4,6},{5,7},{6,4},{7,5},{8,10},{9,11},{10,... | collective-permute-start | bytes 1818632 | tf_op jit(solution)/shard_map/ppermute | solution.py:56
  49.4 21.0 %collective-permute-start.18 = (bf16[256,1024]{1,0:T(8,128)(2,1)S(1)}, bf16[256,1024]{1,0:T(8,128)(2,1)S(1)}, u32[]{:S(2)}, u32[]{:S(2)}) collective-permute-start(bf16[256,1024]{1,0:T(8,128)(2,1)S(1)} %pad_maximum_fusion.24), channel_id=1, source_target_pairs={{0,16},{16,0},{1,17},{17,1},{2,18},{18,2},{3,19},{19,3},{4,20},{20... | collective-permute-start | bytes 1572872 | tf_op jit(solution)/shard_map/ppermute | solution.py:50
  60.2 18.9 %collective-permute-start.13 = (bf16[3,64,512]{2,1,0:T(8,128)(2,1)S(1)}, bf16[3,64,512]{2,1,0:T(8,128)(2,1)S(1)}, u32[]{:S(2)}, u32[]{:S(2)}) collective-permute-start(bf16[3,64,512]{2,1,0:T(8,128)(2,1)S(1)} %get-tuple-element.335), channel_id=1, source_target_pairs={{0,4},{4,0},{8,12},{12,8},{1,5},{5,1},{9,13},{13,9},{2,6},{6,2},{1... | collective-permute-start | bytes 589832 | tf_op jit(solution)/shard_map/ppermute | solution.py:59
  61.4 17.8 %collective-permute-start.14 = (bf16[3,64,512]{2,1,0:T(8,128)(2,1)S(1)}, bf16[3,64,512]{2,1,0:T(8,128)(2,1)S(1)}, u32[]{:S(2)}, u32[]{:S(2)}) collective-permute-start(bf16[3,64,512]{2,1,0:T(8,128)(2,1)S(1)} %get-tuple-element.334), channel_id=1, source_target_pairs={{0,8},{4,12},{8,0},{12,4},{1,9},{5,13},{9,1},{13,5},{2,10},{6,14},... | collective-permute-start | bytes 589832 | tf_op jit(solution)/shard_map/ppermute | solution.py:59
  62.3 16.9 %collective-permute-start.15 = (bf16[3,64,512]{2,1,0:T(8,128)(2,1)S(1)}, bf16[3,64,512]{2,1,0:T(8,128)(2,1)S(1)}, u32[]{:S(2)}, u32[]{:S(2)}) collective-permute-start(bf16[3,64,512]{2,1,0:T(8,128)(2,1)S(1)} %get-tuple-element.333), channel_id=1, source_target_pairs={{0,12},{4,8},{8,4},{12,0},{1,13},{5,9},{9,5},{13,1},{2,14},{6,10},... | collective-permute-start | bytes 589832 | tf_op jit(solution)/shard_map/ppermute | solution.py:59
  82.8 91.3 %all-gather.4.cloned.1.call-start = ((), (), s32[]{:S(2)}) async-start(), calls=%async_computation.5 | async-start | bytes 2621440 | tf_op jit(solution)/shard_map/all_gather | solution.py:139
  84.0 13.5 %collective-permute-start.21 = (bf16[256,256]{1,0:T(8,128)(2,1)S(1)}, bf16[256,256]{1,0:T(8,128)(2,1)S(1)}, u32[]{:S(2)}, u32[]{:S(2)}) collective-permute-start(bf16[256,256]{1,0:T(8,128)(2,1)S(1)} %get-tuple-element.411), channel_id=1, source_target_pairs={{0,4},{4,0},{8,12},{12,8},{1,5},{5,1},{9,13},{13,9},{2,6},{6,2},{1... | collective-permute-start | bytes 393224 | tf_op jit(solution)/shard_map/ppermute | solution.py:59
  86.9 10.7 %collective-permute-start.22 = (bf16[256,256]{1,0:T(8,128)(2,1)S(1)}, bf16[256,256]{1,0:T(8,128)(2,1)}, u32[]{:S(2)}, u32[]{:S(2)}) collective-permute-start(bf16[256,256]{1,0:T(8,128)(2,1)S(1)} %get-tuple-element.411), channel_id=1, source_target_pairs={{0,8},{4,12},{8,0},{12,4},{1,9},{5,13},{9,1},{13,5},{2,10},{6,14},... | collective-permute-start | bytes 393224 | tf_op jit(solution)/shard_map/ppermute | solution.py:59
  89.0 12.7 %collective-permute-start.20 = (bf16[512,256]{1,0:T(8,128)(2,1)S(1)}, bf16[512,256]{1,0:T(8,128)(2,1)S(1)}, u32[]{:S(2)}, u32[]{:S(2)}) collective-permute-start(bf16[512,256]{1,0:T(8,128)(2,1)S(1)} %slice.966), channel_id=1, source_target_pairs={{0,2},{1,3},{2,0},{3,1},{4,6},{5,7},{6,4},{7,5},{8,10},{9,11},{10,... | collective-permute-start | bytes 786440 | tf_op jit(solution)/shard_map/ppermute | solution.py:56
  118.9 12.3 %collective-permute-start.29 = (bf16[128,1024]{1,0:T(8,128)(2,1)S(1)}, bf16[128,1024]{1,0:T(8,128)(2,1)S(1)}, u32[]{:S(2)}, u32[]{:S(2)}) collective-permute-start(bf16[128,1024]{1,0:T(8,128)(2,1)S(1)} %slice.1788), channel_id=1, source_target_pairs={{0,1},{1,0},{2,3},{3,2},{4,5},{5,4},{6,7},{7,6},{8,9},{9,8},{10,11... | collective-permute-start | bytes 786440 | tf_op jit(solution)/shard_map/ppermute | solution.py:53
  119.0 12.2 %collective-permute-start.30 = (bf16[352,256]{1,0:T(8,128)(2,1)S(1)}, bf16[352,256]{1,0:T(8,128)(2,1)S(1)}, u32[]{:S(2)}, u32[]{:S(2)}) collective-permute-start(bf16[352,256]{1,0:T(8,128)(2,1)S(1)} %get-tuple-element.121), channel_id=1, source_target_pairs={{0,2},{1,3},{2,0},{3,1},{4,6},{5,7},{6,4},{7,5},{8,10},{9,11},{10,... | collective-permute-start | bytes 540680 | tf_op jit(solution)/shard_map/ppermute | solution.py:56
  134.3 105.2 %all-gather.8.cloned.1.call-start = ((), (), s32[]{:S(2)}) async-start(), calls=%async_computation.7 | async-start | bytes 5406720 | tf_op jit(solution)/shard_map/all_gather | solution.py:139
  157.0 203.1 %reduce-scatter.5.cloned.1.call-start = ((), (), s32[]{:S(2)}) async-start(), calls=%async_computation.8 | async-start | bytes 5406720 | tf_op jit(solution)/shard_map/reduce_scatter | solution.py:165
  182.4 13.1 %collective-permute-start.38 = (bf16[3,64,512]{2,1,0:T(8,128)(2,1)S(1)}, bf16[3,64,512]{2,1,0:T(8,128)(2,1)S(1)}, u32[]{:S(2)}, u32[]{:S(2)}) collective-permute-start(bf16[3,64,512]{2,1,0:T(8,128)(2,1)S(1)} %get-tuple-element.330), channel_id=1, source_target_pairs={{0,8},{4,12},{8,0},{12,4},{1,9},{5,13},{9,1},{13,5},{2,10},{6,14},... | collective-permute-start | bytes 589832 | tf_op jit(solution)/shard_map/ppermute | solution.py:59
  183.9 15.7 %collective-permute-start.39 = (bf16[3,64,512]{2,1,0:T(8,128)(2,1)S(1)}, bf16[3,64,512]{2,1,0:T(8,128)(2,1)}, u32[]{:S(2)}, u32[]{:S(2)}) collective-permute-start(bf16[3,64,512]{2,1,0:T(8,128)(2,1)S(1)} %get-tuple-element.329), channel_id=1, source_target_pairs={{0,12},{4,8},{8,4},{12,0},{1,13},{5,9},{9,5},{13,1},{2,14},{6,10},... | collective-permute-start | bytes 589832 | tf_op jit(solution)/shard_map/ppermute | solution.py:59
  275.8 13.1 %collective-permute-start.50 = (bf16[256,1024]{1,0:T(8,128)(2,1)}, bf16[256,1024]{1,0:T(8,128)(2,1)}, u32[]{:S(2)}, u32[]{:S(2)}) collective-permute-start(bf16[256,1024]{1,0:T(8,128)(2,1)} %pad_maximum_fusion.29), channel_id=1, source_target_pairs={{0,16},{16,0},{1,17},{17,1},{2,18},{18,2},{3,19},{19,3},{4,20},{20... | collective-permute-start | bytes 1572872 | tf_op jit(solution)/shard_map/ppermute | solution.py:50
  275.8 117.0 %reduce-scatter.7.cloned.1.call-start = ((), (), s32[]{:S(2)}) async-start(), calls=%async_computation.9 | async-start | bytes 2621440 | tf_op jit(solution)/shard_map/reduce_scatter | solution.py:165
  310.8 14.4 %collective-permute-start.56 = (bf16[128,1024]{1,0:T(8,128)(2,1)}, bf16[128,1024]{1,0:T(8,128)(2,1)}, u32[]{:S(2)}, u32[]{:S(2)}) collective-permute-start(bf16[128,1024]{1,0:T(8,128)(2,1)} %constant_dynamic-update-slice_fusion.29), channel_id=1, source_target_pairs={{0,2},{1,3},{2,0},{3,1},{4,6},{5,7},{6,4},{7,5},{8,10},{9,11},{10,... | collective-permute-start | bytes 786440 | tf_op jit(solution)/shard_map/ppermute | solution.py:56
  327.2 11.6 %collective-permute-start.58 = (bf16[3,64,512]{2,1,0:T(8,128)(2,1)S(1)}, bf16[3,64,512]{2,1,0:T(8,128)(2,1)S(1)}, u32[]{:S(2)}, u32[]{:S(2)}) collective-permute-start(bf16[3,64,512]{2,1,0:T(8,128)(2,1)S(1)} %pad_maximum_fusion.52), channel_id=1, source_target_pairs={{0,8},{4,12},{8,0},{12,4},{1,9},{5,13},{9,1},{13,5},{2,10},{6,14},... | collective-permute-start | bytes 589832 | tf_op jit(solution)/shard_map/ppermute | solution.py:59
  327.4 11.4 %collective-permute-start.59 = (bf16[3,64,512]{2,1,0:T(8,128)(2,1)S(1)}, bf16[3,64,512]{2,1,0:T(8,128)(2,1)S(1)}, u32[]{:S(2)}, u32[]{:S(2)}) collective-permute-start(bf16[3,64,512]{2,1,0:T(8,128)(2,1)S(1)} %pad_maximum_fusion.53), channel_id=1, source_target_pairs={{0,12},{4,8},{8,4},{12,0},{1,13},{5,9},{9,5},{13,1},{2,14},{6,10},... | collective-permute-start | bytes 589832 | tf_op jit(solution)/shard_map/ppermute | solution.py:59
  330.4 13.8 %collective-permute-start.61 = (bf16[256,1024]{1,0:T(8,128)(2,1)S(1)}, bf16[256,1024]{1,0:T(8,128)(2,1)S(1)}, u32[]{:S(2)}, u32[]{:S(2)}) collective-permute-start(bf16[256,1024]{1,0:T(8,128)(2,1)S(1)} %pad_maximum_fusion.30), channel_id=1, source_target_pairs={{0,1},{1,0},{2,3},{3,2},{4,5},{5,4},{6,7},{7,6},{8,9},{9,8},{10,11... | collective-permute-start | bytes 1572872 | tf_op jit(solution)/shard_map/ppermute | solution.py:53
  354.1 115.4 %reduce-scatter.9.cloned.1.call-start = ((), (), s32[]{:S(2)}) async-start(), calls=%async_computation.10 | async-start | bytes 5406720 | tf_op jit(solution)/shard_map/reduce_scatter | solution.py:165
  392.8 111.7 %reduce-scatter.11.cloned.1.call-start = ((), (), s32[]{:S(2)}) async-start(), calls=%async_computation.11 | async-start | bytes 2621440 | tf_op jit(solution)/shard_map/reduce_scatter | solution.py:165
  407.7 11.4 %collective-permute-start.73 = (bf16[352,256]{1,0:T(8,128)(2,1)S(1)}, bf16[352,256]{1,0:T(8,128)(2,1)S(1)}, u32[]{:S(2)}, u32[]{:S(2)}) collective-permute-start(bf16[352,256]{1,0:T(8,128)(2,1)S(1)} %get-tuple-element.266), channel_id=1, source_target_pairs={{0,2},{1,3},{2,0},{3,1},{4,6},{5,7},{6,4},{7,5},{8,10},{9,11},{10,... | collective-permute-start | bytes 540680 | tf_op jit(solution)/shard_map/ppermute | solution.py:56
  419.2 14.3 %collective-permute-start.74 = (bf16[352,256]{1,0:T(8,128)(2,1)}, bf16[352,256]{1,0:T(8,128)(2,1)S(1)}, u32[]{:S(2)}, u32[]{:S(2)}) collective-permute-start(bf16[352,256]{1,0:T(8,128)(2,1)} %get-tuple-element.165), channel_id=1, source_target_pairs={{0,2},{1,3},{2,0},{3,1},{4,6},{5,7},{6,4},{7,5},{8,10},{9,11},{10,... | collective-permute-start | bytes 540680 | tf_op jit(solution)/shard_map/ppermute | solution.py:56
  433.6 12.0 %collective-permute-start.75 = (bf16[3,64,512]{2,1,0:T(8,128)(2,1)S(1)}, bf16[3,64,512]{2,1,0:T(8,128)(2,1)S(1)}, u32[]{:S(2)}, u32[]{:S(2)}) collective-permute-start(bf16[3,64,512]{2,1,0:T(8,128)(2,1)S(1)} %pad_maximum_fusion.54), channel_id=1, source_target_pairs={{0,4},{4,0},{8,12},{12,8},{1,5},{5,1},{9,13},{13,9},{2,6},{6,2},{1... | collective-permute-start | bytes 589832 | tf_op jit(solution)/shard_map/ppermute | solution.py:59
  434.6 11.8 %collective-permute-start.76 = (bf16[3,64,512]{2,1,0:T(8,128)(2,1)S(1)}, bf16[3,64,512]{2,1,0:T(8,128)(2,1)S(1)}, u32[]{:S(2)}, u32[]{:S(2)}) collective-permute-start(bf16[3,64,512]{2,1,0:T(8,128)(2,1)S(1)} %pad_maximum_fusion.55), channel_id=1, source_target_pairs={{0,8},{4,12},{8,0},{12,4},{1,9},{5,13},{9,1},{13,5},{2,10},{6,14},... | collective-permute-start | bytes 589832 | tf_op jit(solution)/shard_map/ppermute | solution.py:59
  436.2 18.0 %collective-permute-start.77 = (bf16[3,64,512]{2,1,0:T(8,128)(2,1)S(1)}, bf16[3,64,512]{2,1,0:T(8,128)(2,1)S(1)}, u32[]{:S(2)}, u32[]{:S(2)}) collective-permute-start(bf16[3,64,512]{2,1,0:T(8,128)(2,1)S(1)} %pad_maximum_fusion.56), channel_id=1, source_target_pairs={{0,12},{4,8},{8,4},{12,0},{1,13},{5,9},{9,5},{13,1},{2,14},{6,10},... | collective-permute-start | bytes 589832 | tf_op jit(solution)/shard_map/ppermute | solution.py:59
  437.4 20.7 %collective-permute-start.78 = (bf16[864,256]{1,0:T(8,128)(2,1)S(1)}, bf16[864,256]{1,0:T(8,128)(2,1)S(1)}, u32[]{:S(2)}, u32[]{:S(2)}) collective-permute-start(bf16[864,256]{1,0:T(8,128)(2,1)S(1)} %pad_maximum_fusion.34), channel_id=1, source_target_pairs={{0,2},{1,3},{2,0},{3,1},{4,6},{5,7},{6,4},{7,5},{8,10},{9,11},{10,... | collective-permute-start | bytes 1327112 | tf_op jit(solution)/shard_map/ppermute | solution.py:56
  475.2 11.5 %collective-permute-start.80 = (bf16[128,1024]{1,0:T(8,128)(2,1)S(1)}, bf16[128,1024]{1,0:T(8,128)(2,1)S(1)}, u32[]{:S(2)}, u32[]{:S(2)}) collective-permute-start(bf16[128,1024]{1,0:T(8,128)(2,1)S(1)} %slice.1781), channel_id=1, source_target_pairs={{0,1},{1,0},{2,3},{3,2},{4,5},{5,4},{6,7},{7,6},{8,9},{9,8},{10,11... | collective-permute-start | bytes 786440 | tf_op jit(solution)/shard_map/ppermute | solution.py:53
  476.0 11.5 %collective-permute-start.81 = (bf16[352,256]{1,0:T(8,128)(2,1)S(1)}, bf16[352,256]{1,0:T(8,128)(2,1)S(1)}, u32[]{:S(2)}, u32[]{:S(2)}) collective-permute-start(bf16[352,256]{1,0:T(8,128)(2,1)S(1)} %get-tuple-element.173), channel_id=1, source_target_pairs={{0,2},{1,3},{2,0},{3,1},{4,6},{5,7},{6,4},{7,5},{8,10},{9,11},{10,... | collective-permute-start | bytes 540680 | tf_op jit(solution)/shard_map/ppermute | solution.py:56
  489.5 13.2 %collective-permute-start.82 = (bf16[128,1024]{1,0:T(8,128)(2,1)S(1)}, bf16[128,1024]{1,0:T(8,128)(2,1)S(1)}, u32[]{:S(2)}, u32[]{:S(2)}) collective-permute-start(bf16[128,1024]{1,0:T(8,128)(2,1)S(1)} %constant_dynamic-update-slice_fusion.37), channel_id=1, source_target_pairs={{0,2},{1,3},{2,0},{3,1},{4,6},{5,7},{6,4},{7,5},{8,10},{9,11},{10,... | collective-permute-start | bytes 786440 | tf_op jit(solution)/shard_map/ppermute | solution.py:56
  504.4 20.8 %collective-permute-start.85 = (bf16[256,1024]{1,0:T(8,128)(2,1)S(1)}, bf16[256,1024]{1,0:T(8,128)(2,1)S(1)}, u32[]{:S(2)}, u32[]{:S(2)}) collective-permute-start(bf16[256,1024]{1,0:T(8,128)(2,1)S(1)} %pad_maximum_fusion.33), channel_id=1, source_target_pairs={{0,1},{1,0},{2,3},{3,2},{4,5},{5,4},{6,7},{7,6},{8,9},{9,8},{10,11... | collective-permute-start | bytes 1572872 | tf_op jit(solution)/shard_map/ppermute | solution.py:53
  507.8 20.7 %collective-permute-start.86 = (bf16[704,256]{1,0:T(8,128)(2,1)}, bf16[704,256]{1,0:T(8,128)(2,1)}, u32[]{:S(2)}, u32[]{:S(2)}) collective-permute-start(bf16[704,256]{1,0:T(8,128)(2,1)} %pad_maximum_fusion.44), channel_id=1, source_target_pairs={{0,2},{1,3},{2,0},{3,1},{4,6},{5,7},{6,4},{7,5},{8,10},{9,11},{10,... | collective-permute-start | bytes 1081352 | tf_op jit(solution)/shard_map/ppermute | solution.py:56
  510.5 19.9 %collective-permute-start.89 = (f32[16,256]{1,0:T(8,128)}, f32[16,256]{1,0:T(8,128)}, u32[]{:S(2)}, u32[]{:S(2)}) collective-permute-start(f32[16,256]{1,0:T(8,128)} %get-tuple-element.424), channel_id=1, source_target_pairs={{0,12},{4,8},{8,4},{12,0},{1,13},{5,9},{9,5},{13,1},{2,14},{6,10},... | collective-permute-start | bytes 49160 | tf_op jit(solution)/shard_map/ppermute | solution.py:59
  511.9 18.5 %collective-permute-start.88 = (f32[16,256]{1,0:T(8,128)S(1)}, f32[16,256]{1,0:T(8,128)}, u32[]{:S(2)}, u32[]{:S(2)}) collective-permute-start(f32[16,256]{1,0:T(8,128)S(1)} %get-tuple-element.425), channel_id=1, source_target_pairs={{0,8},{4,12},{8,0},{12,4},{1,9},{5,13},{9,1},{13,5},{2,10},{6,14},... | collective-permute-start | bytes 49160 | tf_op jit(solution)/shard_map/ppermute | solution.py:59
  512.3 18.1 %collective-permute-start.87 = (f32[16,256]{1,0:T(8,128)S(1)}, f32[16,256]{1,0:T(8,128)}, u32[]{:S(2)}, u32[]{:S(2)}) collective-permute-start(f32[16,256]{1,0:T(8,128)S(1)} %get-tuple-element.423), channel_id=1, source_target_pairs={{0,4},{4,0},{8,12},{12,8},{1,5},{5,1},{9,13},{13,9},{2,6},{6,2},{1... | collective-permute-start | bytes 49160 | tf_op jit(solution)/shard_map/ppermute | solution.py:59
  531.9 15.6 %collective-permute-start.90 = (bf16[528,256]{1,0:T(8,128)(2,1)}, bf16[528,256]{1,0:T(8,128)(2,1)}, u32[]{:S(2)}, u32[]{:S(2)}) collective-permute-start(bf16[528,256]{1,0:T(8,128)(2,1)} %pad_maximum_fusion.45), channel_id=1, source_target_pairs={{0,2},{1,3},{2,0},{3,1},{4,6},{5,7},{6,4},{7,5},{8,10},{9,11},{10,... | collective-permute-start | bytes 811016 | tf_op jit(solution)/shard_map/ppermute | solution.py:56
  532.4 17.8 %all-to-all-start = ((bf16[4,128,1024]{2,1,0:T(8,128)(2,1)}), bf16[4,128,1024]{2,1,0:T(8,128)(2,1)S(1)}, u32[]{:S(2)}, u32[]{:S(2)}) async-start(bf16[4,128,1024]{2,1,0:T(8,128)(2,1)} %bitcast.130), calls=%async_computation.3 | async-start | bytes 2097152 | tf_op jit(solution)/shard_map/all_to_all | solution.py:755
  (175 other events, 1058.1 us)
Sparse Core Ops, SparseCore 0:
  82.9 53.6 all-gather.5
  139.0 35.0 all-gather.3
  175.9 61.2 all-gather.7
  275.9 55.5 reduce-scatter.4
  354.2 32.7 reduce-scatter.6
  392.9 61.8 reduce-scatter.8
  462.7 32.5 reduce-scatter.10

commit v3 on v1

--- a/solution.py
+++ b/solution.py
@@ -422,9 +422,9 @@
     for level in range(1, LAYERS):
         own = own_columns(plan, jnp.concatenate(own_weights(level), axis=1))
         own_later.append(own)
-    cuts = [0, qkv_rows + out_rows]
-    for _ in range(3):
-        cuts.append(cuts[-1] + mlp_rows)
+    cut = qkv_rows + out_rows
+    pieces = [(cut, cut + mlp_rows), (0, cut)]
+    pieces += [(cut + i * mlp_rows, cut + (i + 1) * mlp_rows) for i in (1, 2)]
     def own_rows(array):
         mine = lax.dynamic_slice_in_dim(array, plan.part * part_rows, part_rows, 0)
         got = plan.core(
@@ -450,7 +450,7 @@
     own_rest, far_first, grad_rows = together(own_rest, far_first, grad_rows)
     out_branch = gather_rows(plan, grad_rows)
     first = jnp.concatenate([own, far_first, gain_pair], axis=0)
-    first, out_branch = together(all_columns(plan, first, True), out_branch)
+    first = all_columns(plan, first, True)
     w_qkv, gain_full = first[: 2 * qkv_rows], first[2 * qkv_rows :].astype(F32)
     last_far = plan.far(own_rest)
 
@@ -491,6 +491,8 @@
             normed = (stream * scale_attn * gain_full[level : level + 1]).astype(BF)
             normed_all = gather_rows(plan, normed)
         qkv = dot(w_qkv, normed_all, 1, 1)
+        if level + 1 < LAYERS:
+            qkv, own_later[level] = together(qkv, own_later[level])
         qkv = qkv.reshape(2, 3, 2, HEAD, tok_rows)
         query = turn(qkv[:, 0], cos_own, sine_own).astype(BF)
         key = turn(qkv[:, 1], cos_own, sine_own).astype(BF)
@@ -505,21 +507,26 @@
         far_next = []
 
         def next_far():
-            i = len(far_next)
-            piece = own_later[level][cuts[i] : cuts[i + 1]]
+            nonlocal last_far
+            start, end = pieces[len(far_next)]
+            piece = own_later[level][start:end]
             if far_next:
                 piece, far_next[-1] = together(piece, far_next[-1])
+            else:
+                piece, last_far = together(piece, last_far)
             return plan.far(piece)
 
         if level == 0:
-            heads, last_far = together(heads, last_far)
+            got = next_far()
+            heads, last_far, out_branch, got = together(heads, last_far, out_branch, got)
+            far_next.append(got)
             rest = with_far(own_rest, last_far, counts[1:])
             w_o = all_columns(plan, rest[: 2 * out_rows], True)
             rest = all_columns(plan, rest[2 * out_rows :], False)
             w_mlp = (rest[: 2 * width], rest[2 * width :])
         out, out_low, log_total = attend(where_all, first_query, heads)
         if ahead:
-            out_low, got = together(out_low, next_far())
+            out_low, got, w_o = together(out_low, next_far(), w_o)
             far_next.append(got)
         attended = from_heads(plan, [out_low[k] for k in range(4)])
         attended = attended.reshape(4 * HEAD, tok_rows)
@@ -540,12 +547,11 @@
         gate, upward = gate_up[:, :width], gate_up[:, width:]
         hidden = (gate * jax.nn.sigmoid(gate) * upward).astype(BF)
         if ahead:
-            hidden, got = together(hidden, next_far())
-            far_next.append(got)
             own = own_later[level]
-            w_attn = with_far(own[: cuts[1]], far_next[0], counts[:2])
+            w_attn = with_far(own[:cut], far_next[1], counts[:2])
             w_attn = all_columns(plan, w_attn, False)
-            rest = with_far(own[cuts[1] :], jnp.concatenate(far_next[1:], axis=0), counts[2:])
+            got = jnp.concatenate([far_next[0], far_next[2], far_next[3]], axis=0)
+            rest = with_far(own[cut:], got, counts[2:])
             rest = all_columns(plan, rest, False)
             later = (rest[: 2 * width], rest[2 * width :])
             full.append((w_attn[: 2 * qkv_rows], w_attn[2 * qkv_rows :], later))
@@ -729,15 +735,15 @@
         lax.dynamic_index_in_dim(owner_grid, plan.x, 1, False) - plan.x * tok_rows
     ).reshape(tok_rows)
     local_rows = local_rows ^ (plan.part * part_rows)
-    slots, far_e = together(to_pack(rows, other)[local_rows], far_e)
-    grad_tokens = lax.all_to_all(slots, "ctx", split_axis=0, concat_axis=0, tiled=True)
-
-    got = jnp.concatenate([far_d, far_e], axis=0).astype(F32)
-    rest = core_halves(plan, mine_first + got, counts[2:])
     gain_sum = columns_sum(plan, gain_sum + gain_near, True)
     mine, far = far_halves(sum_attn, counts[:2])
     far = jnp.concatenate([far, gain_sum.astype(BF)], axis=0)
+    slots, far_e, far = together(to_pack(rows, other)[local_rows], far_e, far)
     far = plan.far(far)
+    grad_tokens = lax.all_to_all(slots, "ctx", split_axis=0, concat_axis=0, tiled=True)
+
+    got = jnp.concatenate([far_d, far_e], axis=0).astype(F32)
+    rest = core_halves(plan, mine_first + got, counts[2:])
     grad_tokens, far = together(grad_tokens, far)
     grad_tokens = grad_tokens.astype(F32)
     total = jnp.concatenate([mine, gain_sum], axis=0) + far.astype(F32)

time: 570 us -> 562 us (0.986)
  waiting for transfers between devices: 258 us -> 241 us
  other arithmetic: 59.5 us -> 70.4 us
    all_to_all x1, waiting for transfers between devices: 9.44 us -> 0.01 us  [local(): lax.all_to_all(slots, 'ctx', split_axis=0, concat_axis=0, tiled=True)]
    reduce_scatter x4, waiting for transfers between devices: 9.78 us -> 3.19 us  [columns_sum(): return lax.psum_scatter(grad, 'ctx', scatter_dimension=1, tiled=True)]
    ppermute x14, waiting for transfers between devices: 44.5 us -> 50.7 us  [far(): return lax.ppermute(value, 'tp', [(i, i ^ 2) for i in range(self.tp)])]
    ppermute x19, waiting for transfers between devices: 113 us -> 107 us  [near(): return lax.ppermute(value, 'tp', [(i, i ^ 1) for i in range(self.tp)])]
    unnamed x261 -> x279, local copies, waits for them, and re-layouts: 28 us -> 22 us
  transfers between devices with their start and end apart: 102 -> 102, of which waited for: 60 -> 58; matrix products, arithmetic and copies ran while one was open for 23% -> 25% of each run, Pallas kernels for 6% -> 6%
where the time goes in v3:
time: 562 us; the launch traced here: 553 us
  waiting for transfers between devices  241 us (43%)
  starting transfers between devices  90.2 us (16%)
  other arithmetic  70.4 us (13%)
  local copies, waits for them, and re-layouts  60 us (11%)
  matrix products  42.3 us (8%)
  Pallas kernels  31.1 us (6%)
  between operations  17.3 us (3%)
    ppermute x19, waiting for transfers between devices, near(): return lax.ppermute(value, 'tp', [(i, i ^ 1) for i in range(self.tp)])  107 us
    ppermute x33, waiting for transfers between devices, side(): return lax.ppermute(value, 'ctx', [(i, i ^ k) for i in range(self.ctx)])  62.7 us
    ppermute x14, waiting for transfers between devices, far(): return lax.ppermute(value, 'tp', [(i, i ^ 2) for i in range(self.tp)])  50.7 us
    dot_general x24, matrix products, dot(): lax.dot_general(left, right, (((left_dim,), (right_dim,)), ((), ())), pre...  42.3 us
    ppermute x33, starting transfers between devices, side(): return lax.ppermute(value, 'ctx', [(i, i ^ k) for i in range(self.ctx)])  39.6 us
    ppermute x14, starting transfers between devices, far(): return lax.ppermute(value, 'tp', [(i, i ^ 2) for i in range(self.tp)])  23.9 us
    unnamed x279, local copies, waits for them, and re-layouts  22 us
    ppermute x28, waiting for transfers between devices, core(): return lax.ppermute(value, 'fsdp', [(i, i ^ 1) for i in range(self.fsdp)])  17.8 us
  transfers between devices with their start and end apart: 102, of which 58 were waited for; matrix products, arithmetic and copies ran while one was open for 25% of the time, Pallas kernels for 6%

profile of v3, /device:TPU:0, one launch (start us, length us, event | category | flops | bytes accessed | tf_op | source)
XLA Modules:
  0.0 552.6 jit_solution(8953481361608316736)
XLA Ops:
  20.9 3.7 collective-permute-start.3
  29.9 4.5 collective-permute-done.3
  40.4 3.4 collective-permute-start.16
  43.9 5.4 collective-permute-done.17
  50.0 5.3 collective-permute-done.7
  63.1 6.4 %collective-permute-done.16 = bf16[1184,256]{1,0:T(8,128)(2,1)S(1)} collective-permute-done((bf16[1184,256]{1,0:T(8,128)(2,1)S(1)}, bf16[1184,256]{1,0:T(8,128)(2,1)S(1)}, u32[]{:S(2)}, u32[]{:S(2)}) %collective-permute-start.16) | collective-permute-done | bytes 606240 | tf_op jit(solution)/shard_map/ppermute | solution.py:56
  71.4 7.8 %collective-permute-done.19 = bf16[352,256]{1,0:T(8,128)(2,1)S(1)} collective-permute-done((bf16[352,256]{1,0:T(8,128)(2,1)S(1)}, bf16[352,256]{1,0:T(8,128)(2,1)S(1)}, u32[]{:S(2)}, u32[]{:S(2)}) %collective-permute-start.19) | collective-permute-done | bytes 180256 | tf_op jit(solution)/shard_map/ppermute | solution.py:56
  89.5 6.7 %attend.2 = (f32[4,64,512]{2,1,0:T(8,128)}, bf16[4,64,512]{2,1,0:T(8,128)(2,1)}, f32[4,1,512]{2,1,0:T(1,128)}) custom-call(s32[6]{0:T(128)} %pad_add_fusion.2.place_ref, s32[4,1,512]{2,1,0:T(1,128)} %broadcast_in_dim.84.first_ref, bf16[3,64,512]{2,1,0:T(8,128)(2,1)} %get-tuple-element.107.refs_0_, bf16[3,64,512]{2,1,0:T(8,128)(2,1)} %copy-done.42, ...), custom_call_target="tpu_custom_call" | custom-call | tf_op jit(solution)/shard_map/attend/pallas_call | solution.py:291
  97.3 4.3 collective-permute-done.20
  111.6 4.4 collective-permute-done.27
  118.9 3.1 collective-permute-start.30
  122.0 9.0 %collective-permute-done.29 = bf16[128,1024]{1,0:T(8,128)(2,1)S(1)} collective-permute-done((bf16[128,1024]{1,0:T(8,128)(2,1)S(1)}, bf16[128,1024]{1,0:T(8,128)(2,1)S(1)}, u32[]{:S(2)}, u32[]{:S(2)}) %collective-permute-start.29) | collective-permute-done | bytes 262176 | tf_op jit(solution)/shard_map/ppermute | solution.py:53
  134.2 5.6 %collective-permute-done.31 = bf16[128,1024]{1,0:T(8,128)(2,1)} collective-permute-done((bf16[128,1024]{1,0:T(8,128)(2,1)S(1)}, bf16[128,1024]{1,0:T(8,128)(2,1)}, u32[]{:S(2)}, u32[]{:S(2)}) %collective-permute-start.31) | collective-permute-done | bytes 262176 | tf_op jit(solution)/shard_map/ppermute | solution.py:53
  142.8 3.9 fusion.6
  156.9 5.8 %collective-permute-done.34 = bf16[128,1024]{1,0:T(8,128)(2,1)} collective-permute-done((bf16[128,1024]{1,0:T(8,128)(2,1)}, bf16[128,1024]{1,0:T(8,128)(2,1)}, u32[]{:S(2)}, u32[]{:S(2)}) %collective-permute-start.34) | collective-permute-done | bytes 262176 | tf_op jit(solution)/shard_map/ppermute | solution.py:53
  166.7 6.1 %collective-permute-done.35 = bf16[128,1024]{1,0:T(8,128)(2,1)S(1)} collective-permute-done((bf16[128,1024]{1,0:T(8,128)(2,1)S(1)}, bf16[128,1024]{1,0:T(8,128)(2,1)S(1)}, u32[]{:S(2)}, u32[]{:S(2)}) %collective-permute-start.35) | collective-permute-done | bytes 262176 | tf_op jit(solution)/shard_map/ppermute | solution.py:53
  184.3 7.2 %collective-permute-done.37.refs_1_ = bf16[3,64,512]{2,1,0:T(8,128)(2,1)S(1)} collective-permute-done((bf16[3,64,512]{2,1,0:T(8,128)(2,1)S(1)}, bf16[3,64,512]{2,1,0:T(8,128)(2,1)S(1)}, u32[]{:S(2)}, u32[]{:S(2)}) %collective-permute-start.37) | collective-permute-done | bytes 196640 | tf_op jit(solution)/shard_map/ppermute | solution.py:59
  191.5 3.9 collective-permute-done.38.refs_2_
  195.4 4.6 collective-permute-done.39.refs_3_
  200.0 6.8 %attend.3 = (f32[4,64,512]{2,1,0:T(8,128)}, bf16[4,64,512]{2,1,0:T(8,128)(2,1)}, f32[4,1,512]{2,1,0:T(1,128)}) custom-call(s32[6]{0:T(128)} %pad_add_fusion.2.place_ref, s32[4,1,512]{2,1,0:T(1,128)} %broadcast_in_dim.84.first_ref, bf16[3,64,512]{2,1,0:T(8,128)(2,1)} %get-tuple-element.334.refs_0_, bf16[3,64,512]{2,1,0:T(8,128)(2,1)} %copy-done.45, ...), custom_call_target="tpu_custom_call" | custom-call | tf_op jit(solution)/shard_map/attend/pallas_call | solution.py:291
  222.7 7.3 %collective-permute-done.44 = bf16[128,1024]{1,0:T(8,128)(2,1)S(1)} collective-permute-done((bf16[128,1024]{1,0:T(8,128)(2,1)S(1)}, bf16[128,1024]{1,0:T(8,128)(2,1)S(1)}, u32[]{:S(2)}, u32[]{:S(2)}) %collective-permute-start.44) | collective-permute-done | bytes 262176 | tf_op jit(solution)/shard_map/ppermute | solution.py:53
  231.5 6.5 %collective-permute-done.45 = bf16[128,1024]{1,0:T(8,128)(2,1)S(1)} collective-permute-done((bf16[128,1024]{1,0:T(8,128)(2,1)S(1)}, bf16[128,1024]{1,0:T(8,128)(2,1)S(1)}, u32[]{:S(2)}, u32[]{:S(2)}) %collective-permute-start.45) | collective-permute-done | bytes 262176 | tf_op jit(solution)/shard_map/ppermute | solution.py:53
  241.1 4.0 fusion.2
  258.4 5.4 collective-permute-done.48
  267.7 6.7 %collective-permute-done.49 = bf16[128,1024]{1,0:T(8,128)(2,1)S(1)} collective-permute-done((bf16[128,1024]{1,0:T(8,128)(2,1)S(1)}, bf16[128,1024]{1,0:T(8,128)(2,1)S(1)}, u32[]{:S(2)}, u32[]{:S(2)}) %collective-permute-start.49) | collective-permute-done | bytes 262176 | tf_op jit(solution)/shard_map/ppermute | solution.py:53
  291.5 3.5 collective-permute-done.53.refs_7_
  302.3 8.7 %attend_back.2 = (f32[4,64,512]{2,1,0:T(8,128)}, f32[4,64,512]{2,1,0:T(8,128)}, f32[4,64,512]{2,1,0:T(8,128)}) custom-call(s32[6]{0:T(128)} %pad_add_fusion.2.place_ref, s32[4,1,512]{2,1,0:T(1,128)} %broadcast_in_dim.84.first_ref, f32[4,64,512]{2,1,0:T(8,128)} %get-tuple-element.124.out_ref, f32[4,1,512]{2,1,0:T(1,128)} %get-tuple-element.125.lse_ref, ...), custom_call_target="tpu_custom_call" | custom-call | tf_op jit(solution)/shard_map/attend_back/pallas_call | solution.py:350
  319.7 6.6 %collective-permute-done.57 = bf16[3,64,512]{2,1,0:T(8,128)(2,1)S(1)} collective-permute-done((bf16[3,64,512]{2,1,0:T(8,128)(2,1)S(1)}, bf16[3,64,512]{2,1,0:T(8,128)(2,1)S(1)}, u32[]{:S(2)}, u32[]{:S(2)}) %collective-permute-start.57) | collective-permute-done | bytes 196640 | tf_op jit(solution)/shard_map/ppermute | solution.py:59
  326.3 6.2 %collective-permute-done.58 = bf16[3,64,512]{2,1,0:T(8,128)(2,1)S(1)} collective-permute-done((bf16[3,64,512]{2,1,0:T(8,128)(2,1)S(1)}, bf16[3,64,512]{2,1,0:T(8,128)(2,1)S(1)}, u32[]{:S(2)}, u32[]{:S(2)}) %collective-permute-start.58) | collective-permute-done | bytes 196640 | tf_op jit(solution)/shard_map/ppermute | solution.py:59
  343.6 4.5 collective-permute-done.63
  352.6 7.4 %collective-permute-done.64 = bf16[128,1024]{1,0:T(8,128)(2,1)S(1)} collective-permute-done((bf16[128,1024]{1,0:T(8,128)(2,1)S(1)}, bf16[128,1024]{1,0:T(8,128)(2,1)S(1)}, u32[]{:S(2)}, u32[]{:S(2)}) %collective-permute-start.64) | collective-permute-done | bytes 262176 | tf_op jit(solution)/shard_map/ppermute | solution.py:53
  362.0 2.8 multiply_convert_fusion.1
  374.9 6.0 %collective-permute-done.67 = bf16[128,1024]{1,0:T(8,128)(2,1)S(1)} collective-permute-done((bf16[128,1024]{1,0:T(8,128)(2,1)}, bf16[128,1024]{1,0:T(8,128)(2,1)S(1)}, u32[]{:S(2)}, u32[]{:S(2)}) %collective-permute-start.67) | collective-permute-done | bytes 262176 | tf_op jit(solution)/shard_map/ppermute | solution.py:53
  386.6 6.8 %collective-permute-done.68 = bf16[128,1024]{1,0:T(8,128)(2,1)S(1)} collective-permute-done((bf16[128,1024]{1,0:T(8,128)(2,1)S(1)}, bf16[128,1024]{1,0:T(8,128)(2,1)S(1)}, u32[]{:S(2)}, u32[]{:S(2)}) %collective-permute-start.68) | collective-permute-done | bytes 262176 | tf_op jit(solution)/shard_map/ppermute | solution.py:53
  403.6 4.5 collective-permute-done.73
  409.4 2.8 collective-permute-start.74
  412.2 8.8 %attend_back.3 = (f32[4,64,512]{2,1,0:T(8,128)}, f32[4,64,512]{2,1,0:T(8,128)}, f32[4,64,512]{2,1,0:T(8,128)}) custom-call(s32[6]{0:T(128)} %pad_add_fusion.2.place_ref, s32[4,1,512]{2,1,0:T(1,128)} %broadcast_in_dim.84.first_ref, f32[4,64,512]{2,1,0:T(8,128)} %get-tuple-element.153.out_ref, f32[4,1,512]{2,1,0:T(1,128)} %get-tuple-element.154.lse_ref, ...), custom_call_target="tpu_custom_call" | custom-call | tf_op jit(solution)/shard_map/attend_back/pallas_call | solution.py:350
  429.7 6.1 %collective-permute-done.75 = bf16[3,64,512]{2,1,0:T(8,128)(2,1)S(1)} collective-permute-done((bf16[3,64,512]{2,1,0:T(8,128)(2,1)S(1)}, bf16[3,64,512]{2,1,0:T(8,128)(2,1)S(1)}, u32[]{:S(2)}, u32[]{:S(2)}) %collective-permute-start.75) | collective-permute-done | bytes 196640 | tf_op jit(solution)/shard_map/ppermute | solution.py:59
  435.8 2.8 collective-permute-done.76
  438.7 3.7 collective-permute-done.77
  443.3 3.1 reduce-scatter.9.cloned.1.call-done
  465.6 6.2 %collective-permute-done.80 = bf16[128,1024]{1,0:T(8,128)(2,1)S(1)} collective-permute-done((bf16[128,1024]{1,0:T(8,128)(2,1)S(1)}, bf16[128,1024]{1,0:T(8,128)(2,1)S(1)}, u32[]{:S(2)}, u32[]{:S(2)}) %collective-permute-start.80) | collective-permute-done | bytes 262176 | tf_op jit(solution)/shard_map/ppermute | solution.py:53
  477.1 3.2 collective-permute-done.83
  480.3 6.5 %collective-permute-done.82 = bf16[128,1024]{1,0:T(8,128)(2,1)S(1)} collective-permute-done((bf16[128,1024]{1,0:T(8,128)(2,1)S(1)}, bf16[128,1024]{1,0:T(8,128)(2,1)S(1)}, u32[]{:S(2)}, u32[]{:S(2)}) %collective-permute-start.82) | collective-permute-done | bytes 262176 | tf_op jit(solution)/shard_map/ppermute | solution.py:56
  496.6 12.3 %collective-permute-done.85 = bf16[256,1024]{1,0:T(8,128)(2,1)S(1)} collective-permute-done((bf16[256,1024]{1,0:T(8,128)(2,1)S(1)}, bf16[256,1024]{1,0:T(8,128)(2,1)S(1)}, u32[]{:S(2)}, u32[]{:S(2)}) %collective-permute-start.85) | collective-permute-done | bytes 524320 | tf_op jit(solution)/shard_map/ppermute | solution.py:53
  509.0 2.9 gather_fusion
  518.7 3.5 all-to-all-start
  526.3 11.0 %collective-permute-done.90 = bf16[528,256]{1,0:T(8,128)(2,1)} collective-permute-done((bf16[528,256]{1,0:T(8,128)(2,1)}, bf16[528,256]{1,0:T(8,128)(2,1)}, u32[]{:S(2)}, u32[]{:S(2)}) %collective-permute-start.90) | collective-permute-done | bytes 270368 | tf_op jit(solution)/shard_map/ppermute | solution.py:56
  (749 shorter events, 267.5 us)
Async XLA Ops:
  7.2 135.6 %all-gather.6.cloned.1.call-start = ((), (), s32[]{:S(2)}) async-start(), calls=%async_computation.6 | async-start | bytes 5406720 | tf_op jit(solution)/shard_map/all_gather | solution.py:139
  7.2 10.0 %collective-permute-start = (s32[1,2048]{1,0:T(1,128)}, s32[1,2048]{1,0:T(1,128)S(1)}, u32[]{:S(2)}, u32[]{:S(2)}) collective-permute-start(s32[1,2048]{1,0:T(1,128)} %param.15), channel_id=1, source_target_pairs={{0,16},{16,0},{1,17},{17,1},{2,18},{18,2},{3,19},{19,3},{4,20},{20... | collective-permute-start | bytes 24584 | tf_op jit(solution)/shard_map/ppermute | solution.py:50
  11.6 17.0 %collective-permute-start.2 = (bf16[1184,128]{1,0:T(8,128)(2,1)}, bf16[1184,128]{1,0:T(8,128)(2,1)}, u32[]{:S(2)}, u32[]{:S(2)}) collective-permute-start(bf16[1184,128]{1,0:T(8,128)(2,1)} %get-tuple-element.350), channel_id=1, source_target_pairs={{0,16},{16,0},{1,17},{17,1},{2,18},{18,2},{3,19},{19,3},{4,20},{20... | collective-permute-start | bytes 909320 | tf_op jit(solution)/shard_map/ppermute | solution.py:50
  14.2 10.3 %collective-permute-start.4 = (bf16[128,1024]{1,0:T(8,128)(2,1)S(1)}, bf16[128,1024]{1,0:T(8,128)(2,1)}, u32[]{:S(2)}, u32[]{:S(2)}) collective-permute-start(bf16[128,1024]{1,0:T(8,128)(2,1)S(1)} %constant_dynamic-slice_fusion.14), channel_id=1, source_target_pairs={{0,16},{16,0},{1,17},{17,1},{2,18},{18,2},{3,19},{19,3},{4,20},{20... | collective-permute-start | bytes 786440 | tf_op jit(solution)/shard_map/ppermute | solution.py:50
  17.2 21.0 %collective-permute-start.12 = (bf16[1568,128]{1,0:T(8,128)(2,1)}, bf16[1568,128]{1,0:T(8,128)(2,1)S(1)}, u32[]{:S(2)}, u32[]{:S(2)}) collective-permute-start(bf16[1568,128]{1,0:T(8,128)(2,1)} %get-tuple-element.330), channel_id=1, source_target_pairs={{0,16},{16,0},{1,17},{17,1},{2,18},{18,2},{3,19},{19,3},{4,20},{20... | collective-permute-start | bytes 1204232 | tf_op jit(solution)/shard_map/ppermute | solution.py:50
  20.9 13.5 %collective-permute-start.3 = (bf16[384,256]{1,0:T(8,128)(2,1)S(1)}, bf16[384,256]{1,0:T(8,128)(2,1)S(1)}, u32[]{:S(2)}, u32[]{:S(2)}) collective-permute-start(bf16[384,256]{1,0:T(8,128)(2,1)S(1)} %maximum_select_fusion.2), channel_id=1, source_target_pairs={{0,2},{1,3},{2,0},{3,1},{4,6},{5,7},{6,4},{7,5},{8,10},{9,11},{10,... | collective-permute-start | bytes 589832 | tf_op jit(solution)/shard_map/ppermute | solution.py:56
  27.0 13.4 %collective-permute-start.10 = (bf16[128,1024]{1,0:T(8,128)(2,1)S(1)}, bf16[128,1024]{1,0:T(8,128)(2,1)S(1)}, u32[]{:S(2)}, u32[]{:S(2)}) collective-permute-start(bf16[128,1024]{1,0:T(8,128)(2,1)S(1)} %constant_dynamic-update-slice_fusion.8), channel_id=1, source_target_pairs={{0,1},{1,0},{2,3},{3,2},{4,5},{5,4},{6,7},{7,6},{8,9},{9,8},{10,11... | collective-permute-start | bytes 786440 | tf_op jit(solution)/shard_map/ppermute | solution.py:53
  34.7 14.7 %collective-permute-start.6 = (bf16[784,256]{1,0:T(8,128)(2,1)S(1)}, bf16[784,256]{1,0:T(8,128)(2,1)S(1)}, u32[]{:S(2)}, u32[]{:S(2)}) collective-permute-start(bf16[784,256]{1,0:T(8,128)(2,1)S(1)} %get-tuple-element.377), channel_id=1, source_target_pairs={{0,4},{4,0},{8,12},{12,8},{1,5},{5,1},{9,13},{13,9},{2,6},{6,2},{1... | collective-permute-start | bytes 1204232 | tf_op jit(solution)/shard_map/ppermute | solution.py:59
  36.3 19.1 %collective-permute-start.7 = (bf16[784,256]{1,0:T(8,128)(2,1)S(1)}, bf16[784,256]{1,0:T(8,128)(2,1)S(1)}, u32[]{:S(2)}, u32[]{:S(2)}) collective-permute-start(bf16[784,256]{1,0:T(8,128)(2,1)S(1)} %get-tuple-element.377), channel_id=1, source_target_pairs={{0,8},{4,12},{8,0},{12,4},{1,9},{5,13},{9,1},{13,5},{2,10},{6,14},... | collective-permute-start | bytes 1204232 | tf_op jit(solution)/shard_map/ppermute | solution.py:59
  37.8 17.6 %collective-permute-start.8 = (bf16[784,256]{1,0:T(8,128)(2,1)S(1)}, bf16[784,256]{1,0:T(8,128)(2,1)S(1)}, u32[]{:S(2)}, u32[]{:S(2)}) collective-permute-start(bf16[784,256]{1,0:T(8,128)(2,1)S(1)} %get-tuple-element.377), channel_id=1, source_target_pairs={{0,12},{4,8},{8,4},{12,0},{1,13},{5,9},{9,5},{13,1},{2,14},{6,10},... | collective-permute-start | bytes 1204232 | tf_op jit(solution)/shard_map/ppermute | solution.py:59
  38.2 11.1 %collective-permute-start.17 = (bf16[128,1024]{1,0:T(8,128)(2,1)S(1)}, bf16[128,1024]{1,0:T(8,128)(2,1)S(1)}, u32[]{:S(2)}, u32[]{:S(2)}) collective-permute-start(bf16[128,1024]{1,0:T(8,128)(2,1)S(1)} %constant_dynamic-update-slice_fusion), channel_id=1, source_target_pairs={{0,1},{1,0},{2,3},{3,2},{4,5},{5,4},{6,7},{7,6},{8,9},{9,8},{10,11... | collective-permute-start | bytes 786440 | tf_op jit(solution)/shard_map/ppermute | solution.py:53
  40.4 29.2 %collective-permute-start.16 = (bf16[1184,256]{1,0:T(8,128)(2,1)S(1)}, bf16[1184,256]{1,0:T(8,128)(2,1)S(1)}, u32[]{:S(2)}, u32[]{:S(2)}) collective-permute-start(bf16[1184,256]{1,0:T(8,128)(2,1)S(1)} %maximum_select_fusion.1), channel_id=1, source_target_pairs={{0,2},{1,3},{2,0},{3,1},{4,6},{5,7},{6,4},{7,5},{8,10},{9,11},{10,... | collective-permute-start | bytes 1818632 | tf_op jit(solution)/shard_map/ppermute | solution.py:56
  49.4 21.0 %collective-permute-start.18 = (bf16[256,1024]{1,0:T(8,128)(2,1)S(1)}, bf16[256,1024]{1,0:T(8,128)(2,1)S(1)}, u32[]{:S(2)}, u32[]{:S(2)}) collective-permute-start(bf16[256,1024]{1,0:T(8,128)(2,1)S(1)} %pad_maximum_fusion.24), channel_id=1, source_target_pairs={{0,16},{16,0},{1,17},{17,1},{2,18},{18,2},{3,19},{19,3},{4,20},{20... | collective-permute-start | bytes 1572872 | tf_op jit(solution)/shard_map/ppermute | solution.py:50
  59.0 20.2 %collective-permute-start.13 = (bf16[3,64,512]{2,1,0:T(8,128)(2,1)S(1)}, bf16[3,64,512]{2,1,0:T(8,128)(2,1)S(1)}, u32[]{:S(2)}, u32[]{:S(2)}) collective-permute-start(bf16[3,64,512]{2,1,0:T(8,128)(2,1)S(1)} %get-tuple-element.337), channel_id=1, source_target_pairs={{0,4},{4,0},{8,12},{12,8},{1,5},{5,1},{9,13},{13,9},{2,6},{6,2},{1... | collective-permute-start | bytes 589832 | tf_op jit(solution)/shard_map/ppermute | solution.py:59
  60.1 19.0 %collective-permute-start.14 = (bf16[3,64,512]{2,1,0:T(8,128)(2,1)S(1)}, bf16[3,64,512]{2,1,0:T(8,128)(2,1)S(1)}, u32[]{:S(2)}, u32[]{:S(2)}) collective-permute-start(bf16[3,64,512]{2,1,0:T(8,128)(2,1)S(1)} %get-tuple-element.336), channel_id=1, source_target_pairs={{0,8},{4,12},{8,0},{12,4},{1,9},{5,13},{9,1},{13,5},{2,10},{6,14},... | collective-permute-start | bytes 589832 | tf_op jit(solution)/shard_map/ppermute | solution.py:59
  61.0 18.2 %collective-permute-start.15 = (bf16[3,64,512]{2,1,0:T(8,128)(2,1)S(1)}, bf16[3,64,512]{2,1,0:T(8,128)(2,1)S(1)}, u32[]{:S(2)}, u32[]{:S(2)}) collective-permute-start(bf16[3,64,512]{2,1,0:T(8,128)(2,1)S(1)} %get-tuple-element.335), channel_id=1, source_target_pairs={{0,12},{4,8},{8,4},{12,0},{1,13},{5,9},{9,5},{13,1},{2,14},{6,10},... | collective-permute-start | bytes 589832 | tf_op jit(solution)/shard_map/ppermute | solution.py:59
  69.6 9.6 %collective-permute-start.19 = (bf16[352,256]{1,0:T(8,128)(2,1)S(1)}, bf16[352,256]{1,0:T(8,128)(2,1)S(1)}, u32[]{:S(2)}, u32[]{:S(2)}) collective-permute-start(bf16[352,256]{1,0:T(8,128)(2,1)S(1)} %get-tuple-element.106), channel_id=1, source_target_pairs={{0,2},{1,3},{2,0},{3,1},{4,6},{5,7},{6,4},{7,5},{8,10},{9,11},{10,... | collective-permute-start | bytes 540680 | tf_op jit(solution)/shard_map/ppermute | solution.py:56
  82.8 91.0 %all-gather.4.cloned.1.call-start = ((), (), s32[]{:S(2)}) async-start(), calls=%async_computation.5 | async-start | bytes 2621440 | tf_op jit(solution)/shard_map/all_gather | solution.py:139
  84.0 12.3 %collective-permute-start.21 = (bf16[256,256]{1,0:T(8,128)(2,1)S(1)}, bf16[256,256]{1,0:T(8,128)(2,1)S(1)}, u32[]{:S(2)}, u32[]{:S(2)}) collective-permute-start(bf16[256,256]{1,0:T(8,128)(2,1)S(1)} %get-tuple-element.413), channel_id=1, source_target_pairs={{0,4},{4,0},{8,12},{12,8},{1,5},{5,1},{9,13},{13,9},{2,6},{6,2},{1... | collective-permute-start | bytes 393224 | tf_op jit(solution)/shard_map/ppermute | solution.py:59
  86.8 9.5 %collective-permute-start.22 = (bf16[256,256]{1,0:T(8,128)(2,1)S(1)}, bf16[256,256]{1,0:T(8,128)(2,1)}, u32[]{:S(2)}, u32[]{:S(2)}) collective-permute-start(bf16[256,256]{1,0:T(8,128)(2,1)S(1)} %get-tuple-element.413), channel_id=1, source_target_pairs={{0,8},{4,12},{8,0},{12,4},{1,9},{5,13},{9,1},{13,5},{2,10},{6,14},... | collective-permute-start | bytes 393224 | tf_op jit(solution)/shard_map/ppermute | solution.py:59
  88.8 12.7 %collective-permute-start.20 = (bf16[512,256]{1,0:T(8,128)(2,1)S(1)}, bf16[512,256]{1,0:T(8,128)(2,1)S(1)}, u32[]{:S(2)}, u32[]{:S(2)}) collective-permute-start(bf16[512,256]{1,0:T(8,128)(2,1)S(1)} %slice.966), channel_id=1, source_target_pairs={{0,2},{1,3},{2,0},{3,1},{4,6},{5,7},{6,4},{7,5},{8,10},{9,11},{10,... | collective-permute-start | bytes 786440 | tf_op jit(solution)/shard_map/ppermute | solution.py:56
  118.8 12.3 %collective-permute-start.29 = (bf16[128,1024]{1,0:T(8,128)(2,1)S(1)}, bf16[128,1024]{1,0:T(8,128)(2,1)S(1)}, u32[]{:S(2)}, u32[]{:S(2)}) collective-permute-start(bf16[128,1024]{1,0:T(8,128)(2,1)S(1)} %slice.1789), channel_id=1, source_target_pairs={{0,1},{1,0},{2,3},{3,2},{4,5},{5,4},{6,7},{7,6},{8,9},{9,8},{10,11... | collective-permute-start | bytes 786440 | tf_op jit(solution)/shard_map/ppermute | solution.py:53
  118.9 12.2 %collective-permute-start.30 = (bf16[352,256]{1,0:T(8,128)(2,1)S(1)}, bf16[352,256]{1,0:T(8,128)(2,1)S(1)}, u32[]{:S(2)}, u32[]{:S(2)}) collective-permute-start(bf16[352,256]{1,0:T(8,128)(2,1)S(1)} %get-tuple-element.122), channel_id=1, source_target_pairs={{0,2},{1,3},{2,0},{3,1},{4,6},{5,7},{6,4},{7,5},{8,10},{9,11},{10,... | collective-permute-start | bytes 540680 | tf_op jit(solution)/shard_map/ppermute | solution.py:56
  134.1 104.8 %all-gather.8.cloned.1.call-start = ((), (), s32[]{:S(2)}) async-start(), calls=%async_computation.7 | async-start | bytes 5406720 | tf_op jit(solution)/shard_map/all_gather | solution.py:139
  156.8 192.5 %reduce-scatter.5.cloned.1.call-start = ((), (), s32[]{:S(2)}) async-start(), calls=%async_computation.8 | async-start | bytes 5406720 | tf_op jit(solution)/shard_map/reduce_scatter | solution.py:165
  180.8 10.6 %collective-permute-start.37 = (bf16[3,64,512]{2,1,0:T(8,128)(2,1)S(1)}, bf16[3,64,512]{2,1,0:T(8,128)(2,1)S(1)}, u32[]{:S(2)}, u32[]{:S(2)}) collective-permute-start(bf16[3,64,512]{2,1,0:T(8,128)(2,1)S(1)} %get-tuple-element.333), channel_id=1, source_target_pairs={{0,4},{4,0},{8,12},{12,8},{1,5},{5,1},{9,13},{13,9},{2,6},{6,2},{1... | collective-permute-start | bytes 589832 | tf_op jit(solution)/shard_map/ppermute | solution.py:59
  182.3 13.1 %collective-permute-start.38 = (bf16[3,64,512]{2,1,0:T(8,128)(2,1)S(1)}, bf16[3,64,512]{2,1,0:T(8,128)(2,1)S(1)}, u32[]{:S(2)}, u32[]{:S(2)}) collective-permute-start(bf16[3,64,512]{2,1,0:T(8,128)(2,1)S(1)} %get-tuple-element.332), channel_id=1, source_target_pairs={{0,8},{4,12},{8,0},{12,4},{1,9},{5,13},{9,1},{13,5},{2,10},{6,14},... | collective-permute-start | bytes 589832 | tf_op jit(solution)/shard_map/ppermute | solution.py:59
  183.8 16.2 %collective-permute-start.39 = (bf16[3,64,512]{2,1,0:T(8,128)(2,1)S(1)}, bf16[3,64,512]{2,1,0:T(8,128)(2,1)}, u32[]{:S(2)}, u32[]{:S(2)}) collective-permute-start(bf16[3,64,512]{2,1,0:T(8,128)(2,1)S(1)} %get-tuple-element.331), channel_id=1, source_target_pairs={{0,12},{4,8},{8,4},{12,0},{1,13},{5,9},{9,5},{13,1},{2,14},{6,10},... | collective-permute-start | bytes 589832 | tf_op jit(solution)/shard_map/ppermute | solution.py:59
  275.2 106.9 %reduce-scatter.7.cloned.1.call-start = ((), (), s32[]{:S(2)}) async-start(), calls=%async_computation.9 | async-start | bytes 2621440 | tf_op jit(solution)/shard_map/reduce_scatter | solution.py:165
  300.0 14.4 %collective-permute-start.56 = (bf16[128,1024]{1,0:T(8,128)(2,1)}, bf16[128,1024]{1,0:T(8,128)(2,1)}, u32[]{:S(2)}, u32[]{:S(2)}) collective-permute-start(bf16[128,1024]{1,0:T(8,128)(2,1)} %constant_dynamic-update-slice_fusion.29), channel_id=1, source_target_pairs={{0,2},{1,3},{2,0},{3,1},{4,6},{5,7},{6,4},{7,5},{8,10},{9,11},{10,... | collective-permute-start | bytes 786440 | tf_op jit(solution)/shard_map/ppermute | solution.py:56
  314.5 11.7 %collective-permute-start.57 = (bf16[3,64,512]{2,1,0:T(8,128)(2,1)S(1)}, bf16[3,64,512]{2,1,0:T(8,128)(2,1)S(1)}, u32[]{:S(2)}, u32[]{:S(2)}) collective-permute-start(bf16[3,64,512]{2,1,0:T(8,128)(2,1)S(1)} %pad_maximum_fusion.51), channel_id=1, source_target_pairs={{0,4},{4,0},{8,12},{12,8},{1,5},{5,1},{9,13},{13,9},{2,6},{6,2},{1... | collective-permute-start | bytes 589832 | tf_op jit(solution)/shard_map/ppermute | solution.py:59
  316.4 16.1 %collective-permute-start.58 = (bf16[3,64,512]{2,1,0:T(8,128)(2,1)S(1)}, bf16[3,64,512]{2,1,0:T(8,128)(2,1)S(1)}, u32[]{:S(2)}, u32[]{:S(2)}) collective-permute-start(bf16[3,64,512]{2,1,0:T(8,128)(2,1)S(1)} %pad_maximum_fusion.52), channel_id=1, source_target_pairs={{0,8},{4,12},{8,0},{12,4},{1,9},{5,13},{9,1},{13,5},{2,10},{6,14},... | collective-permute-start | bytes 589832 | tf_op jit(solution)/shard_map/ppermute | solution.py:59
  316.7 15.8 %collective-permute-start.59 = (bf16[3,64,512]{2,1,0:T(8,128)(2,1)S(1)}, bf16[3,64,512]{2,1,0:T(8,128)(2,1)S(1)}, u32[]{:S(2)}, u32[]{:S(2)}) collective-permute-start(bf16[3,64,512]{2,1,0:T(8,128)(2,1)S(1)} %pad_maximum_fusion.53), channel_id=1, source_target_pairs={{0,12},{4,8},{8,4},{12,0},{1,13},{5,9},{9,5},{13,1},{2,14},{6,10},... | collective-permute-start | bytes 589832 | tf_op jit(solution)/shard_map/ppermute | solution.py:59
  319.6 13.8 %collective-permute-start.61 = (bf16[256,1024]{1,0:T(8,128)(2,1)S(1)}, bf16[256,1024]{1,0:T(8,128)(2,1)S(1)}, u32[]{:S(2)}, u32[]{:S(2)}) collective-permute-start(bf16[256,1024]{1,0:T(8,128)(2,1)S(1)} %pad_maximum_fusion.30), channel_id=1, source_target_pairs={{0,1},{1,0},{2,3},{3,2},{4,5},{5,4},{6,7},{7,6},{8,9},{9,8},{10,11... | collective-permute-start | bytes 1572872 | tf_op jit(solution)/shard_map/ppermute | solution.py:53
  343.4 103.0 %reduce-scatter.9.cloned.1.call-start = ((), (), s32[]{:S(2)}) async-start(), calls=%async_computation.10 | async-start | bytes 5406720 | tf_op jit(solution)/shard_map/reduce_scatter | solution.py:165
  382.1 129.7 %reduce-scatter.11.cloned.1.call-start = ((), (), s32[]{:S(2)}) async-start(), calls=%async_computation.11 | async-start | bytes 2621440 | tf_op jit(solution)/shard_map/reduce_scatter | solution.py:165
  396.7 11.5 %collective-permute-start.73 = (bf16[352,256]{1,0:T(8,128)(2,1)S(1)}, bf16[352,256]{1,0:T(8,128)(2,1)S(1)}, u32[]{:S(2)}, u32[]{:S(2)}) collective-permute-start(bf16[352,256]{1,0:T(8,128)(2,1)S(1)} %get-tuple-element.268), channel_id=1, source_target_pairs={{0,2},{1,3},{2,0},{3,1},{4,6},{5,7},{6,4},{7,5},{8,10},{9,11},{10,... | collective-permute-start | bytes 540680 | tf_op jit(solution)/shard_map/ppermute | solution.py:56
  409.4 14.3 %collective-permute-start.74 = (bf16[352,256]{1,0:T(8,128)(2,1)}, bf16[352,256]{1,0:T(8,128)(2,1)S(1)}, u32[]{:S(2)}, u32[]{:S(2)}) collective-permute-start(bf16[352,256]{1,0:T(8,128)(2,1)} %get-tuple-element.165), channel_id=1, source_target_pairs={{0,2},{1,3},{2,0},{3,1},{4,6},{5,7},{6,4},{7,5},{8,10},{9,11},{10,... | collective-permute-start | bytes 540680 | tf_op jit(solution)/shard_map/ppermute | solution.py:56
  423.7 12.1 %collective-permute-start.75 = (bf16[3,64,512]{2,1,0:T(8,128)(2,1)S(1)}, bf16[3,64,512]{2,1,0:T(8,128)(2,1)S(1)}, u32[]{:S(2)}, u32[]{:S(2)}) collective-permute-start(bf16[3,64,512]{2,1,0:T(8,128)(2,1)S(1)} %pad_maximum_fusion.54), channel_id=1, source_target_pairs={{0,4},{4,0},{8,12},{12,8},{1,5},{5,1},{9,13},{13,9},{2,6},{6,2},{1... | collective-permute-start | bytes 589832 | tf_op jit(solution)/shard_map/ppermute | solution.py:59
  424.5 14.2 %collective-permute-start.76 = (bf16[3,64,512]{2,1,0:T(8,128)(2,1)S(1)}, bf16[3,64,512]{2,1,0:T(8,128)(2,1)S(1)}, u32[]{:S(2)}, u32[]{:S(2)}) collective-permute-start(bf16[3,64,512]{2,1,0:T(8,128)(2,1)S(1)} %pad_maximum_fusion.55), channel_id=1, source_target_pairs={{0,8},{4,12},{8,0},{12,4},{1,9},{5,13},{9,1},{13,5},{2,10},{6,14},... | collective-permute-start | bytes 589832 | tf_op jit(solution)/shard_map/ppermute | solution.py:59
  424.9 17.4 %collective-permute-start.77 = (bf16[3,64,512]{2,1,0:T(8,128)(2,1)S(1)}, bf16[3,64,512]{2,1,0:T(8,128)(2,1)S(1)}, u32[]{:S(2)}, u32[]{:S(2)}) collective-permute-start(bf16[3,64,512]{2,1,0:T(8,128)(2,1)S(1)} %pad_maximum_fusion.56), channel_id=1, source_target_pairs={{0,12},{4,8},{8,4},{12,0},{1,13},{5,9},{9,5},{13,1},{2,14},{6,10},... | collective-permute-start | bytes 589832 | tf_op jit(solution)/shard_map/ppermute | solution.py:59
  427.5 21.1 %collective-permute-start.78 = (bf16[864,256]{1,0:T(8,128)(2,1)}, bf16[864,256]{1,0:T(8,128)(2,1)S(1)}, u32[]{:S(2)}, u32[]{:S(2)}) collective-permute-start(bf16[864,256]{1,0:T(8,128)(2,1)} %pad_maximum_fusion.34), channel_id=1, source_target_pairs={{0,2},{1,3},{2,0},{3,1},{4,6},{5,7},{6,4},{7,5},{8,10},{9,11},{10,... | collective-permute-start | bytes 1327112 | tf_op jit(solution)/shard_map/ppermute | solution.py:56
  453.4 18.5 %collective-permute-start.81 = (bf16[352,256]{1,0:T(8,128)(2,1)}, bf16[352,256]{1,0:T(8,128)(2,1)}, u32[]{:S(2)}, u32[]{:S(2)}) collective-permute-start(bf16[352,256]{1,0:T(8,128)(2,1)} %get-tuple-element.174), channel_id=1, source_target_pairs={{0,2},{1,3},{2,0},{3,1},{4,6},{5,7},{6,4},{7,5},{8,10},{9,11},{10,... | collective-permute-start | bytes 540680 | tf_op jit(solution)/shard_map/ppermute | solution.py:56
  472.5 14.3 %collective-permute-start.82 = (bf16[128,1024]{1,0:T(8,128)(2,1)S(1)}, bf16[128,1024]{1,0:T(8,128)(2,1)S(1)}, u32[]{:S(2)}, u32[]{:S(2)}) collective-permute-start(bf16[128,1024]{1,0:T(8,128)(2,1)S(1)} %constant_dynamic-update-slice_fusion.37), channel_id=1, source_target_pairs={{0,2},{1,3},{2,0},{3,1},{4,6},{5,7},{6,4},{7,5},{8,10},{9,11},{10,... | collective-permute-start | bytes 786440 | tf_op jit(solution)/shard_map/ppermute | solution.py:56
  488.5 20.4 %collective-permute-start.85 = (bf16[256,1024]{1,0:T(8,128)(2,1)S(1)}, bf16[256,1024]{1,0:T(8,128)(2,1)S(1)}, u32[]{:S(2)}, u32[]{:S(2)}) collective-permute-start(bf16[256,1024]{1,0:T(8,128)(2,1)S(1)} %pad_maximum_fusion.33), channel_id=1, source_target_pairs={{0,1},{1,0},{2,3},{3,2},{4,5},{5,4},{6,7},{7,6},{8,9},{9,8},{10,11... | collective-permute-start | bytes 1572872 | tf_op jit(solution)/shard_map/ppermute | solution.py:53
  493.4 22.5 %collective-permute-start.86 = (bf16[704,256]{1,0:T(8,128)(2,1)}, bf16[704,256]{1,0:T(8,128)(2,1)}, u32[]{:S(2)}, u32[]{:S(2)}) collective-permute-start(bf16[704,256]{1,0:T(8,128)(2,1)} %pad_maximum_fusion.44), channel_id=1, source_target_pairs={{0,2},{1,3},{2,0},{3,1},{4,6},{5,7},{6,4},{7,5},{8,10},{9,11},{10,... | collective-permute-start | bytes 1081352 | tf_op jit(solution)/shard_map/ppermute | solution.py:56
  518.7 18.7 %all-to-all-start = ((bf16[4,128,1024]{2,1,0:T(8,128)(2,1)}), bf16[4,128,1024]{2,1,0:T(8,128)(2,1)S(1)}, u32[]{:S(2)}, u32[]{:S(2)}) async-start(bf16[4,128,1024]{2,1,0:T(8,128)(2,1)} %bitcast.130), calls=%async_computation.4 | async-start | bytes 2097152 | tf_op jit(solution)/shard_map/all_to_all | solution.py:743
  522.2 15.2 %collective-permute-start.90 = (bf16[528,256]{1,0:T(8,128)(2,1)}, bf16[528,256]{1,0:T(8,128)(2,1)}, u32[]{:S(2)}, u32[]{:S(2)}) collective-permute-start(bf16[528,256]{1,0:T(8,128)(2,1)} %pad_maximum_fusion.45), channel_id=1, source_target_pairs={{0,2},{1,3},{2,0},{3,1},{4,6},{5,7},{6,4},{7,5},{8,10},{9,11},{10,... | collective-permute-start | bytes 811016 | tf_op jit(solution)/shard_map/ppermute | solution.py:56
  (173 other events, 978.2 us)
Sparse Core Ops, SparseCore 0:
  82.9 53.1 all-gather.5
  138.4 35.0 all-gather.3
  175.3 61.6 all-gather.7
  275.3 64.5 reduce-scatter.4
  343.5 35.0 reduce-scatter.6
  382.3 64.0 reduce-scatter.8
  459.7 33.3 reduce-scatter.10

commit v4 on v2

--- a/solution.py
+++ b/solution.py
@@ -713,17 +713,15 @@
         grad_qkv = from_heads(plan, grad_heads).reshape(2, 2, 3, HEAD, tok_rows)
         grad_qkv = jnp.swapaxes(grad_qkv, 1, 2).reshape(-1, tok_rows)
         if level == 0:
+            mine_first, far = far_halves(sum_mlp, counts[2:])
+            far_d, far_c = together(far[:mlp_rows], far_c)
+            far_d = plan.far(far_d)
             grad_qkv, far_c = together(grad_qkv, far_c)
         elif level == LAYERS - 1:
             grad_qkv, last = together(grad_qkv, last)
             outputs = natural_rows(plan, last)
         grad_wqkv = dot(grad_qkv, normed_all, 1, 0).astype(BF)
-        partial = dot(grad_qkv, w_qkv, 0, 0)
-        if level == 0:
-            mine_first, far = far_halves(sum_mlp, counts[2:])
-            far_d, partial = together(far[:mlp_rows], partial)
-            far_d = plan.far(far_d)
-        grad_normed = sum_rows(plan, partial)
+        grad_normed = sum_rows(plan, dot(grad_qkv, w_qkv, 0, 0))
         if level == 0:
             far_e = far[mlp_rows:]
             grad_normed, far_d, far_e = together(grad_normed, far_d, far_e)
@@ -751,15 +749,16 @@
         lax.dynamic_index_in_dim(owner_grid, plan.x, 1, False) - plan.x * tok_rows
     ).reshape(tok_rows)
     local_rows = local_rows ^ (plan.part * part_rows)
-    slots, far_e = together(to_pack(rows, other)[local_rows], far_e)
-    grad_tokens = lax.all_to_all(slots, "ctx", split_axis=0, concat_axis=0, tiled=True)
-
-    got = jnp.concatenate([far_d, far_e], axis=0).astype(F32)
-    rest = core_halves(plan, mine_first + got, counts[2:])
     gain_sum = columns_sum(plan, gain_sum + gain_near, True)
     mine, far = far_halves(sum_attn, counts[:2])
     far = jnp.concatenate([far, gain_sum.astype(BF)], axis=0)
+    block, far_e, far = together(to_pack(rows, other), far_e, far)
     far = plan.far(far)
+    slots = block[local_rows]
+    grad_tokens = lax.all_to_all(slots, "ctx", split_axis=0, concat_axis=0, tiled=True)
+
+    got = jnp.concatenate([far_d, far_e], axis=0).astype(F32)
+    rest = core_halves(plan, mine_first + got, counts[2:])
     grad_tokens, far = together(grad_tokens, far)
     grad_tokens = grad_tokens.astype(F32)
     total = jnp.concatenate([mine, gain_sum], axis=0) + far.astype(F32)

time: 575 us -> 570 us (level)
  transfers between devices with their start and end apart: 102 -> 102, of which waited for: 60 -> 58; matrix products, arithmetic and copies ran while one was open for 26% -> 25% of each run, Pallas kernels for 6% -> 6%
where the time goes in v4:
time: 570 us; the launch traced here: 561 us
  waiting for transfers between devices  243 us (43%)
  starting transfers between devices  90.7 us (16%)
  other arithmetic  70.4 us (12%)
  local copies, waits for them, and re-layouts  60.6 us (11%)
  matrix products  42.5 us (7%)
  Pallas kernels  35.8 us (6%)
  between operations  17.3 us (3%)
    ppermute x19, waiting for transfers between devices, near(): return lax.ppermute(value, 'tp', [(i, i ^ 1) for i in range(self.tp)])  113 us
    ppermute x33, waiting for transfers between devices, side(): return lax.ppermute(value, 'ctx', [(i, i ^ k) for i in range(self.ctx)])  61.2 us
    ppermute x14, waiting for transfers between devices, far(): return lax.ppermute(value, 'tp', [(i, i ^ 2) for i in range(self.tp)])  51.7 us
    dot_general x24, matrix products, dot(): lax.dot_general(left, right, (((left_dim,), (right_dim,)), ((), ())), pre...  42.5 us
    ppermute x33, starting transfers between devices, side(): return lax.ppermute(value, 'ctx', [(i, i ^ k) for i in range(self.ctx)])  39.6 us
    unnamed x283, local copies, waits for them, and re-layouts  22.1 us
    pallas_call x2, Pallas kernels, attend_back(): pl.pallas_call(functools.partial(back_kernel, count), out_shape=(jax.Shap...  20.2 us
    ppermute x28, waiting for transfers between devices, core(): return lax.ppermute(value, 'fsdp', [(i, i ^ 1) for i in range(self.fsdp)])  17.6 us
  transfers between devices with their start and end apart: 102, of which 58 were waited for; matrix products, arithmetic and copies ran while one was open for 25% of the time, Pallas kernels for 6%

profile of v4, /device:TPU:0, one launch (start us, length us, event | category | flops | bytes accessed | tf_op | source)
XLA Modules:
  0.0 560.8 jit_solution(15667266036062539690)
XLA Ops:
  20.9 3.7 collective-permute-start.3
  29.9 4.5 collective-permute-done.3
  40.4 3.4 collective-permute-start.16
  43.9 5.4 collective-permute-done.17
  50.0 5.3 collective-permute-done.7
  63.1 6.5 %collective-permute-done.16 = bf16[1184,256]{1,0:T(8,128)(2,1)S(1)} collective-permute-done((bf16[1184,256]{1,0:T(8,128)(2,1)S(1)}, bf16[1184,256]{1,0:T(8,128)(2,1)S(1)}, u32[]{:S(2)}, u32[]{:S(2)}) %collective-permute-start.16) | collective-permute-done | bytes 606240 | tf_op jit(solution)/shard_map/ppermute | solution.py:56
  71.4 7.8 %collective-permute-done.19 = bf16[352,256]{1,0:T(8,128)(2,1)S(1)} collective-permute-done((bf16[352,256]{1,0:T(8,128)(2,1)S(1)}, bf16[352,256]{1,0:T(8,128)(2,1)S(1)}, u32[]{:S(2)}, u32[]{:S(2)}) %collective-permute-start.19) | collective-permute-done | bytes 180256 | tf_op jit(solution)/shard_map/ppermute | solution.py:56
  89.6 7.9 %attend.2 = (f32[4,64,512]{2,1,0:T(8,128)}, bf16[4,64,512]{2,1,0:T(8,128)(2,1)}, f32[4,1,512]{2,1,0:T(1,128)}) custom-call(s32[6]{0:T(128)} %pad_add_fusion.2.place_ref, s32[4,1,512]{2,1,0:T(1,128)} %broadcast_in_dim.84.first_ref, bf16[3,64,512]{2,1,0:T(8,128)(2,1)} %get-tuple-element.107.refs_0_, bf16[3,64,512]{2,1,0:T(8,128)(2,1)} %copy-done.42, ...), custom_call_target="tpu_custom_call" | custom-call | tf_op jit(solution)/shard_map/attend/pallas_call | solution.py:295
  98.5 3.1 collective-permute-done.20
  111.7 4.4 collective-permute-done.27
  119.0 3.1 collective-permute-start.30
  122.1 9.0 %collective-permute-done.29 = bf16[128,1024]{1,0:T(8,128)(2,1)S(1)} collective-permute-done((bf16[128,1024]{1,0:T(8,128)(2,1)S(1)}, bf16[128,1024]{1,0:T(8,128)(2,1)S(1)}, u32[]{:S(2)}, u32[]{:S(2)}) %collective-permute-start.29) | collective-permute-done | bytes 262176 | tf_op jit(solution)/shard_map/ppermute | solution.py:53
  134.6 5.3 collective-permute-done.31
  143.0 3.9 fusion.6
  157.0 5.8 %collective-permute-done.34 = bf16[128,1024]{1,0:T(8,128)(2,1)} collective-permute-done((bf16[128,1024]{1,0:T(8,128)(2,1)}, bf16[128,1024]{1,0:T(8,128)(2,1)}, u32[]{:S(2)}, u32[]{:S(2)}) %collective-permute-start.34) | collective-permute-done | bytes 262176 | tf_op jit(solution)/shard_map/ppermute | solution.py:53
  166.9 6.1 %collective-permute-done.35 = bf16[128,1024]{1,0:T(8,128)(2,1)S(1)} collective-permute-done((bf16[128,1024]{1,0:T(8,128)(2,1)S(1)}, bf16[128,1024]{1,0:T(8,128)(2,1)S(1)}, u32[]{:S(2)}, u32[]{:S(2)}) %collective-permute-start.35) | collective-permute-done | bytes 262176 | tf_op jit(solution)/shard_map/ppermute | solution.py:53
  184.4 6.7 %collective-permute-done.37.refs_1_ = bf16[3,64,512]{2,1,0:T(8,128)(2,1)S(1)} collective-permute-done((bf16[3,64,512]{2,1,0:T(8,128)(2,1)S(1)}, bf16[3,64,512]{2,1,0:T(8,128)(2,1)S(1)}, u32[]{:S(2)}, u32[]{:S(2)}) %collective-permute-start.37) | collective-permute-done | bytes 196640 | tf_op jit(solution)/shard_map/ppermute | solution.py:59
  191.1 4.3 collective-permute-done.38.refs_2_
  195.5 4.1 collective-permute-done.39.refs_3_
  199.6 7.8 %attend.3 = (f32[4,64,512]{2,1,0:T(8,128)}, bf16[4,64,512]{2,1,0:T(8,128)(2,1)}, f32[4,1,512]{2,1,0:T(1,128)}) custom-call(s32[6]{0:T(128)} %pad_add_fusion.2.place_ref, s32[4,1,512]{2,1,0:T(1,128)} %broadcast_in_dim.84.first_ref, bf16[3,64,512]{2,1,0:T(8,128)(2,1)} %get-tuple-element.334.refs_0_, bf16[3,64,512]{2,1,0:T(8,128)(2,1)} %copy-done.45, ...), custom_call_target="tpu_custom_call" | custom-call | tf_op jit(solution)/shard_map/attend/pallas_call | solution.py:295
  223.3 7.3 %collective-permute-done.44 = bf16[128,1024]{1,0:T(8,128)(2,1)S(1)} collective-permute-done((bf16[128,1024]{1,0:T(8,128)(2,1)S(1)}, bf16[128,1024]{1,0:T(8,128)(2,1)S(1)}, u32[]{:S(2)}, u32[]{:S(2)}) %collective-permute-start.44) | collective-permute-done | bytes 262176 | tf_op jit(solution)/shard_map/ppermute | solution.py:53
  232.1 6.5 %collective-permute-done.45 = bf16[128,1024]{1,0:T(8,128)(2,1)S(1)} collective-permute-done((bf16[128,1024]{1,0:T(8,128)(2,1)S(1)}, bf16[128,1024]{1,0:T(8,128)(2,1)S(1)}, u32[]{:S(2)}, u32[]{:S(2)}) %collective-permute-start.45) | collective-permute-done | bytes 262176 | tf_op jit(solution)/shard_map/ppermute | solution.py:53
  241.7 4.0 fusion.2
  258.9 5.4 collective-permute-done.48
  268.2 6.7 %collective-permute-done.49 = bf16[128,1024]{1,0:T(8,128)(2,1)S(1)} collective-permute-done((bf16[128,1024]{1,0:T(8,128)(2,1)S(1)}, bf16[128,1024]{1,0:T(8,128)(2,1)S(1)}, u32[]{:S(2)}, u32[]{:S(2)}) %collective-permute-start.49) | collective-permute-done | bytes 262176 | tf_op jit(solution)/shard_map/ppermute | solution.py:53
  275.8 10.2 %reduce-scatter.7.cloned.1.call-start = ((), (), s32[]{:S(2)}) async-start(), calls=%async_computation.9 | async-start | bytes 2621440 | tf_op jit(solution)/shard_map/reduce_scatter | solution.py:165
  302.2 3.5 collective-permute-done.53.refs_7_
  310.8 10.1 %attend_back.2 = (f32[4,64,512]{2,1,0:T(8,128)}, f32[4,64,512]{2,1,0:T(8,128)}, f32[4,64,512]{2,1,0:T(8,128)}) custom-call(s32[6]{0:T(128)} %pad_add_fusion.2.place_ref, s32[4,1,512]{2,1,0:T(1,128)} %broadcast_in_dim.84.first_ref, f32[4,64,512]{2,1,0:T(8,128)} %get-tuple-element.124.out_ref, f32[4,1,512]{2,1,0:T(1,128)} %get-tuple-element.125.lse_ref, ...), custom_call_target="tpu_custom_call" | custom-call | tf_op jit(solution)/shard_map/attend_back/pallas_call | solution.py:362
  327.3 2.9 collective-permute-start.59
  330.5 3.0 collective-permute-done.57
  333.5 5.2 collective-permute-done.58
  338.9 5.3 collective-permute-done.61
  354.2 4.8 collective-permute-done.63
  363.4 7.1 %collective-permute-done.64 = bf16[128,1024]{1,0:T(8,128)(2,1)S(1)} collective-permute-done((bf16[128,1024]{1,0:T(8,128)(2,1)S(1)}, bf16[128,1024]{1,0:T(8,128)(2,1)S(1)}, u32[]{:S(2)}, u32[]{:S(2)}) %collective-permute-start.64) | collective-permute-done | bytes 262176 | tf_op jit(solution)/shard_map/ppermute | solution.py:53
  372.6 2.9 multiply_convert_fusion.1
  379.0 2.8 convolution_convert_fusion
  385.8 5.8 %collective-permute-done.67 = bf16[128,1024]{1,0:T(8,128)(2,1)S(1)} collective-permute-done((bf16[128,1024]{1,0:T(8,128)(2,1)}, bf16[128,1024]{1,0:T(8,128)(2,1)S(1)}, u32[]{:S(2)}, u32[]{:S(2)}) %collective-permute-start.67) | collective-permute-done | bytes 262176 | tf_op jit(solution)/shard_map/ppermute | solution.py:53
  397.6 6.8 %collective-permute-done.68 = bf16[128,1024]{1,0:T(8,128)(2,1)S(1)} collective-permute-done((bf16[128,1024]{1,0:T(8,128)(2,1)S(1)}, bf16[128,1024]{1,0:T(8,128)(2,1)S(1)}, u32[]{:S(2)}, u32[]{:S(2)}) %collective-permute-start.68) | collective-permute-done | bytes 262176 | tf_op jit(solution)/shard_map/ppermute | solution.py:53
  413.6 5.5 collective-permute-done.73
  420.9 10.1 %attend_back.3 = (f32[4,64,512]{2,1,0:T(8,128)}, f32[4,64,512]{2,1,0:T(8,128)}, f32[4,64,512]{2,1,0:T(8,128)}) custom-call(s32[6]{0:T(128)} %pad_add_fusion.2.place_ref, s32[4,1,512]{2,1,0:T(1,128)} %broadcast_in_dim.84.first_ref, f32[4,64,512]{2,1,0:T(8,128)} %get-tuple-element.153.out_ref, f32[4,1,512]{2,1,0:T(1,128)} %get-tuple-element.154.lse_ref, ...), custom_call_target="tpu_custom_call" | custom-call | tf_op jit(solution)/shard_map/attend_back/pallas_call | solution.py:362
  437.5 8.2 %collective-permute-done.75 = bf16[3,64,512]{2,1,0:T(8,128)(2,1)S(1)} collective-permute-done((bf16[3,64,512]{2,1,0:T(8,128)(2,1)S(1)}, bf16[3,64,512]{2,1,0:T(8,128)(2,1)S(1)}, u32[]{:S(2)}, u32[]{:S(2)}) %collective-permute-start.75) | collective-permute-done | bytes 196640 | tf_op jit(solution)/shard_map/ppermute | solution.py:59
  446.4 7.8 %collective-permute-done.77 = bf16[3,64,512]{2,1,0:T(8,128)(2,1)S(1)} collective-permute-done((bf16[3,64,512]{2,1,0:T(8,128)(2,1)S(1)}, bf16[3,64,512]{2,1,0:T(8,128)(2,1)S(1)}, u32[]{:S(2)}, u32[]{:S(2)}) %collective-permute-start.77) | collective-permute-done | bytes 196640 | tf_op jit(solution)/shard_map/ppermute | solution.py:59
  473.2 7.1 %collective-permute-done.80 = bf16[128,1024]{1,0:T(8,128)(2,1)S(1)} collective-permute-done((bf16[128,1024]{1,0:T(8,128)(2,1)S(1)}, bf16[128,1024]{1,0:T(8,128)(2,1)S(1)}, u32[]{:S(2)}, u32[]{:S(2)}) %collective-permute-start.80) | collective-permute-done | bytes 262176 | tf_op jit(solution)/shard_map/ppermute | solution.py:53
  484.6 4.7 collective-permute-done.83
  489.4 5.8 %collective-permute-done.82 = bf16[128,1024]{1,0:T(8,128)(2,1)S(1)} collective-permute-done((bf16[128,1024]{1,0:T(8,128)(2,1)S(1)}, bf16[128,1024]{1,0:T(8,128)(2,1)S(1)}, u32[]{:S(2)}, u32[]{:S(2)}) %collective-permute-start.82) | collective-permute-done | bytes 262176 | tf_op jit(solution)/shard_map/ppermute | solution.py:56
  505.0 11.8 %collective-permute-done.85 = bf16[256,1024]{1,0:T(8,128)(2,1)S(1)} collective-permute-done((bf16[256,1024]{1,0:T(8,128)(2,1)S(1)}, bf16[256,1024]{1,0:T(8,128)(2,1)S(1)}, u32[]{:S(2)}, u32[]{:S(2)}) %collective-permute-start.85) | collective-permute-done | bytes 524320 | tf_op jit(solution)/shard_map/ppermute | solution.py:53
  526.6 3.5 all-to-all-start
  534.5 11.1 %collective-permute-done.90 = bf16[528,256]{1,0:T(8,128)(2,1)} collective-permute-done((bf16[528,256]{1,0:T(8,128)(2,1)}, bf16[528,256]{1,0:T(8,128)(2,1)}, u32[]{:S(2)}, u32[]{:S(2)}) %collective-permute-start.90) | collective-permute-done | bytes 270368 | tf_op jit(solution)/shard_map/ppermute | solution.py:56
  (753 shorter events, 259.4 us)
Async XLA Ops:
  7.2 135.8 %all-gather.6.cloned.1.call-start = ((), (), s32[]{:S(2)}) async-start(), calls=%async_computation.6 | async-start | bytes 5406720 | tf_op jit(solution)/shard_map/all_gather | solution.py:139
  7.2 10.0 %collective-permute-start = (s32[1,2048]{1,0:T(1,128)}, s32[1,2048]{1,0:T(1,128)S(1)}, u32[]{:S(2)}, u32[]{:S(2)}) collective-permute-start(s32[1,2048]{1,0:T(1,128)} %param.15), channel_id=1, source_target_pairs={{0,16},{16,0},{1,17},{17,1},{2,18},{18,2},{3,19},{19,3},{4,20},{20... | collective-permute-start | bytes 24584 | tf_op jit(solution)/shard_map/ppermute | solution.py:50
  11.6 17.0 %collective-permute-start.2 = (bf16[1184,128]{1,0:T(8,128)(2,1)}, bf16[1184,128]{1,0:T(8,128)(2,1)}, u32[]{:S(2)}, u32[]{:S(2)}) collective-permute-start(bf16[1184,128]{1,0:T(8,128)(2,1)} %get-tuple-element.350), channel_id=1, source_target_pairs={{0,16},{16,0},{1,17},{17,1},{2,18},{18,2},{3,19},{19,3},{4,20},{20... | collective-permute-start | bytes 909320 | tf_op jit(solution)/shard_map/ppermute | solution.py:50
  14.2 10.3 %collective-permute-start.4 = (bf16[128,1024]{1,0:T(8,128)(2,1)S(1)}, bf16[128,1024]{1,0:T(8,128)(2,1)}, u32[]{:S(2)}, u32[]{:S(2)}) collective-permute-start(bf16[128,1024]{1,0:T(8,128)(2,1)S(1)} %constant_dynamic-slice_fusion.14), channel_id=1, source_target_pairs={{0,16},{16,0},{1,17},{17,1},{2,18},{18,2},{3,19},{19,3},{4,20},{20... | collective-permute-start | bytes 786440 | tf_op jit(solution)/shard_map/ppermute | solution.py:50
  17.2 21.0 %collective-permute-start.12 = (bf16[1568,128]{1,0:T(8,128)(2,1)}, bf16[1568,128]{1,0:T(8,128)(2,1)S(1)}, u32[]{:S(2)}, u32[]{:S(2)}) collective-permute-start(bf16[1568,128]{1,0:T(8,128)(2,1)} %get-tuple-element.330), channel_id=1, source_target_pairs={{0,16},{16,0},{1,17},{17,1},{2,18},{18,2},{3,19},{19,3},{4,20},{20... | collective-permute-start | bytes 1204232 | tf_op jit(solution)/shard_map/ppermute | solution.py:50
  20.9 13.5 %collective-permute-start.3 = (bf16[384,256]{1,0:T(8,128)(2,1)S(1)}, bf16[384,256]{1,0:T(8,128)(2,1)S(1)}, u32[]{:S(2)}, u32[]{:S(2)}) collective-permute-start(bf16[384,256]{1,0:T(8,128)(2,1)S(1)} %maximum_select_fusion.2), channel_id=1, source_target_pairs={{0,2},{1,3},{2,0},{3,1},{4,6},{5,7},{6,4},{7,5},{8,10},{9,11},{10,... | collective-permute-start | bytes 589832 | tf_op jit(solution)/shard_map/ppermute | solution.py:56
  27.0 13.4 %collective-permute-start.10 = (bf16[128,1024]{1,0:T(8,128)(2,1)S(1)}, bf16[128,1024]{1,0:T(8,128)(2,1)S(1)}, u32[]{:S(2)}, u32[]{:S(2)}) collective-permute-start(bf16[128,1024]{1,0:T(8,128)(2,1)S(1)} %constant_dynamic-update-slice_fusion.8), channel_id=1, source_target_pairs={{0,1},{1,0},{2,3},{3,2},{4,5},{5,4},{6,7},{7,6},{8,9},{9,8},{10,11... | collective-permute-start | bytes 786440 | tf_op jit(solution)/shard_map/ppermute | solution.py:53
  34.7 14.7 %collective-permute-start.6 = (bf16[784,256]{1,0:T(8,128)(2,1)S(1)}, bf16[784,256]{1,0:T(8,128)(2,1)S(1)}, u32[]{:S(2)}, u32[]{:S(2)}) collective-permute-start(bf16[784,256]{1,0:T(8,128)(2,1)S(1)} %get-tuple-element.377), channel_id=1, source_target_pairs={{0,4},{4,0},{8,12},{12,8},{1,5},{5,1},{9,13},{13,9},{2,6},{6,2},{1... | collective-permute-start | bytes 1204232 | tf_op jit(solution)/shard_map/ppermute | solution.py:59
  36.3 19.1 %collective-permute-start.7 = (bf16[784,256]{1,0:T(8,128)(2,1)S(1)}, bf16[784,256]{1,0:T(8,128)(2,1)S(1)}, u32[]{:S(2)}, u32[]{:S(2)}) collective-permute-start(bf16[784,256]{1,0:T(8,128)(2,1)S(1)} %get-tuple-element.377), channel_id=1, source_target_pairs={{0,8},{4,12},{8,0},{12,4},{1,9},{5,13},{9,1},{13,5},{2,10},{6,14},... | collective-permute-start | bytes 1204232 | tf_op jit(solution)/shard_map/ppermute | solution.py:59
  37.8 17.6 %collective-permute-start.8 = (bf16[784,256]{1,0:T(8,128)(2,1)S(1)}, bf16[784,256]{1,0:T(8,128)(2,1)S(1)}, u32[]{:S(2)}, u32[]{:S(2)}) collective-permute-start(bf16[784,256]{1,0:T(8,128)(2,1)S(1)} %get-tuple-element.377), channel_id=1, source_target_pairs={{0,12},{4,8},{8,4},{12,0},{1,13},{5,9},{9,5},{13,1},{2,14},{6,10},... | collective-permute-start | bytes 1204232 | tf_op jit(solution)/shard_map/ppermute | solution.py:59
  38.2 11.1 %collective-permute-start.17 = (bf16[128,1024]{1,0:T(8,128)(2,1)S(1)}, bf16[128,1024]{1,0:T(8,128)(2,1)S(1)}, u32[]{:S(2)}, u32[]{:S(2)}) collective-permute-start(bf16[128,1024]{1,0:T(8,128)(2,1)S(1)} %constant_dynamic-update-slice_fusion), channel_id=1, source_target_pairs={{0,1},{1,0},{2,3},{3,2},{4,5},{5,4},{6,7},{7,6},{8,9},{9,8},{10,11... | collective-permute-start | bytes 786440 | tf_op jit(solution)/shard_map/ppermute | solution.py:53
  40.4 29.2 %collective-permute-start.16 = (bf16[1184,256]{1,0:T(8,128)(2,1)S(1)}, bf16[1184,256]{1,0:T(8,128)(2,1)S(1)}, u32[]{:S(2)}, u32[]{:S(2)}) collective-permute-start(bf16[1184,256]{1,0:T(8,128)(2,1)S(1)} %maximum_select_fusion.1), channel_id=1, source_target_pairs={{0,2},{1,3},{2,0},{3,1},{4,6},{5,7},{6,4},{7,5},{8,10},{9,11},{10,... | collective-permute-start | bytes 1818632 | tf_op jit(solution)/shard_map/ppermute | solution.py:56
  49.4 21.0 %collective-permute-start.18 = (bf16[256,1024]{1,0:T(8,128)(2,1)S(1)}, bf16[256,1024]{1,0:T(8,128)(2,1)S(1)}, u32[]{:S(2)}, u32[]{:S(2)}) collective-permute-start(bf16[256,1024]{1,0:T(8,128)(2,1)S(1)} %pad_maximum_fusion.24), channel_id=1, source_target_pairs={{0,16},{16,0},{1,17},{17,1},{2,18},{18,2},{3,19},{19,3},{4,20},{20... | collective-permute-start | bytes 1572872 | tf_op jit(solution)/shard_map/ppermute | solution.py:50
  59.0 20.2 %collective-permute-start.13 = (bf16[3,64,512]{2,1,0:T(8,128)(2,1)S(1)}, bf16[3,64,512]{2,1,0:T(8,128)(2,1)S(1)}, u32[]{:S(2)}, u32[]{:S(2)}) collective-permute-start(bf16[3,64,512]{2,1,0:T(8,128)(2,1)S(1)} %get-tuple-element.337), channel_id=1, source_target_pairs={{0,4},{4,0},{8,12},{12,8},{1,5},{5,1},{9,13},{13,9},{2,6},{6,2},{1... | collective-permute-start | bytes 589832 | tf_op jit(solution)/shard_map/ppermute | solution.py:59
  60.1 19.1 %collective-permute-start.14 = (bf16[3,64,512]{2,1,0:T(8,128)(2,1)S(1)}, bf16[3,64,512]{2,1,0:T(8,128)(2,1)S(1)}, u32[]{:S(2)}, u32[]{:S(2)}) collective-permute-start(bf16[3,64,512]{2,1,0:T(8,128)(2,1)S(1)} %get-tuple-element.336), channel_id=1, source_target_pairs={{0,8},{4,12},{8,0},{12,4},{1,9},{5,13},{9,1},{13,5},{2,10},{6,14},... | collective-permute-start | bytes 589832 | tf_op jit(solution)/shard_map/ppermute | solution.py:59
  61.0 18.2 %collective-permute-start.15 = (bf16[3,64,512]{2,1,0:T(8,128)(2,1)S(1)}, bf16[3,64,512]{2,1,0:T(8,128)(2,1)S(1)}, u32[]{:S(2)}, u32[]{:S(2)}) collective-permute-start(bf16[3,64,512]{2,1,0:T(8,128)(2,1)S(1)} %get-tuple-element.335), channel_id=1, source_target_pairs={{0,12},{4,8},{8,4},{12,0},{1,13},{5,9},{9,5},{13,1},{2,14},{6,10},... | collective-permute-start | bytes 589832 | tf_op jit(solution)/shard_map/ppermute | solution.py:59
  82.8 91.3 %all-gather.4.cloned.1.call-start = ((), (), s32[]{:S(2)}) async-start(), calls=%async_computation.5 | async-start | bytes 2621440 | tf_op jit(solution)/shard_map/all_gather | solution.py:139
  84.0 13.5 %collective-permute-start.21 = (bf16[256,256]{1,0:T(8,128)(2,1)S(1)}, bf16[256,256]{1,0:T(8,128)(2,1)S(1)}, u32[]{:S(2)}, u32[]{:S(2)}) collective-permute-start(bf16[256,256]{1,0:T(8,128)(2,1)S(1)} %get-tuple-element.413), channel_id=1, source_target_pairs={{0,4},{4,0},{8,12},{12,8},{1,5},{5,1},{9,13},{13,9},{2,6},{6,2},{1... | collective-permute-start | bytes 393224 | tf_op jit(solution)/shard_map/ppermute | solution.py:59
  86.9 10.7 %collective-permute-start.22 = (bf16[256,256]{1,0:T(8,128)(2,1)S(1)}, bf16[256,256]{1,0:T(8,128)(2,1)}, u32[]{:S(2)}, u32[]{:S(2)}) collective-permute-start(bf16[256,256]{1,0:T(8,128)(2,1)S(1)} %get-tuple-element.413), channel_id=1, source_target_pairs={{0,8},{4,12},{8,0},{12,4},{1,9},{5,13},{9,1},{13,5},{2,10},{6,14},... | collective-permute-start | bytes 393224 | tf_op jit(solution)/shard_map/ppermute | solution.py:59
  88.5 10.0 %collective-permute-start.23 = (bf16[256,256]{1,0:T(8,128)(2,1)S(1)}, bf16[256,256]{1,0:T(8,128)(2,1)S(1)}, u32[]{:S(2)}, u32[]{:S(2)}) collective-permute-start(bf16[256,256]{1,0:T(8,128)(2,1)S(1)} %get-tuple-element.413), channel_id=1, source_target_pairs={{0,12},{4,8},{8,4},{12,0},{1,13},{5,9},{9,5},{13,1},{2,14},{6,10},... | collective-permute-start | bytes 393224 | tf_op jit(solution)/shard_map/ppermute | solution.py:59
  89.0 12.7 %collective-permute-start.20 = (bf16[512,256]{1,0:T(8,128)(2,1)S(1)}, bf16[512,256]{1,0:T(8,128)(2,1)S(1)}, u32[]{:S(2)}, u32[]{:S(2)}) collective-permute-start(bf16[512,256]{1,0:T(8,128)(2,1)S(1)} %slice.966), channel_id=1, source_target_pairs={{0,2},{1,3},{2,0},{3,1},{4,6},{5,7},{6,4},{7,5},{8,10},{9,11},{10,... | collective-permute-start | bytes 786440 | tf_op jit(solution)/shard_map/ppermute | solution.py:56
  118.9 12.3 %collective-permute-start.29 = (bf16[128,1024]{1,0:T(8,128)(2,1)S(1)}, bf16[128,1024]{1,0:T(8,128)(2,1)S(1)}, u32[]{:S(2)}, u32[]{:S(2)}) collective-permute-start(bf16[128,1024]{1,0:T(8,128)(2,1)S(1)} %slice.1789), channel_id=1, source_target_pairs={{0,1},{1,0},{2,3},{3,2},{4,5},{5,4},{6,7},{7,6},{8,9},{9,8},{10,11... | collective-permute-start | bytes 786440 | tf_op jit(solution)/shard_map/ppermute | solution.py:53
  119.0 12.2 %collective-permute-start.30 = (bf16[352,256]{1,0:T(8,128)(2,1)S(1)}, bf16[352,256]{1,0:T(8,128)(2,1)S(1)}, u32[]{:S(2)}, u32[]{:S(2)}) collective-permute-start(bf16[352,256]{1,0:T(8,128)(2,1)S(1)} %get-tuple-element.122), channel_id=1, source_target_pairs={{0,2},{1,3},{2,0},{3,1},{4,6},{5,7},{6,4},{7,5},{8,10},{9,11},{10,... | collective-permute-start | bytes 540680 | tf_op jit(solution)/shard_map/ppermute | solution.py:56
  134.3 105.2 %all-gather.8.cloned.1.call-start = ((), (), s32[]{:S(2)}) async-start(), calls=%async_computation.7 | async-start | bytes 5406720 | tf_op jit(solution)/shard_map/all_gather | solution.py:139
  157.0 203.1 %reduce-scatter.5.cloned.1.call-start = ((), (), s32[]{:S(2)}) async-start(), calls=%async_computation.8 | async-start | bytes 5406720 | tf_op jit(solution)/shard_map/reduce_scatter | solution.py:165
  180.9 10.2 %collective-permute-start.37 = (bf16[3,64,512]{2,1,0:T(8,128)(2,1)S(1)}, bf16[3,64,512]{2,1,0:T(8,128)(2,1)S(1)}, u32[]{:S(2)}, u32[]{:S(2)}) collective-permute-start(bf16[3,64,512]{2,1,0:T(8,128)(2,1)S(1)} %get-tuple-element.333), channel_id=1, source_target_pairs={{0,4},{4,0},{8,12},{12,8},{1,5},{5,1},{9,13},{13,9},{2,6},{6,2},{1... | collective-permute-start | bytes 589832 | tf_op jit(solution)/shard_map/ppermute | solution.py:59
  182.4 13.1 %collective-permute-start.38 = (bf16[3,64,512]{2,1,0:T(8,128)(2,1)S(1)}, bf16[3,64,512]{2,1,0:T(8,128)(2,1)S(1)}, u32[]{:S(2)}, u32[]{:S(2)}) collective-permute-start(bf16[3,64,512]{2,1,0:T(8,128)(2,1)S(1)} %get-tuple-element.332), channel_id=1, source_target_pairs={{0,8},{4,12},{8,0},{12,4},{1,9},{5,13},{9,1},{13,5},{2,10},{6,14},... | collective-permute-start | bytes 589832 | tf_op jit(solution)/shard_map/ppermute | solution.py:59
  183.9 15.7 %collective-permute-start.39 = (bf16[3,64,512]{2,1,0:T(8,128)(2,1)S(1)}, bf16[3,64,512]{2,1,0:T(8,128)(2,1)}, u32[]{:S(2)}, u32[]{:S(2)}) collective-permute-start(bf16[3,64,512]{2,1,0:T(8,128)(2,1)S(1)} %get-tuple-element.331), channel_id=1, source_target_pairs={{0,12},{4,8},{8,4},{12,0},{1,13},{5,9},{9,5},{13,1},{2,14},{6,10},... | collective-permute-start | bytes 589832 | tf_op jit(solution)/shard_map/ppermute | solution.py:59
  275.8 13.1 %collective-permute-start.50 = (bf16[256,1024]{1,0:T(8,128)(2,1)}, bf16[256,1024]{1,0:T(8,128)(2,1)}, u32[]{:S(2)}, u32[]{:S(2)}) collective-permute-start(bf16[256,1024]{1,0:T(8,128)(2,1)} %pad_maximum_fusion.29), channel_id=1, source_target_pairs={{0,16},{16,0},{1,17},{17,1},{2,18},{18,2},{3,19},{19,3},{4,20},{20... | collective-permute-start | bytes 1572872 | tf_op jit(solution)/shard_map/ppermute | solution.py:50
  275.8 116.9 %reduce-scatter.7.cloned.1.call-start = ((), (), s32[]{:S(2)}) async-start(), calls=%async_computation.9 | async-start | bytes 2621440 | tf_op jit(solution)/shard_map/reduce_scatter | solution.py:165
  310.8 14.4 %collective-permute-start.56 = (bf16[128,1024]{1,0:T(8,128)(2,1)}, bf16[128,1024]{1,0:T(8,128)(2,1)}, u32[]{:S(2)}, u32[]{:S(2)}) collective-permute-start(bf16[128,1024]{1,0:T(8,128)(2,1)} %constant_dynamic-update-slice_fusion.29), channel_id=1, source_target_pairs={{0,2},{1,3},{2,0},{3,1},{4,6},{5,7},{6,4},{7,5},{8,10},{9,11},{10,... | collective-permute-start | bytes 786440 | tf_op jit(solution)/shard_map/ppermute | solution.py:56
  327.2 11.6 %collective-permute-start.58 = (bf16[3,64,512]{2,1,0:T(8,128)(2,1)S(1)}, bf16[3,64,512]{2,1,0:T(8,128)(2,1)S(1)}, u32[]{:S(2)}, u32[]{:S(2)}) collective-permute-start(bf16[3,64,512]{2,1,0:T(8,128)(2,1)S(1)} %pad_maximum_fusion.52), channel_id=1, source_target_pairs={{0,8},{4,12},{8,0},{12,4},{1,9},{5,13},{9,1},{13,5},{2,10},{6,14},... | collective-permute-start | bytes 589832 | tf_op jit(solution)/shard_map/ppermute | solution.py:59
  327.3 11.4 %collective-permute-start.59 = (bf16[3,64,512]{2,1,0:T(8,128)(2,1)S(1)}, bf16[3,64,512]{2,1,0:T(8,128)(2,1)S(1)}, u32[]{:S(2)}, u32[]{:S(2)}) collective-permute-start(bf16[3,64,512]{2,1,0:T(8,128)(2,1)S(1)} %pad_maximum_fusion.53), channel_id=1, source_target_pairs={{0,12},{4,8},{8,4},{12,0},{1,13},{5,9},{9,5},{13,1},{2,14},{6,10},... | collective-permute-start | bytes 589832 | tf_op jit(solution)/shard_map/ppermute | solution.py:59
  330.4 13.8 %collective-permute-start.61 = (bf16[256,1024]{1,0:T(8,128)(2,1)S(1)}, bf16[256,1024]{1,0:T(8,128)(2,1)S(1)}, u32[]{:S(2)}, u32[]{:S(2)}) collective-permute-start(bf16[256,1024]{1,0:T(8,128)(2,1)S(1)} %pad_maximum_fusion.30), channel_id=1, source_target_pairs={{0,1},{1,0},{2,3},{3,2},{4,5},{5,4},{6,7},{7,6},{8,9},{9,8},{10,11... | collective-permute-start | bytes 1572872 | tf_op jit(solution)/shard_map/ppermute | solution.py:53
  354.1 101.0 %reduce-scatter.9.cloned.1.call-start = ((), (), s32[]{:S(2)}) async-start(), calls=%async_computation.10 | async-start | bytes 5406720 | tf_op jit(solution)/shard_map/reduce_scatter | solution.py:165
  392.8 124.1 %reduce-scatter.11.cloned.1.call-start = ((), (), s32[]{:S(2)}) async-start(), calls=%async_computation.11 | async-start | bytes 2621440 | tf_op jit(solution)/shard_map/reduce_scatter | solution.py:165
  407.7 11.4 %collective-permute-start.73 = (bf16[352,256]{1,0:T(8,128)(2,1)S(1)}, bf16[352,256]{1,0:T(8,128)(2,1)S(1)}, u32[]{:S(2)}, u32[]{:S(2)}) collective-permute-start(bf16[352,256]{1,0:T(8,128)(2,1)S(1)} %get-tuple-element.268), channel_id=1, source_target_pairs={{0,2},{1,3},{2,0},{3,1},{4,6},{5,7},{6,4},{7,5},{8,10},{9,11},{10,... | collective-permute-start | bytes 540680 | tf_op jit(solution)/shard_map/ppermute | solution.py:56
  419.1 14.3 %collective-permute-start.74 = (bf16[352,256]{1,0:T(8,128)(2,1)}, bf16[352,256]{1,0:T(8,128)(2,1)S(1)}, u32[]{:S(2)}, u32[]{:S(2)}) collective-permute-start(bf16[352,256]{1,0:T(8,128)(2,1)} %get-tuple-element.165), channel_id=1, source_target_pairs={{0,2},{1,3},{2,0},{3,1},{4,6},{5,7},{6,4},{7,5},{8,10},{9,11},{10,... | collective-permute-start | bytes 540680 | tf_op jit(solution)/shard_map/ppermute | solution.py:56
  433.6 12.0 %collective-permute-start.75 = (bf16[3,64,512]{2,1,0:T(8,128)(2,1)S(1)}, bf16[3,64,512]{2,1,0:T(8,128)(2,1)S(1)}, u32[]{:S(2)}, u32[]{:S(2)}) collective-permute-start(bf16[3,64,512]{2,1,0:T(8,128)(2,1)S(1)} %pad_maximum_fusion.54), channel_id=1, source_target_pairs={{0,4},{4,0},{8,12},{12,8},{1,5},{5,1},{9,13},{13,9},{2,6},{6,2},{1... | collective-permute-start | bytes 589832 | tf_op jit(solution)/shard_map/ppermute | solution.py:59
  434.6 11.8 %collective-permute-start.76 = (bf16[3,64,512]{2,1,0:T(8,128)(2,1)S(1)}, bf16[3,64,512]{2,1,0:T(8,128)(2,1)S(1)}, u32[]{:S(2)}, u32[]{:S(2)}) collective-permute-start(bf16[3,64,512]{2,1,0:T(8,128)(2,1)S(1)} %pad_maximum_fusion.55), channel_id=1, source_target_pairs={{0,8},{4,12},{8,0},{12,4},{1,9},{5,13},{9,1},{13,5},{2,10},{6,14},... | collective-permute-start | bytes 589832 | tf_op jit(solution)/shard_map/ppermute | solution.py:59
  436.2 18.0 %collective-permute-start.77 = (bf16[3,64,512]{2,1,0:T(8,128)(2,1)S(1)}, bf16[3,64,512]{2,1,0:T(8,128)(2,1)S(1)}, u32[]{:S(2)}, u32[]{:S(2)}) collective-permute-start(bf16[3,64,512]{2,1,0:T(8,128)(2,1)S(1)} %pad_maximum_fusion.56), channel_id=1, source_target_pairs={{0,12},{4,8},{8,4},{12,0},{1,13},{5,9},{9,5},{13,1},{2,14},{6,10},... | collective-permute-start | bytes 589832 | tf_op jit(solution)/shard_map/ppermute | solution.py:59
  437.4 20.8 %collective-permute-start.78 = (bf16[864,256]{1,0:T(8,128)(2,1)}, bf16[864,256]{1,0:T(8,128)(2,1)S(1)}, u32[]{:S(2)}, u32[]{:S(2)}) collective-permute-start(bf16[864,256]{1,0:T(8,128)(2,1)} %pad_maximum_fusion.34), channel_id=1, source_target_pairs={{0,2},{1,3},{2,0},{3,1},{4,6},{5,7},{6,4},{7,5},{8,10},{9,11},{10,... | collective-permute-start | bytes 1327112 | tf_op jit(solution)/shard_map/ppermute | solution.py:56
  463.0 17.4 %collective-permute-start.81 = (bf16[352,256]{1,0:T(8,128)(2,1)}, bf16[352,256]{1,0:T(8,128)(2,1)}, u32[]{:S(2)}, u32[]{:S(2)}) collective-permute-start(bf16[352,256]{1,0:T(8,128)(2,1)} %get-tuple-element.174), channel_id=1, source_target_pairs={{0,2},{1,3},{2,0},{3,1},{4,6},{5,7},{6,4},{7,5},{8,10},{9,11},{10,... | collective-permute-start | bytes 540680 | tf_op jit(solution)/shard_map/ppermute | solution.py:56
  481.0 14.1 %collective-permute-start.82 = (bf16[128,1024]{1,0:T(8,128)(2,1)S(1)}, bf16[128,1024]{1,0:T(8,128)(2,1)S(1)}, u32[]{:S(2)}, u32[]{:S(2)}) collective-permute-start(bf16[128,1024]{1,0:T(8,128)(2,1)S(1)} %constant_dynamic-update-slice_fusion.37), channel_id=1, source_target_pairs={{0,2},{1,3},{2,0},{3,1},{4,6},{5,7},{6,4},{7,5},{8,10},{9,11},{10,... | collective-permute-start | bytes 786440 | tf_op jit(solution)/shard_map/ppermute | solution.py:56
  496.9 19.9 %collective-permute-start.85 = (bf16[256,1024]{1,0:T(8,128)(2,1)S(1)}, bf16[256,1024]{1,0:T(8,128)(2,1)S(1)}, u32[]{:S(2)}, u32[]{:S(2)}) collective-permute-start(bf16[256,1024]{1,0:T(8,128)(2,1)S(1)} %pad_maximum_fusion.33), channel_id=1, source_target_pairs={{0,1},{1,0},{2,3},{3,2},{4,5},{5,4},{6,7},{7,6},{8,9},{9,8},{10,11... | collective-permute-start | bytes 1572872 | tf_op jit(solution)/shard_map/ppermute | solution.py:53
  501.8 19.1 %collective-permute-start.86 = (bf16[704,256]{1,0:T(8,128)(2,1)}, bf16[704,256]{1,0:T(8,128)(2,1)}, u32[]{:S(2)}, u32[]{:S(2)}) collective-permute-start(bf16[704,256]{1,0:T(8,128)(2,1)} %pad_maximum_fusion.44), channel_id=1, source_target_pairs={{0,2},{1,3},{2,0},{3,1},{4,6},{5,7},{6,4},{7,5},{8,10},{9,11},{10,... | collective-permute-start | bytes 1081352 | tf_op jit(solution)/shard_map/ppermute | solution.py:56
  526.6 19.1 %all-to-all-start = ((bf16[4,128,1024]{2,1,0:T(8,128)(2,1)}), bf16[4,128,1024]{2,1,0:T(8,128)(2,1)S(1)}, u32[]{:S(2)}, u32[]{:S(2)}) async-start(bf16[4,128,1024]{2,1,0:T(8,128)(2,1)} %bitcast.130), calls=%async_computation.4 | async-start | bytes 2097152 | tf_op jit(solution)/shard_map/all_to_all | solution.py:758
  530.1 15.5 %collective-permute-start.90 = (bf16[528,256]{1,0:T(8,128)(2,1)}, bf16[528,256]{1,0:T(8,128)(2,1)}, u32[]{:S(2)}, u32[]{:S(2)}) collective-permute-start(bf16[528,256]{1,0:T(8,128)(2,1)} %pad_maximum_fusion.45), channel_id=1, source_target_pairs={{0,2},{1,3},{2,0},{3,1},{4,6},{5,7},{6,4},{7,5},{8,10},{9,11},{10,... | collective-permute-start | bytes 811016 | tf_op jit(solution)/shard_map/ppermute | solution.py:56
  (175 other events, 995.5 us)
Sparse Core Ops, SparseCore 0:
  82.9 53.6 all-gather.5
  139.0 35.0 all-gather.3
  175.9 61.2 all-gather.7
  275.9 55.5 reduce-scatter.4
  354.2 32.7 reduce-scatter.6
  392.9 61.8 reduce-scatter.8
  468.1 33.7 reduce-scatter.10

commit v5 on v3

--- a/solution.py
+++ b/solution.py
@@ -447,8 +447,7 @@
         jnp.concatenate([gains, got], axis=1),
         jnp.concatenate([got, gains], axis=1),
     )
-    own_rest, far_first, grad_rows = together(own_rest, far_first, grad_rows)
-    out_branch = gather_rows(plan, grad_rows)
+    own_rest, far_first = together(own_rest, far_first)
     first = jnp.concatenate([own, far_first, gain_pair], axis=0)
     first = all_columns(plan, first, True)
     w_qkv, gain_full = first[: 2 * qkv_rows], first[2 * qkv_rows :].astype(F32)
@@ -492,7 +491,8 @@
             normed_all = gather_rows(plan, normed)
         qkv = dot(w_qkv, normed_all, 1, 1)
         if level + 1 < LAYERS:
-            qkv, own_later[level] = together(qkv, own_later[level])
+            qkv, own_later[level], grad_rows = together(qkv, own_later[level], grad_rows)
+            out_branch = gather_rows(plan, grad_rows)
         qkv = qkv.reshape(2, 3, 2, HEAD, tok_rows)
         query = turn(qkv[:, 0], cos_own, sine_own).astype(BF)
         key = turn(qkv[:, 1], cos_own, sine_own).astype(BF)

time: 562 us -> 571 us (1.016)
  waiting for transfers between devices: 241 us -> 256 us
    ppermute x19, waiting for transfers between devices: 107 us -> 117 us  [near(): return lax.ppermute(value, 'tp', [(i, i ^ 1) for i in range(self.tp)])]
    ppermute x33, waiting for transfers between devices: 62.7 us -> 71.1 us  [side(): return lax.ppermute(value, 'ctx', [(i, i ^ k) for i in range(self.ctx)])]
where the time goes in v5:
time: 571 us; the launch traced here: 562 us
  waiting for transfers between devices  256 us (45%)
  starting transfers between devices  84.5 us (15%)
  other arithmetic  70.2 us (12%)
  local copies, waits for them, and re-layouts  59.8 us (10%)
  matrix products  42.5 us (7%)
  Pallas kernels  31.1 us (5%)
  between operations  17.5 us (3%)
    ppermute x19, waiting for transfers between devices, near(): return lax.ppermute(value, 'tp', [(i, i ^ 1) for i in range(self.tp)])  117 us
    ppermute x33, waiting for transfers between devices, side(): return lax.ppermute(value, 'ctx', [(i, i ^ k) for i in range(self.ctx)])  71.1 us
    ppermute x14, waiting for transfers between devices, far(): return lax.ppermute(value, 'tp', [(i, i ^ 2) for i in range(self.tp)])  45.9 us
    dot_general x24, matrix products, dot(): lax.dot_general(left, right, (((left_dim,), (right_dim,)), ((), ())), pre...  42.5 us
    ppermute x33, starting transfers between devices, side(): return lax.ppermute(value, 'ctx', [(i, i ^ k) for i in range(self.ctx)])  39.5 us
    unnamed x279, local copies, waits for them, and re-layouts  21.9 us
    ppermute x14, starting transfers between devices, far(): return lax.ppermute(value, 'tp', [(i, i ^ 2) for i in range(self.tp)])  20.3 us
    ppermute x28, waiting for transfers between devices, core(): return lax.ppermute(value, 'fsdp', [(i, i ^ 1) for i in range(self.fsdp)])  17.8 us
  transfers between devices with their start and end apart: 102, of which 58 were waited for; matrix products, arithmetic and copies ran while one was open for 25% of the time, Pallas kernels for 6%

profile of v5, /device:TPU:0, one launch (start us, length us, event | category | flops | bytes accessed | tf_op | source)
XLA Modules:
  0.0 561.9 jit_solution(13015134747322957657)
XLA Ops:
  21.0 3.7 collective-permute-start.3
  30.0 4.5 collective-permute-done.3
  40.7 6.3 %collective-permute-done.5 = bf16[784,256]{1,0:T(8,128)(2,1)S(1)} collective-permute-done((bf16[784,256]{1,0:T(8,128)(2,1)S(1)}, bf16[784,256]{1,0:T(8,128)(2,1)S(1)}, u32[]{:S(2)}, u32[]{:S(2)}) %collective-permute-start.5) | collective-permute-done | bytes 401440 | tf_op jit(solution)/shard_map/ppermute | solution.py:59
  47.1 8.5 %collective-permute-done.6 = bf16[784,256]{1,0:T(8,128)(2,1)S(1)} collective-permute-done((bf16[784,256]{1,0:T(8,128)(2,1)S(1)}, bf16[784,256]{1,0:T(8,128)(2,1)S(1)}, u32[]{:S(2)}, u32[]{:S(2)}) %collective-permute-start.6) | collective-permute-done | bytes 401440 | tf_op jit(solution)/shard_map/ppermute | solution.py:59
  58.8 13.7 %collective-permute-done.17 = bf16[128,1024]{1,0:T(8,128)(2,1)S(1)} collective-permute-done((bf16[128,1024]{1,0:T(8,128)(2,1)S(1)}, bf16[128,1024]{1,0:T(8,128)(2,1)S(1)}, u32[]{:S(2)}, u32[]{:S(2)}) %collective-permute-start.17) | collective-permute-done | bytes 262176 | tf_op jit(solution)/shard_map/ppermute | solution.py:53
  79.4 8.0 %collective-permute-done.19 = bf16[352,256]{1,0:T(8,128)(2,1)S(1)} collective-permute-done((bf16[352,256]{1,0:T(8,128)(2,1)S(1)}, bf16[352,256]{1,0:T(8,128)(2,1)S(1)}, u32[]{:S(2)}, u32[]{:S(2)}) %collective-permute-start.19) | collective-permute-done | bytes 180256 | tf_op jit(solution)/shard_map/ppermute | solution.py:56
  97.8 6.8 %attend.2 = (f32[4,64,512]{2,1,0:T(8,128)}, bf16[4,64,512]{2,1,0:T(8,128)(2,1)}, f32[4,1,512]{2,1,0:T(1,128)}) custom-call(s32[6]{0:T(128)} %pad_add_fusion.2.place_ref, s32[4,1,512]{2,1,0:T(1,128)} %broadcast_in_dim.84.first_ref, bf16[3,64,512]{2,1,0:T(8,128)(2,1)} %get-tuple-element.107.refs_0_, bf16[3,64,512]{2,1,0:T(8,128)(2,1)} %copy-done.42, ...), custom_call_target="tpu_custom_call" | custom-call | tf_op jit(solution)/shard_map/attend/pallas_call | solution.py:291
  105.6 5.0 collective-permute-done.20
  120.3 4.9 collective-permute-done.27
  128.2 2.8 collective-permute-start.30
  131.0 9.3 %collective-permute-done.29 = bf16[128,1024]{1,0:T(8,128)(2,1)S(1)} collective-permute-done((bf16[128,1024]{1,0:T(8,128)(2,1)S(1)}, bf16[128,1024]{1,0:T(8,128)(2,1)S(1)}, u32[]{:S(2)}, u32[]{:S(2)}) %collective-permute-start.29) | collective-permute-done | bytes 262176 | tf_op jit(solution)/shard_map/ppermute | solution.py:53
  143.1 5.8 %collective-permute-done.31 = bf16[128,1024]{1,0:T(8,128)(2,1)} collective-permute-done((bf16[128,1024]{1,0:T(8,128)(2,1)S(1)}, bf16[128,1024]{1,0:T(8,128)(2,1)}, u32[]{:S(2)}, u32[]{:S(2)}) %collective-permute-start.31) | collective-permute-done | bytes 262176 | tf_op jit(solution)/shard_map/ppermute | solution.py:53
  152.1 4.1 fusion.6
  165.9 6.3 %collective-permute-done.34 = bf16[128,1024]{1,0:T(8,128)(2,1)} collective-permute-done((bf16[128,1024]{1,0:T(8,128)(2,1)}, bf16[128,1024]{1,0:T(8,128)(2,1)}, u32[]{:S(2)}, u32[]{:S(2)}) %collective-permute-start.34) | collective-permute-done | bytes 262176 | tf_op jit(solution)/shard_map/ppermute | solution.py:53
  175.8 6.5 %collective-permute-done.35 = bf16[128,1024]{1,0:T(8,128)(2,1)S(1)} collective-permute-done((bf16[128,1024]{1,0:T(8,128)(2,1)S(1)}, bf16[128,1024]{1,0:T(8,128)(2,1)S(1)}, u32[]{:S(2)}, u32[]{:S(2)}) %collective-permute-start.35) | collective-permute-done | bytes 262176 | tf_op jit(solution)/shard_map/ppermute | solution.py:53
  193.8 8.2 %collective-permute-done.37.refs_1_ = bf16[3,64,512]{2,1,0:T(8,128)(2,1)S(1)} collective-permute-done((bf16[3,64,512]{2,1,0:T(8,128)(2,1)S(1)}, bf16[3,64,512]{2,1,0:T(8,128)(2,1)S(1)}, u32[]{:S(2)}, u32[]{:S(2)}) %collective-permute-start.37) | collective-permute-done | bytes 196640 | tf_op jit(solution)/shard_map/ppermute | solution.py:59
  204.1 5.9 %collective-permute-done.39.refs_3_ = bf16[3,64,512]{2,1,0:T(8,128)(2,1)} collective-permute-done((bf16[3,64,512]{2,1,0:T(8,128)(2,1)S(1)}, bf16[3,64,512]{2,1,0:T(8,128)(2,1)}, u32[]{:S(2)}, u32[]{:S(2)}) %collective-permute-start.39) | collective-permute-done | bytes 196640 | tf_op jit(solution)/shard_map/ppermute | solution.py:59
  210.0 6.8 %attend.3 = (f32[4,64,512]{2,1,0:T(8,128)}, bf16[4,64,512]{2,1,0:T(8,128)(2,1)}, f32[4,1,512]{2,1,0:T(1,128)}) custom-call(s32[6]{0:T(128)} %pad_add_fusion.2.place_ref, s32[4,1,512]{2,1,0:T(1,128)} %broadcast_in_dim.84.first_ref, bf16[3,64,512]{2,1,0:T(8,128)(2,1)} %get-tuple-element.334.refs_0_, bf16[3,64,512]{2,1,0:T(8,128)(2,1)} %copy-done.45, ...), custom_call_target="tpu_custom_call" | custom-call | tf_op jit(solution)/shard_map/attend/pallas_call | solution.py:291
  232.0 7.4 %collective-permute-done.44 = bf16[128,1024]{1,0:T(8,128)(2,1)S(1)} collective-permute-done((bf16[128,1024]{1,0:T(8,128)(2,1)S(1)}, bf16[128,1024]{1,0:T(8,128)(2,1)S(1)}, u32[]{:S(2)}, u32[]{:S(2)}) %collective-permute-start.44) | collective-permute-done | bytes 262176 | tf_op jit(solution)/shard_map/ppermute | solution.py:53
  240.7 6.7 %collective-permute-done.45 = bf16[128,1024]{1,0:T(8,128)(2,1)S(1)} collective-permute-done((bf16[128,1024]{1,0:T(8,128)(2,1)S(1)}, bf16[128,1024]{1,0:T(8,128)(2,1)S(1)}, u32[]{:S(2)}, u32[]{:S(2)}) %collective-permute-start.45) | collective-permute-done | bytes 262176 | tf_op jit(solution)/shard_map/ppermute | solution.py:53
  250.6 4.0 fusion.2
  259.6 2.7 convolution_convert_fusion.1
  267.6 5.5 collective-permute-done.48
  276.9 6.8 %collective-permute-done.49 = bf16[128,1024]{1,0:T(8,128)(2,1)S(1)} collective-permute-done((bf16[128,1024]{1,0:T(8,128)(2,1)S(1)}, bf16[128,1024]{1,0:T(8,128)(2,1)S(1)}, u32[]{:S(2)}, u32[]{:S(2)}) %collective-permute-start.49) | collective-permute-done | bytes 262176 | tf_op jit(solution)/shard_map/ppermute | solution.py:53
  301.4 2.8 collective-permute-done.53.refs_7_
  311.5 8.7 %attend_back.2 = (f32[4,64,512]{2,1,0:T(8,128)}, f32[4,64,512]{2,1,0:T(8,128)}, f32[4,64,512]{2,1,0:T(8,128)}) custom-call(s32[6]{0:T(128)} %pad_add_fusion.2.place_ref, s32[4,1,512]{2,1,0:T(1,128)} %broadcast_in_dim.84.first_ref, f32[4,64,512]{2,1,0:T(8,128)} %get-tuple-element.124.out_ref, f32[4,1,512]{2,1,0:T(1,128)} %get-tuple-element.125.lse_ref, ...), custom_call_target="tpu_custom_call" | custom-call | tf_op jit(solution)/shard_map/attend_back/pallas_call | solution.py:350
  328.9 6.1 %collective-permute-done.57 = bf16[3,64,512]{2,1,0:T(8,128)(2,1)S(1)} collective-permute-done((bf16[3,64,512]{2,1,0:T(8,128)(2,1)S(1)}, bf16[3,64,512]{2,1,0:T(8,128)(2,1)S(1)}, u32[]{:S(2)}, u32[]{:S(2)}) %collective-permute-start.57) | collective-permute-done | bytes 196640 | tf_op jit(solution)/shard_map/ppermute | solution.py:59
  335.1 6.8 %collective-permute-done.58 = bf16[3,64,512]{2,1,0:T(8,128)(2,1)S(1)} collective-permute-done((bf16[3,64,512]{2,1,0:T(8,128)(2,1)S(1)}, bf16[3,64,512]{2,1,0:T(8,128)(2,1)S(1)}, u32[]{:S(2)}, u32[]{:S(2)}) %collective-permute-start.58) | collective-permute-done | bytes 196640 | tf_op jit(solution)/shard_map/ppermute | solution.py:59
  352.9 4.5 collective-permute-done.63
  361.8 7.4 %collective-permute-done.64 = bf16[128,1024]{1,0:T(8,128)(2,1)S(1)} collective-permute-done((bf16[128,1024]{1,0:T(8,128)(2,1)S(1)}, bf16[128,1024]{1,0:T(8,128)(2,1)S(1)}, u32[]{:S(2)}, u32[]{:S(2)}) %collective-permute-start.64) | collective-permute-done | bytes 262176 | tf_op jit(solution)/shard_map/ppermute | solution.py:53
  371.2 2.8 multiply_convert_fusion.1
  377.6 2.8 convolution_convert_fusion
  384.2 6.0 %collective-permute-done.67 = bf16[128,1024]{1,0:T(8,128)(2,1)S(1)} collective-permute-done((bf16[128,1024]{1,0:T(8,128)(2,1)}, bf16[128,1024]{1,0:T(8,128)(2,1)S(1)}, u32[]{:S(2)}, u32[]{:S(2)}) %collective-permute-start.67) | collective-permute-done | bytes 262176 | tf_op jit(solution)/shard_map/ppermute | solution.py:53
  395.9 6.8 %collective-permute-done.68 = bf16[128,1024]{1,0:T(8,128)(2,1)S(1)} collective-permute-done((bf16[128,1024]{1,0:T(8,128)(2,1)S(1)}, bf16[128,1024]{1,0:T(8,128)(2,1)S(1)}, u32[]{:S(2)}, u32[]{:S(2)}) %collective-permute-start.68) | collective-permute-done | bytes 262176 | tf_op jit(solution)/shard_map/ppermute | solution.py:53
  412.8 4.6 collective-permute-done.73
  418.1 2.8 collective-permute-start.74
  421.0 8.8 %attend_back.3 = (f32[4,64,512]{2,1,0:T(8,128)}, f32[4,64,512]{2,1,0:T(8,128)}, f32[4,64,512]{2,1,0:T(8,128)}) custom-call(s32[6]{0:T(128)} %pad_add_fusion.2.place_ref, s32[4,1,512]{2,1,0:T(1,128)} %broadcast_in_dim.84.first_ref, f32[4,64,512]{2,1,0:T(8,128)} %get-tuple-element.153.out_ref, f32[4,1,512]{2,1,0:T(1,128)} %get-tuple-element.154.lse_ref, ...), custom_call_target="tpu_custom_call" | custom-call | tf_op jit(solution)/shard_map/attend_back/pallas_call | solution.py:350
  438.4 5.9 %collective-permute-done.75 = bf16[3,64,512]{2,1,0:T(8,128)(2,1)S(1)} collective-permute-done((bf16[3,64,512]{2,1,0:T(8,128)(2,1)S(1)}, bf16[3,64,512]{2,1,0:T(8,128)(2,1)S(1)}, u32[]{:S(2)}, u32[]{:S(2)}) %collective-permute-start.75) | collective-permute-done | bytes 196640 | tf_op jit(solution)/shard_map/ppermute | solution.py:59
  444.4 3.3 collective-permute-done.76
  447.7 2.8 collective-permute-done.77
  451.5 4.2 reduce-scatter.9.cloned.1.call-done
  474.9 6.2 %collective-permute-done.80 = bf16[128,1024]{1,0:T(8,128)(2,1)S(1)} collective-permute-done((bf16[128,1024]{1,0:T(8,128)(2,1)S(1)}, bf16[128,1024]{1,0:T(8,128)(2,1)S(1)}, u32[]{:S(2)}, u32[]{:S(2)}) %collective-permute-start.80) | collective-permute-done | bytes 262176 | tf_op jit(solution)/shard_map/ppermute | solution.py:53
  486.4 3.2 collective-permute-done.83
  489.6 6.5 %collective-permute-done.82 = bf16[128,1024]{1,0:T(8,128)(2,1)S(1)} collective-permute-done((bf16[128,1024]{1,0:T(8,128)(2,1)S(1)}, bf16[128,1024]{1,0:T(8,128)(2,1)S(1)}, u32[]{:S(2)}, u32[]{:S(2)}) %collective-permute-start.82) | collective-permute-done | bytes 262176 | tf_op jit(solution)/shard_map/ppermute | solution.py:56
  505.9 12.2 %collective-permute-done.85 = bf16[256,1024]{1,0:T(8,128)(2,1)S(1)} collective-permute-done((bf16[256,1024]{1,0:T(8,128)(2,1)S(1)}, bf16[256,1024]{1,0:T(8,128)(2,1)S(1)}, u32[]{:S(2)}, u32[]{:S(2)}) %collective-permute-start.85) | collective-permute-done | bytes 524320 | tf_op jit(solution)/shard_map/ppermute | solution.py:53
  518.2 2.9 gather_fusion
  527.9 3.5 all-to-all-start
  535.6 11.1 %collective-permute-done.90 = bf16[528,256]{1,0:T(8,128)(2,1)} collective-permute-done((bf16[528,256]{1,0:T(8,128)(2,1)}, bf16[528,256]{1,0:T(8,128)(2,1)}, u32[]{:S(2)}, u32[]{:S(2)}) %collective-permute-start.90) | collective-permute-done | bytes 270368 | tf_op jit(solution)/shard_map/ppermute | solution.py:56
  (749 shorter events, 261.3 us)
Async XLA Ops:
  7.2 144.9 %all-gather.6.cloned.1.call-start = ((), (), s32[]{:S(2)}) async-start(), calls=%async_computation.6 | async-start | bytes 5406720 | tf_op jit(solution)/shard_map/all_gather | solution.py:139
  7.2 10.1 %collective-permute-start = (s32[1,2048]{1,0:T(1,128)}, s32[1,2048]{1,0:T(1,128)S(1)}, u32[]{:S(2)}, u32[]{:S(2)}) collective-permute-start(s32[1,2048]{1,0:T(1,128)} %param.15), channel_id=1, source_target_pairs={{0,16},{16,0},{1,17},{17,1},{2,18},{18,2},{3,19},{19,3},{4,20},{20... | collective-permute-start | bytes 24584 | tf_op jit(solution)/shard_map/ppermute | solution.py:50
  11.6 17.1 %collective-permute-start.2 = (bf16[1184,128]{1,0:T(8,128)(2,1)}, bf16[1184,128]{1,0:T(8,128)(2,1)}, u32[]{:S(2)}, u32[]{:S(2)}) collective-permute-start(bf16[1184,128]{1,0:T(8,128)(2,1)} %get-tuple-element.350), channel_id=1, source_target_pairs={{0,16},{16,0},{1,17},{17,1},{2,18},{18,2},{3,19},{19,3},{4,20},{20... | collective-permute-start | bytes 909320 | tf_op jit(solution)/shard_map/ppermute | solution.py:50
  14.2 10.5 %collective-permute-start.8 = (bf16[128,1024]{1,0:T(8,128)(2,1)S(1)}, bf16[128,1024]{1,0:T(8,128)(2,1)}, u32[]{:S(2)}, u32[]{:S(2)}) collective-permute-start(bf16[128,1024]{1,0:T(8,128)(2,1)S(1)} %constant_dynamic-slice_fusion.14), channel_id=1, source_target_pairs={{0,16},{16,0},{1,17},{17,1},{2,18},{18,2},{3,19},{19,3},{4,20},{20... | collective-permute-start | bytes 786440 | tf_op jit(solution)/shard_map/ppermute | solution.py:50
  17.2 21.2 %collective-permute-start.11 = (bf16[1568,128]{1,0:T(8,128)(2,1)}, bf16[1568,128]{1,0:T(8,128)(2,1)S(1)}, u32[]{:S(2)}, u32[]{:S(2)}) collective-permute-start(bf16[1568,128]{1,0:T(8,128)(2,1)} %get-tuple-element.330), channel_id=1, source_target_pairs={{0,16},{16,0},{1,17},{17,1},{2,18},{18,2},{3,19},{19,3},{4,20},{20... | collective-permute-start | bytes 1204232 | tf_op jit(solution)/shard_map/ppermute | solution.py:50
  17.4 10.2 %collective-permute-start.12 = (bf16[128,1024]{1,0:T(8,128)(2,1)S(1)}, bf16[128,1024]{1,0:T(8,128)(2,1)S(1)}, u32[]{:S(2)}, u32[]{:S(2)}) collective-permute-start(bf16[128,1024]{1,0:T(8,128)(2,1)S(1)} %constant_dynamic-slice_fusion.13), channel_id=1, source_target_pairs={{0,16},{16,0},{1,17},{17,1},{2,18},{18,2},{3,19},{19,3},{4,20},{20... | collective-permute-start | bytes 786440 | tf_op jit(solution)/shard_map/ppermute | solution.py:50
  21.0 13.5 %collective-permute-start.3 = (bf16[384,256]{1,0:T(8,128)(2,1)S(1)}, bf16[384,256]{1,0:T(8,128)(2,1)S(1)}, u32[]{:S(2)}, u32[]{:S(2)}) collective-permute-start(bf16[384,256]{1,0:T(8,128)(2,1)S(1)} %maximum_select_fusion.2), channel_id=1, source_target_pairs={{0,2},{1,3},{2,0},{3,1},{4,6},{5,7},{6,4},{7,5},{8,10},{9,11},{10,... | collective-permute-start | bytes 589832 | tf_op jit(solution)/shard_map/ppermute | solution.py:56
  25.9 14.7 %collective-permute-start.9 = (bf16[128,1024]{1,0:T(8,128)(2,1)S(1)}, bf16[128,1024]{1,0:T(8,128)(2,1)S(1)}, u32[]{:S(2)}, u32[]{:S(2)}) collective-permute-start(bf16[128,1024]{1,0:T(8,128)(2,1)S(1)} %constant_dynamic-update-slice_fusion), channel_id=1, source_target_pairs={{0,1},{1,0},{2,3},{3,2},{4,5},{5,4},{6,7},{7,6},{8,9},{9,8},{10,11... | collective-permute-start | bytes 786440 | tf_op jit(solution)/shard_map/ppermute | solution.py:53
  34.8 12.2 %collective-permute-start.5 = (bf16[784,256]{1,0:T(8,128)(2,1)S(1)}, bf16[784,256]{1,0:T(8,128)(2,1)S(1)}, u32[]{:S(2)}, u32[]{:S(2)}) collective-permute-start(bf16[784,256]{1,0:T(8,128)(2,1)S(1)} %get-tuple-element.377), channel_id=1, source_target_pairs={{0,4},{4,0},{8,12},{12,8},{1,5},{5,1},{9,13},{13,9},{2,6},{6,2},{1... | collective-permute-start | bytes 1204232 | tf_op jit(solution)/shard_map/ppermute | solution.py:59
  36.4 19.1 %collective-permute-start.6 = (bf16[784,256]{1,0:T(8,128)(2,1)S(1)}, bf16[784,256]{1,0:T(8,128)(2,1)S(1)}, u32[]{:S(2)}, u32[]{:S(2)}) collective-permute-start(bf16[784,256]{1,0:T(8,128)(2,1)S(1)} %get-tuple-element.377), channel_id=1, source_target_pairs={{0,8},{4,12},{8,0},{12,4},{1,9},{5,13},{9,1},{13,5},{2,10},{6,14},... | collective-permute-start | bytes 1204232 | tf_op jit(solution)/shard_map/ppermute | solution.py:59
  38.0 17.6 %collective-permute-start.7 = (bf16[784,256]{1,0:T(8,128)(2,1)S(1)}, bf16[784,256]{1,0:T(8,128)(2,1)S(1)}, u32[]{:S(2)}, u32[]{:S(2)}) collective-permute-start(bf16[784,256]{1,0:T(8,128)(2,1)S(1)} %get-tuple-element.377), channel_id=1, source_target_pairs={{0,12},{4,8},{8,4},{12,0},{1,13},{5,9},{9,5},{13,1},{2,14},{6,10},... | collective-permute-start | bytes 1204232 | tf_op jit(solution)/shard_map/ppermute | solution.py:59
  38.4 39.1 %collective-permute-start.16 = (bf16[1184,256]{1,0:T(8,128)(2,1)S(1)}, bf16[1184,256]{1,0:T(8,128)(2,1)S(1)}, u32[]{:S(2)}, u32[]{:S(2)}) collective-permute-start(bf16[1184,256]{1,0:T(8,128)(2,1)S(1)} %maximum_select_fusion.1), channel_id=1, source_target_pairs={{0,2},{1,3},{2,0},{3,1},{4,6},{5,7},{6,4},{7,5},{8,10},{9,11},{10,... | collective-permute-start | bytes 1818632 | tf_op jit(solution)/shard_map/ppermute | solution.py:56
  40.6 15.1 %collective-permute-start.10 = (bf16[256,1024]{1,0:T(8,128)(2,1)S(1)}, bf16[256,1024]{1,0:T(8,128)(2,1)S(1)}, u32[]{:S(2)}, u32[]{:S(2)}) collective-permute-start(bf16[256,1024]{1,0:T(8,128)(2,1)S(1)} %pad_maximum_fusion.23), channel_id=1, source_target_pairs={{0,16},{16,0},{1,17},{17,1},{2,18},{18,2},{3,19},{19,3},{4,20},{20... | collective-permute-start | bytes 1572872 | tf_op jit(solution)/shard_map/ppermute | solution.py:50
  57.3 15.2 %collective-permute-start.17 = (bf16[128,1024]{1,0:T(8,128)(2,1)S(1)}, bf16[128,1024]{1,0:T(8,128)(2,1)S(1)}, u32[]{:S(2)}, u32[]{:S(2)}) collective-permute-start(bf16[128,1024]{1,0:T(8,128)(2,1)S(1)} %constant_dynamic-update-slice_fusion.15), channel_id=1, source_target_pairs={{0,1},{1,0},{2,3},{3,2},{4,5},{5,4},{6,7},{7,6},{8,9},{9,8},{10,11... | collective-permute-start | bytes 786440 | tf_op jit(solution)/shard_map/ppermute | solution.py:53
  73.4 14.0 %collective-permute-start.13 = (bf16[3,64,512]{2,1,0:T(8,128)(2,1)S(1)}, bf16[3,64,512]{2,1,0:T(8,128)(2,1)S(1)}, u32[]{:S(2)}, u32[]{:S(2)}) collective-permute-start(bf16[3,64,512]{2,1,0:T(8,128)(2,1)S(1)} %get-tuple-element.337), channel_id=1, source_target_pairs={{0,4},{4,0},{8,12},{12,8},{1,5},{5,1},{9,13},{13,9},{2,6},{6,2},{1... | collective-permute-start | bytes 589832 | tf_op jit(solution)/shard_map/ppermute | solution.py:59
  74.6 12.8 %collective-permute-start.14 = (bf16[3,64,512]{2,1,0:T(8,128)(2,1)S(1)}, bf16[3,64,512]{2,1,0:T(8,128)(2,1)S(1)}, u32[]{:S(2)}, u32[]{:S(2)}) collective-permute-start(bf16[3,64,512]{2,1,0:T(8,128)(2,1)S(1)} %get-tuple-element.336), channel_id=1, source_target_pairs={{0,8},{4,12},{8,0},{12,4},{1,9},{5,13},{9,1},{13,5},{2,10},{6,14},... | collective-permute-start | bytes 589832 | tf_op jit(solution)/shard_map/ppermute | solution.py:59
  76.1 11.3 %collective-permute-start.15 = (bf16[3,64,512]{2,1,0:T(8,128)(2,1)S(1)}, bf16[3,64,512]{2,1,0:T(8,128)(2,1)S(1)}, u32[]{:S(2)}, u32[]{:S(2)}) collective-permute-start(bf16[3,64,512]{2,1,0:T(8,128)(2,1)S(1)} %get-tuple-element.335), channel_id=1, source_target_pairs={{0,12},{4,8},{8,4},{12,0},{1,13},{5,9},{9,5},{13,1},{2,14},{6,10},... | collective-permute-start | bytes 589832 | tf_op jit(solution)/shard_map/ppermute | solution.py:59
  77.5 9.8 %collective-permute-start.19 = (bf16[352,256]{1,0:T(8,128)(2,1)S(1)}, bf16[352,256]{1,0:T(8,128)(2,1)S(1)}, u32[]{:S(2)}, u32[]{:S(2)}) collective-permute-start(bf16[352,256]{1,0:T(8,128)(2,1)S(1)} %get-tuple-element.106), channel_id=1, source_target_pairs={{0,2},{1,3},{2,0},{3,1},{4,6},{5,7},{6,4},{7,5},{8,10},{9,11},{10,... | collective-permute-start | bytes 540680 | tf_op jit(solution)/shard_map/ppermute | solution.py:56
  91.0 92.2 %all-gather.4.cloned.1.call-start = ((), (), s32[]{:S(2)}) async-start(), calls=%async_computation.5 | async-start | bytes 2621440 | tf_op jit(solution)/shard_map/all_gather | solution.py:139
  92.2 12.3 %collective-permute-start.21 = (bf16[256,256]{1,0:T(8,128)(2,1)S(1)}, bf16[256,256]{1,0:T(8,128)(2,1)S(1)}, u32[]{:S(2)}, u32[]{:S(2)}) collective-permute-start(bf16[256,256]{1,0:T(8,128)(2,1)S(1)} %get-tuple-element.413), channel_id=1, source_target_pairs={{0,4},{4,0},{8,12},{12,8},{1,5},{5,1},{9,13},{13,9},{2,6},{6,2},{1... | collective-permute-start | bytes 393224 | tf_op jit(solution)/shard_map/ppermute | solution.py:59
  97.1 13.5 %collective-permute-start.20 = (bf16[512,256]{1,0:T(8,128)(2,1)S(1)}, bf16[512,256]{1,0:T(8,128)(2,1)S(1)}, u32[]{:S(2)}, u32[]{:S(2)}) collective-permute-start(bf16[512,256]{1,0:T(8,128)(2,1)S(1)} %slice.966), channel_id=1, source_target_pairs={{0,2},{1,3},{2,0},{3,1},{4,6},{5,7},{6,4},{7,5},{8,10},{9,11},{10,... | collective-permute-start | bytes 786440 | tf_op jit(solution)/shard_map/ppermute | solution.py:56
  128.0 12.3 %collective-permute-start.29 = (bf16[128,1024]{1,0:T(8,128)(2,1)S(1)}, bf16[128,1024]{1,0:T(8,128)(2,1)S(1)}, u32[]{:S(2)}, u32[]{:S(2)}) collective-permute-start(bf16[128,1024]{1,0:T(8,128)(2,1)S(1)} %slice.1789), channel_id=1, source_target_pairs={{0,1},{1,0},{2,3},{3,2},{4,5},{5,4},{6,7},{7,6},{8,9},{9,8},{10,11... | collective-permute-start | bytes 786440 | tf_op jit(solution)/shard_map/ppermute | solution.py:53
  128.2 12.2 %collective-permute-start.30 = (bf16[352,256]{1,0:T(8,128)(2,1)S(1)}, bf16[352,256]{1,0:T(8,128)(2,1)S(1)}, u32[]{:S(2)}, u32[]{:S(2)}) collective-permute-start(bf16[352,256]{1,0:T(8,128)(2,1)S(1)} %get-tuple-element.122), channel_id=1, source_target_pairs={{0,2},{1,3},{2,0},{3,1},{4,6},{5,7},{6,4},{7,5},{8,10},{9,11},{10,... | collective-permute-start | bytes 540680 | tf_op jit(solution)/shard_map/ppermute | solution.py:56
  143.1 105.2 %all-gather.8.cloned.1.call-start = ((), (), s32[]{:S(2)}) async-start(), calls=%async_computation.7 | async-start | bytes 5406720 | tf_op jit(solution)/shard_map/all_gather | solution.py:139
  165.9 192.7 %reduce-scatter.5.cloned.1.call-start = ((), (), s32[]{:S(2)}) async-start(), calls=%async_computation.8 | async-start | bytes 5406720 | tf_op jit(solution)/shard_map/reduce_scatter | solution.py:165
  190.3 11.7 %collective-permute-start.37 = (bf16[3,64,512]{2,1,0:T(8,128)(2,1)S(1)}, bf16[3,64,512]{2,1,0:T(8,128)(2,1)S(1)}, u32[]{:S(2)}, u32[]{:S(2)}) collective-permute-start(bf16[3,64,512]{2,1,0:T(8,128)(2,1)S(1)} %get-tuple-element.333), channel_id=1, source_target_pairs={{0,4},{4,0},{8,12},{12,8},{1,5},{5,1},{9,13},{13,9},{2,6},{6,2},{1... | collective-permute-start | bytes 589832 | tf_op jit(solution)/shard_map/ppermute | solution.py:59
  191.4 12.7 %collective-permute-start.38 = (bf16[3,64,512]{2,1,0:T(8,128)(2,1)S(1)}, bf16[3,64,512]{2,1,0:T(8,128)(2,1)S(1)}, u32[]{:S(2)}, u32[]{:S(2)}) collective-permute-start(bf16[3,64,512]{2,1,0:T(8,128)(2,1)S(1)} %get-tuple-element.332), channel_id=1, source_target_pairs={{0,8},{4,12},{8,0},{12,4},{1,9},{5,13},{9,1},{13,5},{2,10},{6,14},... | collective-permute-start | bytes 589832 | tf_op jit(solution)/shard_map/ppermute | solution.py:59
  192.9 17.0 %collective-permute-start.39 = (bf16[3,64,512]{2,1,0:T(8,128)(2,1)S(1)}, bf16[3,64,512]{2,1,0:T(8,128)(2,1)}, u32[]{:S(2)}, u32[]{:S(2)}) collective-permute-start(bf16[3,64,512]{2,1,0:T(8,128)(2,1)S(1)} %get-tuple-element.331), channel_id=1, source_target_pairs={{0,12},{4,8},{8,4},{12,0},{1,13},{5,9},{9,5},{13,1},{2,14},{6,10},... | collective-permute-start | bytes 589832 | tf_op jit(solution)/shard_map/ppermute | solution.py:59
  284.7 106.7 %reduce-scatter.7.cloned.1.call-start = ((), (), s32[]{:S(2)}) async-start(), calls=%async_computation.9 | async-start | bytes 2621440 | tf_op jit(solution)/shard_map/reduce_scatter | solution.py:165
  309.3 14.4 %collective-permute-start.56 = (bf16[128,1024]{1,0:T(8,128)(2,1)}, bf16[128,1024]{1,0:T(8,128)(2,1)}, u32[]{:S(2)}, u32[]{:S(2)}) collective-permute-start(bf16[128,1024]{1,0:T(8,128)(2,1)} %constant_dynamic-update-slice_fusion.29), channel_id=1, source_target_pairs={{0,2},{1,3},{2,0},{3,1},{4,6},{5,7},{6,4},{7,5},{8,10},{9,11},{10,... | collective-permute-start | bytes 786440 | tf_op jit(solution)/shard_map/ppermute | solution.py:56
  323.8 11.3 %collective-permute-start.57 = (bf16[3,64,512]{2,1,0:T(8,128)(2,1)S(1)}, bf16[3,64,512]{2,1,0:T(8,128)(2,1)S(1)}, u32[]{:S(2)}, u32[]{:S(2)}) collective-permute-start(bf16[3,64,512]{2,1,0:T(8,128)(2,1)S(1)} %pad_maximum_fusion.51), channel_id=1, source_target_pairs={{0,4},{4,0},{8,12},{12,8},{1,5},{5,1},{9,13},{13,9},{2,6},{6,2},{1... | collective-permute-start | bytes 589832 | tf_op jit(solution)/shard_map/ppermute | solution.py:59
  325.8 16.1 %collective-permute-start.58 = (bf16[3,64,512]{2,1,0:T(8,128)(2,1)S(1)}, bf16[3,64,512]{2,1,0:T(8,128)(2,1)S(1)}, u32[]{:S(2)}, u32[]{:S(2)}) collective-permute-start(bf16[3,64,512]{2,1,0:T(8,128)(2,1)S(1)} %pad_maximum_fusion.52), channel_id=1, source_target_pairs={{0,8},{4,12},{8,0},{12,4},{1,9},{5,13},{9,1},{13,5},{2,10},{6,14},... | collective-permute-start | bytes 589832 | tf_op jit(solution)/shard_map/ppermute | solution.py:59
  326.5 15.4 %collective-permute-start.59 = (bf16[3,64,512]{2,1,0:T(8,128)(2,1)S(1)}, bf16[3,64,512]{2,1,0:T(8,128)(2,1)S(1)}, u32[]{:S(2)}, u32[]{:S(2)}) collective-permute-start(bf16[3,64,512]{2,1,0:T(8,128)(2,1)S(1)} %pad_maximum_fusion.53), channel_id=1, source_target_pairs={{0,12},{4,8},{8,4},{12,0},{1,13},{5,9},{9,5},{13,1},{2,14},{6,10},... | collective-permute-start | bytes 589832 | tf_op jit(solution)/shard_map/ppermute | solution.py:59
  328.9 13.8 %collective-permute-start.61 = (bf16[256,1024]{1,0:T(8,128)(2,1)S(1)}, bf16[256,1024]{1,0:T(8,128)(2,1)S(1)}, u32[]{:S(2)}, u32[]{:S(2)}) collective-permute-start(bf16[256,1024]{1,0:T(8,128)(2,1)S(1)} %pad_maximum_fusion.30), channel_id=1, source_target_pairs={{0,1},{1,0},{2,3},{3,2},{4,5},{5,4},{6,7},{7,6},{8,9},{9,8},{10,11... | collective-permute-start | bytes 1572872 | tf_op jit(solution)/shard_map/ppermute | solution.py:53
  352.6 103.1 %reduce-scatter.9.cloned.1.call-start = ((), (), s32[]{:S(2)}) async-start(), calls=%async_computation.10 | async-start | bytes 5406720 | tf_op jit(solution)/shard_map/reduce_scatter | solution.py:165
  391.4 129.8 %reduce-scatter.11.cloned.1.call-start = ((), (), s32[]{:S(2)}) async-start(), calls=%async_computation.11 | async-start | bytes 2621440 | tf_op jit(solution)/shard_map/reduce_scatter | solution.py:165
  405.9 11.5 %collective-permute-start.73 = (bf16[352,256]{1,0:T(8,128)(2,1)S(1)}, bf16[352,256]{1,0:T(8,128)(2,1)S(1)}, u32[]{:S(2)}, u32[]{:S(2)}) collective-permute-start(bf16[352,256]{1,0:T(8,128)(2,1)S(1)} %get-tuple-element.268), channel_id=1, source_target_pairs={{0,2},{1,3},{2,0},{3,1},{4,6},{5,7},{6,4},{7,5},{8,10},{9,11},{10,... | collective-permute-start | bytes 540680 | tf_op jit(solution)/shard_map/ppermute | solution.py:56
  418.1 14.1 %collective-permute-start.74 = (bf16[352,256]{1,0:T(8,128)(2,1)}, bf16[352,256]{1,0:T(8,128)(2,1)S(1)}, u32[]{:S(2)}, u32[]{:S(2)}) collective-permute-start(bf16[352,256]{1,0:T(8,128)(2,1)} %get-tuple-element.165), channel_id=1, source_target_pairs={{0,2},{1,3},{2,0},{3,1},{4,6},{5,7},{6,4},{7,5},{8,10},{9,11},{10,... | collective-permute-start | bytes 540680 | tf_op jit(solution)/shard_map/ppermute | solution.py:56
  432.3 12.0 %collective-permute-start.75 = (bf16[3,64,512]{2,1,0:T(8,128)(2,1)S(1)}, bf16[3,64,512]{2,1,0:T(8,128)(2,1)S(1)}, u32[]{:S(2)}, u32[]{:S(2)}) collective-permute-start(bf16[3,64,512]{2,1,0:T(8,128)(2,1)S(1)} %pad_maximum_fusion.54), channel_id=1, source_target_pairs={{0,4},{4,0},{8,12},{12,8},{1,5},{5,1},{9,13},{13,9},{2,6},{6,2},{1... | collective-permute-start | bytes 589832 | tf_op jit(solution)/shard_map/ppermute | solution.py:59
  433.1 14.5 %collective-permute-start.76 = (bf16[3,64,512]{2,1,0:T(8,128)(2,1)S(1)}, bf16[3,64,512]{2,1,0:T(8,128)(2,1)S(1)}, u32[]{:S(2)}, u32[]{:S(2)}) collective-permute-start(bf16[3,64,512]{2,1,0:T(8,128)(2,1)S(1)} %pad_maximum_fusion.55), channel_id=1, source_target_pairs={{0,8},{4,12},{8,0},{12,4},{1,9},{5,13},{9,1},{13,5},{2,10},{6,14},... | collective-permute-start | bytes 589832 | tf_op jit(solution)/shard_map/ppermute | solution.py:59
  433.9 16.6 %collective-permute-start.77 = (bf16[3,64,512]{2,1,0:T(8,128)(2,1)S(1)}, bf16[3,64,512]{2,1,0:T(8,128)(2,1)S(1)}, u32[]{:S(2)}, u32[]{:S(2)}) collective-permute-start(bf16[3,64,512]{2,1,0:T(8,128)(2,1)S(1)} %pad_maximum_fusion.56), channel_id=1, source_target_pairs={{0,12},{4,8},{8,4},{12,0},{1,13},{5,9},{9,5},{13,1},{2,14},{6,10},... | collective-permute-start | bytes 589832 | tf_op jit(solution)/shard_map/ppermute | solution.py:59
  436.1 21.8 %collective-permute-start.78 = (bf16[864,256]{1,0:T(8,128)(2,1)}, bf16[864,256]{1,0:T(8,128)(2,1)S(1)}, u32[]{:S(2)}, u32[]{:S(2)}) collective-permute-start(bf16[864,256]{1,0:T(8,128)(2,1)} %pad_maximum_fusion.34), channel_id=1, source_target_pairs={{0,2},{1,3},{2,0},{3,1},{4,6},{5,7},{6,4},{7,5},{8,10},{9,11},{10,... | collective-permute-start | bytes 1327112 | tf_op jit(solution)/shard_map/ppermute | solution.py:56
  462.7 18.5 %collective-permute-start.81 = (bf16[352,256]{1,0:T(8,128)(2,1)}, bf16[352,256]{1,0:T(8,128)(2,1)}, u32[]{:S(2)}, u32[]{:S(2)}) collective-permute-start(bf16[352,256]{1,0:T(8,128)(2,1)} %get-tuple-element.174), channel_id=1, source_target_pairs={{0,2},{1,3},{2,0},{3,1},{4,6},{5,7},{6,4},{7,5},{8,10},{9,11},{10,... | collective-permute-start | bytes 540680 | tf_op jit(solution)/shard_map/ppermute | solution.py:56
  481.8 14.3 %collective-permute-start.82 = (bf16[128,1024]{1,0:T(8,128)(2,1)S(1)}, bf16[128,1024]{1,0:T(8,128)(2,1)S(1)}, u32[]{:S(2)}, u32[]{:S(2)}) collective-permute-start(bf16[128,1024]{1,0:T(8,128)(2,1)S(1)} %constant_dynamic-update-slice_fusion.37), channel_id=1, source_target_pairs={{0,2},{1,3},{2,0},{3,1},{4,6},{5,7},{6,4},{7,5},{8,10},{9,11},{10,... | collective-permute-start | bytes 786440 | tf_op jit(solution)/shard_map/ppermute | solution.py:56
  497.7 20.4 %collective-permute-start.85 = (bf16[256,1024]{1,0:T(8,128)(2,1)S(1)}, bf16[256,1024]{1,0:T(8,128)(2,1)S(1)}, u32[]{:S(2)}, u32[]{:S(2)}) collective-permute-start(bf16[256,1024]{1,0:T(8,128)(2,1)S(1)} %pad_maximum_fusion.33), channel_id=1, source_target_pairs={{0,1},{1,0},{2,3},{3,2},{4,5},{5,4},{6,7},{7,6},{8,9},{9,8},{10,11... | collective-permute-start | bytes 1572872 | tf_op jit(solution)/shard_map/ppermute | solution.py:53
  502.7 22.4 %collective-permute-start.86 = (bf16[704,256]{1,0:T(8,128)(2,1)}, bf16[704,256]{1,0:T(8,128)(2,1)}, u32[]{:S(2)}, u32[]{:S(2)}) collective-permute-start(bf16[704,256]{1,0:T(8,128)(2,1)} %pad_maximum_fusion.44), channel_id=1, source_target_pairs={{0,2},{1,3},{2,0},{3,1},{4,6},{5,7},{6,4},{7,5},{8,10},{9,11},{10,... | collective-permute-start | bytes 1081352 | tf_op jit(solution)/shard_map/ppermute | solution.py:56
  527.9 18.7 %all-to-all-start = ((bf16[4,128,1024]{2,1,0:T(8,128)(2,1)}), bf16[4,128,1024]{2,1,0:T(8,128)(2,1)S(1)}, u32[]{:S(2)}, u32[]{:S(2)}) async-start(bf16[4,128,1024]{2,1,0:T(8,128)(2,1)} %bitcast.130), calls=%async_computation.4 | async-start | bytes 2097152 | tf_op jit(solution)/shard_map/all_to_all | solution.py:743
  531.5 15.2 %collective-permute-start.90 = (bf16[528,256]{1,0:T(8,128)(2,1)}, bf16[528,256]{1,0:T(8,128)(2,1)}, u32[]{:S(2)}, u32[]{:S(2)}) collective-permute-start(bf16[528,256]{1,0:T(8,128)(2,1)} %pad_maximum_fusion.45), channel_id=1, source_target_pairs={{0,2},{1,3},{2,0},{3,1},{4,6},{5,7},{6,4},{7,5},{8,10},{9,11},{10,... | collective-permute-start | bytes 811016 | tf_op jit(solution)/shard_map/ppermute | solution.py:56
  (173 other events, 997.6 us)
Sparse Core Ops, SparseCore 0:
  91.1 53.1 all-gather.5
  146.7 35.0 all-gather.3
  183.6 62.8 all-gather.7
  284.8 64.4 reduce-scatter.4
  352.7 35.1 reduce-scatter.6
  391.5 64.1 reduce-scatter.8
  469.0 33.3 reduce-scatter.10
